TPU v7x, 32 devices: a whole 2x2x4 slice. The times are simulated.
32 devices in a mesh: expert: 8 (over z, y), tensor: 4 (over x, core).
Axes of the slice: x: 2, y: 2, z: 4, core: 2. Of those that a mesh axis runs over, the one named last changes fastest.
Arguments:
- grad_out: bfloat16 [1024, 4096], P('expert', 'tensor'), may hold values from -0.796875 to 0.796875
- gate_weights: bfloat16 [1024, 8], P('expert'), may hold values from 0.049804688 to 1
- slot_lists: int32 [8, 8, 128], P('expert'), may hold values from -1 to 1023, as said below
- saved_gate: bfloat16 [8, 1024, 1536], P('expert', None, 'tensor'), may hold values from -6 to 6
- saved_up: bfloat16 [8, 1024, 1536], P('expert', None, 'tensor'), may hold values from -6 to 6
- w_gate: bfloat16 [8, 4096, 1536], P('expert', None, 'tensor'), may hold values from -0.09375 to 0.09375
- w_up: bfloat16 [8, 4096, 1536], P('expert', None, 'tensor'), may hold values from -0.09375 to 0.09375
- w_down: bfloat16 [8, 1536, 4096], P('expert', 'tensor'), may hold values from -0.15625 to 0.15625
Outputs:
- grad_in: bfloat16 [1024, 4096], P('expert', 'tensor')
- grad_gate: float32 [1024, 8], P('expert')
Inputs may be any that keep to these rules, and one draw needn't show every extreme that they name: slot_lists[s, e, c] is t * 8 + k where expert e is the k-th of the 8 different experts chosen by token t of group s, or -1 for an empty slot; every pair (t, k) of a group stands in exactly one slot, the live slots of each list come first, and in every draw one expert's list holds 128 live entries from every group.
All inputs are finite; a program needn't handle non-finite values.
Results may differ from a plain program's by a relative error of at most 0.012.
Values may be sent and summed in bfloat16 or wider, within the bound.
No kernel may reach another device: no remote copies, remote signals or barrier semaphores. Data moves between devices by JAX's collectives and lax.ppermute only.
A program may use at most 128 MiB of HBM per device.

v0:
```python
import jax
import jax.numpy as jnp
from jax import lax
from jax.sharding import PartitionSpec as P


def silu_pair(pre_act):
    sigma = jax.nn.sigmoid(pre_act)
    return (pre_act * sigma, sigma * (1.0 + pre_act * (1.0 - sigma)))


def local(grad_out, gate_weights, slot_lists, saved_gate, saved_up, w_gate, w_up, w_down):
    slot_table = slot_lists[0]
    experts, capacity = slot_table.shape
    tok_count, quarter = grad_out.shape
    top_count = gate_weights.shape[1]
    entries = slot_table.reshape(-1)
    occupied = entries >= 0
    owner_token = jnp.where(occupied, entries // top_count, -1)
    picker = owner_token[:, None] == jnp.arange(tok_count, dtype=jnp.int32)[None, :]
    picker_half = picker.astype(jnp.bfloat16)
    send_rows = jnp.dot(picker_half, grad_out, preferred_element_type=jnp.float32).astype(
        jnp.bfloat16
    )
    send_gate = jnp.where(
        occupied, gate_weights.reshape(-1)[jnp.maximum(entries, 0)], jnp.zeros((), jnp.bfloat16)
    )
    got_rows, got_gate = (
        lax.all_to_all(
            send_rows.reshape(experts, capacity, quarter),
            "expert",
            split_axis=0,
            concat_axis=0,
            tiled=True,
        ),
        lax.all_to_all(
            send_gate.reshape(experts, capacity), "expert", split_axis=0, concat_axis=0, tiled=True
        ),
    )
    slot_count = got_rows.shape[0] * capacity
    routed = got_rows.reshape(slot_count, quarter)
    down_proj = w_down[0]
    contract = (((1,), (1,)), ((), ()))
    back_hidden = lax.dot_general(
        lax.all_gather(routed, "tensor", axis=1, tiled=True),
        down_proj,
        contract,
        preferred_element_type=jnp.float32,
    )
    gate_pre = saved_gate[0].astype(jnp.float32)
    up_pre = saved_up[0].astype(jnp.float32)
    activated, derivative = silu_pair(gate_pre)
    hidden = activated * up_pre
    slot_gate_grad = lax.psum(jnp.sum(back_hidden * hidden, axis=1), "tensor")
    scaled = got_gate.reshape(slot_count).astype(jnp.float32)[:, None] * back_hidden
    grad_pre_gate = (scaled * up_pre * derivative).astype(jnp.bfloat16)
    grad_pre_up = (scaled * activated).astype(jnp.bfloat16)
    gate_proj = w_gate[0]
    up_proj = w_up[0]
    partial_rows = lax.dot_general(
        gate_proj, grad_pre_gate, contract, preferred_element_type=jnp.float32
    )
    partial_rows = (
        partial_rows
        + lax.dot_general(up_proj, grad_pre_up, contract, preferred_element_type=jnp.float32)
    ).astype(jnp.bfloat16)
    back_rows = lax.all_to_all(partial_rows, "expert", split_axis=1, concat_axis=1, tiled=True)
    back_gate = lax.all_to_all(
        slot_gate_grad.reshape(1, slot_count), "expert", split_axis=1, concat_axis=1, tiled=True
    )
    local_sums = lax.dot_general(
        picker_half, back_rows, (((0,), (1,)), ((), ())), preferred_element_type=jnp.float32
    )
    grad_in = lax.psum_scatter(
        local_sums.astype(jnp.bfloat16), "tensor", scatter_dimension=1, tiled=True
    )
    position = jnp.where(occupied, entries, tok_count * top_count)
    gate_sums = (
        jnp.zeros((tok_count * top_count + 1,), jnp.float32).at[position].add(back_gate.reshape(-1))
    )
    grad_gate = gate_sums[:-1].reshape(tok_count, top_count)
    return (grad_in, grad_gate)


def solution(mesh):
    in_specs = (
        P("expert", "tensor"),
        P("expert", None),
        P("expert", None, None),
        P("expert", None, "tensor"),
        P("expert", None, "tensor"),
        P("expert", None, "tensor"),
        P("expert", None, "tensor"),
        P("expert", "tensor", None),
    )
    out_specs = (P("expert", "tensor"), P("expert", None))
    return jax.shard_map(local, mesh=mesh, in_specs=in_specs, out_specs=out_specs, check_vma=False)
```

profile of v0, /device:TPU:0, one launch (start us, length us, event | category | flops | bytes accessed | tf_op | source)
XLA Modules:
  0.0 379.0 jit_solution(10828798680132189546)
XLA Ops:
  7.2 0.8 fusion.23
  8.1 1.8 convolution_convert_fusion.1
  9.8 55.4 %all_to_all.32 = bf16[8,128,1024]{2,1,0:T(8,128)(2,1)} all-to-all(bf16[8,128,1024]{2,1,0:T(8,128)(2,1)S(1)} %bitcast.71), channel_id=1, replica_groups=mesh['expert'=8,'tensor'=4] {'expert'}, dimensions={0} | all-to-all | bytes 4194304 | tf_op jit(solution)/shard_map/all_to_all | solution.py:29
  65.3 0.7 copy-done.5
  65.9 0.1 copy.20
  66.1 0.1 reshape.135
  66.2 6.8 %gather_fusion = bf16[1024]{0:T(1024)(128)(2,1)S(1)} fusion(bf16[1024]{0:T(1024)(128)(2,1)S(1)} %reshape.135, s32[1024]{0:T(1024)S(1)} %broadcast_clamp_fusion), kind=kCustom, calls=%fused_computation | custom fusion | bytes 8192 | tf_op jit(solution)/shard_map/gather | solution.py:26
  73.0 0.6 copy.21
  73.6 3.6 all-to-all-start
  77.3 2.3 copy.23
  79.6 2.3 copy.22
  81.9 1.7 all-to-all-done
  83.6 39.1 %all-gather.2.cloned.1.call-done = bf16[1024,4096]{1,0:T(8,128)(2,1)} async-done(((bf16[1024,1024]{1,0:T(8,128)(2,1)}), bf16[1024,4096]{1,0:T(8,128)(2,1)}) %all-gather.2.cloned.1.call-update) | async-done | bytes 8388624 | tf_op jit(solution)/shard_map/all_gather | solution.py:45
  122.8 8.5 %fusion.8 = (f32[1024]{0:T(1024)S(1)}, f32[1024,384]{0,1:T(8,128)S(1)}) fusion(bf16[1,1024,384]{1,2,0:T(8,128)(2,1)} %copy.22, bf16[1,1024,384]{1,2,0:T(8,128)(2,1)} %copy.23, bf16[1024,4096]{1,0:T(8,128)(2,1)} %all-gather.2.cloned.1.call-done, bf16[1,384,4096]{2,1,0:T(8,128)(2,1)} %param.15), kind=kOutput, calls=%fused_computation.18 | convolution fusion | flops 3224763392 | bytes 14684160 | tf_op jit(solution)/shard_map/dot_general | solution.py:44
  131.3 1.2 copy-done.1
  132.5 8.8 %fusion.1 = f32[1024,4096]{1,0:T(8,128)} fusion(bf16[1,4096,384]{2,1,0:T(8,128)(2,1)S(1)} %copy-done, f32[1024,384]{0,1:T(8,128)S(1)} %get-tuple-element.11, bf16[1,1024,384]{1,2,0:T(8,128)(2,1)S(1)} %copy-done.3, bf16[1,1024,384]{1,2,0:T(8,128)(2,1)S(1)} %copy-done.2, f32[1024]{0:T(1024)S(1)} %bitcast.72), kind=kOutput, calls=%fused_computation.5 | convolution fusion | flops 3226337280 | bytes 23072768 | tf_op jit(solution)/shard_map/dot_general | solution.py:60
  141.2 15.3 %add_convert_fusion = bf16[1024,4096]{1,0:T(8,128)(2,1)} fusion(f32[1024,4096]{1,0:T(8,128)} %fusion.1, bf16[1,4096,384]{2,1,0:T(8,128)(2,1)} %param.14, f32[1024,384]{0,1:T(8,128)} %copy-done.1, f32[1024]{0:T(1024)S(1)} %bitcast.73, bf16[1,1024,384]{1,2,0:T(8,128)(2,1)} %copy.23), kind=kOutput, calls=%fused_computation.2 | convolution fusion | flops 3232759808 | bytes 30674944 | tf_op jit(solution)/shard_map/dot_general | solution.py:65
  156.5 189.0 %all_to_all.33 = bf16[4096,8,128]{0,2,1:T(8,128)(2,1)S(1)} all-to-all(bf16[4096,8,128]{0,2,1:T(8,128)(2,1)} %bitcast.69), channel_id=1, replica_groups=mesh['expert'=8,'tensor'=4] {'expert'}, dimensions={1} | all-to-all | bytes 16777216 | tf_op jit(solution)/shard_map/all_to_all | solution.py:67
  345.5 2.4 convolution_convert_fusion
  347.9 6.0 %psum.7 = f32[1,8,128]{2,0,1:T(1,128)S(1)} all-reduce(f32[1,8,128]{2,0,1:T(1,128)S(1)} %bitcast.77), channel_id=1, replica_groups=mesh['expert'=8,'tensor'=4] {'tensor'}, use_global_device_ids=true, to_apply=%region_2.3 | all-reduce | flops 1024 | bytes 8192 | tf_op jit(solution)/shard_map/psum | solution.py:54
  353.9 9.9 %all_to_all.34 = f32[1,8,128]{2,0,1:T(1,128)S(1)} all-to-all(f32[1,8,128]{2,0,1:T(1,128)S(1)} %psum.7), channel_id=1, replica_groups=mesh['expert'=8,'tensor'=4] {'expert'}, dimensions={1} | all-to-all | bytes 8192 | tf_op jit(solution)/shard_map/all_to_all | solution.py:68
  363.8 7.6 %scatter_custom_fusion = f32[1025]{0:T(1024)S(1)} fusion(s32[1024]{0:T(1024)S(1)} %bitcast.76, f32[1024]{0:T(1024)S(1)} %bitcast.78, f32[]{:T(128)} %constant.28.clone.1), kind=kCustom, calls=%fused_computation.45 | custom fusion | flops 1024 | bytes 4104 | tf_op jit(solution)/shard_map/scatter-add | solution.py:79
  371.4 0.1 reshape.139
  371.5 0.7 copy.24
  (20 shorter events, 0.2 us)
Async XLA Ops:
  7.2 125.3 %copy-start = (bf16[1,4096,384]{2,1,0:T(8,128)(2,1)S(1)}, bf16[1,4096,384]{2,1,0:T(8,128)(2,1)}, u32[]{:S(2)}) copy-start(bf16[1,4096,384]{2,1,0:T(8,128)(2,1)} %param.13) | copy-start | bytes 9437188
  7.2 115.6 %all-gather.2.cloned.1.call-start = ((), (), s32[]{:S(2)}) async-start(), calls=%async_computation.5 | async-start | bytes 10485760 | tf_op jit(solution)/shard_map/all_gather | solution.py:45
  65.3 0.7 copy-start.5
  65.3 0.9 copy-start.4
  73.6 10.0 %all-to-all-start = ((bf16[8,1,128]{2,1,0:T(2,128)(2,1)}), bf16[8,1,128]{2,1,0:T(2,128)(2,1)S(1)}, u32[]{:S(2)}, u32[]{:S(2)}) async-start(bf16[8,1,128]{2,1,0:T(2,128)(2,1)} %copy.21), calls=%async_computation | async-start | bytes 8192 | tf_op jit(solution)/shard_map/all_to_all | solution.py:36
  77.2 294.9 %reduce-scatter.2.cloned.1.call-start = ((), (), s32[]{:S(2)}) async-start(), calls=%async_computation.6 | async-start | bytes 1310720 | tf_op jit(solution)/shard_map/reduce_scatter | solution.py:74
  122.8 9.7 %copy-start.2 = (bf16[1,1024,384]{1,2,0:T(8,128)(2,1)S(1)}, bf16[1,1024,384]{1,2,0:T(8,128)(2,1)}, u32[]{:S(2)}) copy-start(bf16[1,1024,384]{1,2,0:T(8,128)(2,1)} %copy.23) | copy-start | bytes 2359300
  122.8 9.7 %copy-start.3 = (bf16[1,1024,384]{1,2,0:T(8,128)(2,1)S(1)}, bf16[1,1024,384]{1,2,0:T(8,128)(2,1)}, u32[]{:S(2)}) copy-start(bf16[1,1024,384]{1,2,0:T(8,128)(2,1)} %copy.22) | copy-start | bytes 2359300
  131.2 1.2 copy-start.1
Sparse Core Ops, SparseCore 0:
  65.4 57.3 all-gather.1
  348.0 23.0 reduce-scatter.1
where the time goes:
time: 379 us
  blocking collectives  260 us (69%)
  waiting for transfers between devices  40.9 us (11%)
  matrix products  36.7 us (10%)
  local copies, waits for them, and re-layouts  14.9 us (4%)
  between operations  14.1 us (4%)
  other arithmetic  8.5 us (2%)
    all_to_all x1, blocking collectives, local(): lax.all_to_all(partial_rows, 'expert', split_axis=1, concat_axis=1, tiled...  189 us
    all_to_all x1, blocking collectives, local(): lax.all_to_all(send_rows.reshape(experts, capacity, quarter), 'expert', s...  55.4 us
    all_gather x1, waiting for transfers between devices, local(): lax.all_gather(routed, 'tensor', axis=1, tiled=True)  39.1 us
    dot_general x1, matrix products, local(): lax.dot_general(up_proj, grad_pre_up, contract, preferred_element_type=jn...  15.3 us
    all_to_all x1, blocking collectives, local(): lax.all_to_all(slot_gate_grad.reshape(1, slot_count), 'expert', split_axi...  9.88 us
    dot_general x1, matrix products, local(): lax.dot_general(gate_proj, grad_pre_gate, contract, preferred_element_typ...  8.76 us
    dot_general x1, matrix products, local(): lax.dot_general(lax.all_gather(routed, 'tensor', axis=1, tiled=True), dow...  8.49 us
    scatter-add x1, other arithmetic, local(): jnp.zeros((tok_count * top_count + 1,), jnp.float32).at[position]  7.62 us
  transfers between devices with their start and end apart: 3, of which 2 were waited for; matrix products, arithmetic and copies ran while one was open for 5% of the time, Pallas kernels for 0%

commit v1 on v0

--- a/solution.py
+++ b/solution.py
@@ -3,13 +3,17 @@
 from jax import lax
 from jax.sharding import PartitionSpec as P
 
+BOTH = ("expert", "tensor")
+F32 = jnp.float32
+BF16 = jnp.bfloat16
+
 
 def silu_pair(pre_act):
     sigma = jax.nn.sigmoid(pre_act)
     return (pre_act * sigma, sigma * (1.0 + pre_act * (1.0 - sigma)))
 
 
-def local(grad_out, gate_weights, slot_lists, saved_gate, saved_up, w_gate, w_up, w_down):
+def routed_local(grad_out, gate_weights, slot_lists, saved_gate, saved_up, w_gate, w_up, w_down):
     slot_table = slot_lists[0]
     experts, capacity = slot_table.shape
     tok_count, quarter = grad_out.shape
@@ -82,6 +86,164 @@
     return (grad_in, grad_gate)
 
 
+NZ, NY, NX, NC = 4, 2, 2, 2
+
+
+def _pairs(move):
+    pairs = []
+    for z in range(NZ):
+        for y in range(NY):
+            for x in range(NX):
+                for c in range(NC):
+                    tz, ty, tx, tc = move(z, y, x, c)
+                    pairs.append((((z * NY + y) * NX + x) * NC + c, ((tz * NY + ty) * NX + tx) * NC + tc))
+    return pairs
+
+
+TO_X = _pairs(lambda z, y, x, c: (z, y, 1 - x, c))
+TO_Y = _pairs(lambda z, y, x, c: (z, 1 - y, x, c))
+TO_CORE = _pairs(lambda z, y, x, c: (z, y, x, 1 - c))
+CORNER = _pairs(lambda z, y, x, c: (z, y, 1 - x, c) if c == 0 else (z, 1 - y, x, c))
+Z_UP = [_pairs(lambda z, y, x, c, d=d: ((z + d) % NZ, y, x, c)) for d in range(NZ)]
+
+
+def send(value, pairs):
+    return lax.ppermute(value, BOTH, pairs)
+
+
+def dot_nt(a, b):
+    return lax.dot_general(a, b, (((1,), (1,)), ((), ())), preferred_element_type=F32)
+
+
+def dense_local(grad_out, gate_weights, slot_lists, saved_gate, saved_up, w_gate, w_up, w_down):
+    tokens, quarter = grad_out.shape
+    experts = slot_lists.shape[1]
+    top_count = gate_weights.shape[1]
+    hid = saved_gate.shape[2]
+    expert = lax.axis_index("expert")
+    block = lax.axis_index("tensor")
+    z, y = expert // NY, expert % NY
+    x, c = block // NC, block % NC
+    chunks = 2
+    rows = tokens // chunks
+
+    pieces = []
+    for j in range(chunks):
+        own = grad_out[j * rows : (j + 1) * rows]
+        p00 = jnp.concatenate([own] + [send(own, Z_UP[d]) for d in range(1, NZ)], axis=0)
+        p10 = send(p00, TO_Y)
+        p01 = send(p00, TO_X)
+        p11 = send(jnp.where(c == 0, p10, p01), CORNER)
+        pieces.append(((p00, p01), (p10, p11)))
+
+    entries = slot_lists[0]
+    owner, choice = entries // top_count, entries % top_count
+    token_ids = jnp.arange(tokens, dtype=jnp.int32)
+    hit = owner[:, :, None] == token_ids[None, None, :]
+    choice_of = jnp.sum(jnp.where(hit, choice[:, :, None], 0), axis=1)
+    slot_of = jnp.sum(jnp.where(hit, token_ids[None, :, None], 0), axis=1)
+    choice_ids = jnp.arange(top_count, dtype=jnp.int32)
+    chosen = choice_of[:, :, None] == choice_ids[None, None, :]
+    gate_of = jnp.sum(jnp.where(chosen, gate_weights[None].astype(F32), 0.0), axis=2)
+    table = lax.all_gather(jnp.stack([slot_of.astype(F32), gate_of], axis=1), "expert", axis=0)
+    table = lax.dynamic_index_in_dim(table, expert, axis=1, keepdims=False)
+
+    def halves(w, axis):
+        shape = w.shape[:axis] + (NX, NC, quarter) + w.shape[axis + 1 :]
+        w = w.reshape(shape)
+        keep = lax.dynamic_index_in_dim(w, c, axis=axis + 1, keepdims=False)
+        give = lax.dynamic_index_in_dim(w, 1 - c, axis=axis + 1, keepdims=False)
+        got = send(give, TO_CORE)
+
+        def near(v, dx):
+            return lax.dynamic_index_in_dim(v, jnp.where(dx == 0, x, 1 - x), axis=axis, keepdims=False)
+
+        return [(near(keep, dx), near(got, dx)) for dx in range(NX)]
+
+    down = halves(w_down[0], 1)
+    gate_w = halves(w_gate[0], 0)
+    up_w = halves(w_up[0], 0)
+
+    factors = []
+    sg = saved_gate[0].reshape(experts, tokens, hid)
+    su = saved_up[0].reshape(experts, tokens, hid)
+    for dy in range(NY):
+        line = []
+        for d in range(NZ):
+            group = ((z + NZ - d) % NZ) * NY + (y if dy == 0 else 1 - y)
+            slot_row = lax.dynamic_index_in_dim(table, group, axis=0, keepdims=False)
+            pick = (slot_row[0].astype(jnp.int32)[:, None] == token_ids[None, :]).astype(BF16)
+            gate_pre = jnp.dot(pick, lax.dynamic_index_in_dim(sg, group, 0, False), preferred_element_type=F32)
+            up_pre = jnp.dot(pick, lax.dynamic_index_in_dim(su, group, 0, False), preferred_element_type=F32)
+            activated, derivative = silu_pair(gate_pre)
+            scale = slot_row[1][:, None]
+            line.append((activated * up_pre, scale * up_pre * derivative, scale * activated))
+        factors.append(line)
+
+    gate_terms = []
+    results = []
+    for j in range(chunks):
+        lo, hi = j * rows, (j + 1) * rows
+        ready = []
+        for dy in range(NY):
+            (a, b) = pieces[j][dy]
+            mine = dot_nt(a, down[0][0]) + dot_nt(b, down[1][0])
+            theirs = dot_nt(a, down[0][1]) + dot_nt(b, down[1][1])
+            ready.append((mine, theirs))
+        back = send(jnp.concatenate([r[1] for r in ready], axis=0), TO_CORE)
+        gp, up, terms = [], [], []
+        for dy in range(NY):
+            bh = ready[dy][0] + back[dy * NZ * rows : (dy + 1) * NZ * rows]
+            f = [jnp.concatenate([factors[dy][d][i][lo:hi] for d in range(NZ)], axis=0) for i in range(3)]
+            terms.append(jnp.sum(bh * f[0], axis=1))
+            gp.append((bh * f[1]).astype(BF16))
+            up.append((bh * f[2]).astype(BF16))
+        gate_terms.append(jnp.stack(terms).reshape(NY, NZ, rows))
+        mine = jnp.concatenate([jnp.concatenate(gp, 0), jnp.concatenate(up, 0)], axis=1)
+        theirs = send(mine, TO_CORE)
+
+        def grad(dy, dx):
+            s = slice(dy * NZ * rows, (dy + 1) * NZ * rows)
+            m, t = mine[s], theirs[s]
+            return (
+                dot_nt(m[:, :hid], gate_w[dx][0])
+                + dot_nt(m[:, hid:], up_w[dx][0])
+                + dot_nt(t[:, :hid], gate_w[dx][1])
+                + dot_nt(t[:, hid:], up_w[dx][1])
+            )
+
+        r11 = send(grad(1, 1).astype(BF16), CORNER).astype(F32)
+        r10 = (grad(1, 0) + jnp.where(c == 0, r11, 0.0)).astype(BF16)
+        r01 = (grad(0, 1) + jnp.where(c == 0, 0.0, r11)).astype(BF16)
+        r00 = grad(0, 0) + send(r10, TO_Y).astype(F32) + send(r01, TO_X).astype(F32)
+        total = r00[:rows]
+        for d in range(1, NZ):
+            total = total + send(r00[d * rows : (d + 1) * rows].astype(BF16), Z_UP[NZ - d]).astype(F32)
+        results.append(total.astype(BF16))
+    grad_in = jnp.concatenate(results, axis=0)
+
+    terms = jnp.concatenate(gate_terms, axis=2)
+    everyone = lax.all_gather(terms, BOTH, axis=0)
+    everyone = everyone.reshape(NZ, NY, NX * NC, NY, NZ, tokens)
+    everyone = jnp.sum(everyone, axis=2)
+    src_z = jnp.arange(NZ, dtype=jnp.int32)
+    src_y = jnp.arange(NY, dtype=jnp.int32)
+    want = ((src_z[:, None] - jnp.arange(NZ)[None, :]) % NZ == z)[:, None, None, :]
+    want = want & ((src_y[:, None] ^ src_y[None, :]) == y)[None, :, :, None]
+    slot_grad = jnp.sum(jnp.where(want[..., None], everyone, 0.0), axis=(2, 3)).reshape(experts, tokens)
+    grad_gate = jnp.sum(jnp.where(chosen, slot_grad[:, :, None], 0.0), axis=0)
+    return (grad_in, grad_gate)
+
+
+def local(grad_out, gate_weights, slot_lists, *rest):
+    tokens = grad_out.shape[0]
+    _, experts, capacity = slot_lists.shape
+    dense = experts == gate_weights.shape[1] == NZ * NY and capacity == tokens
+    dense = dense and lax.axis_size("expert") == NZ * NY and lax.axis_size("tensor") == NX * NC
+    program = dense_local if dense else routed_local
+    return program(grad_out, gate_weights, slot_lists, *rest)
+
+
 def solution(mesh):
     in_specs = (
         P("expert", "tensor"),

time: 379 us -> 270 us (0.71)
  blocking collectives: 260 us -> 72.6 us
  matrix products: 36.7 us -> 76 us
  starting transfers between devices: 3.66 us -> 27.6 us
  local copies, waits for them, and re-layouts: 14.9 us -> 38.3 us
  between operations: 14.1 us -> 2.02 us
  other arithmetic: 8.5 us -> 12.5 us
    all_to_all x3 -> x0, blocking collectives: 254 us -> none  [the longest x1 189 us: local(): lax.all_to_all(partial_rows, 'expert', split_axis=1, concat_axis=1, tiled...]
    all_gather x0 -> x2, blocking collectives: none -> 72.6 us  [the longest x1 40 us: dense_local(): everyone = lax.all_gather(terms, BOTH, axis=0)]
    dot_general x5 -> x64, matrix products: 36.7 us -> 76 us  [the longest x48 70.5 us: dot_nt(): lax.dot_general(a, b, (((1,), (1,)), ((), ())), preferred_element_type=F32)]
    all_gather x1 -> x0, waiting for transfers between devices: 39.1 us -> none  [local(): lax.all_gather(routed, 'tensor', axis=1, tiled=True)]
    ppermute x0 -> x31, waiting for transfers between devices: none -> 39 us  [send(): return lax.ppermute(value, BOTH, pairs)]
    ppermute x0 -> x31, starting transfers between devices: none -> 27.6 us  [send(): return lax.ppermute(value, BOTH, pairs)]
    slice x1 -> x27, local copies, waits for them, and re-layouts: 0.01 us -> 18 us  [the longest x24 16.8 us: dense_local(): factors[dy][d][i][lo:hi]]
    scatter-add x1 -> x0, other arithmetic: 7.62 us -> none  [local(): jnp.zeros((tok_count * top_count + 1,), jnp.float32).at[position]]
  transfers between devices with their start and end apart: 3 -> 31, of which waited for: 2 -> 9; matrix products, arithmetic and copies ran while one was open for 5% -> 45% of each run, Pallas kernels for 0% -> 0%
where the time goes in v1:
time: 270 us; the launch traced here: 268 us
  matrix products  76 us (28%)
  blocking collectives  72.6 us (27%)
  waiting for transfers between devices  39 us (14%)
  local copies, waits for them, and re-layouts  38.3 us (14%)
  starting transfers between devices  27.6 us (10%)
  other arithmetic  12.5 us (5%)
    dot_general x48, matrix products, dot_nt(): lax.dot_general(a, b, (((1,), (1,)), ((), ())), preferred_element_type=F32)  70.5 us
    all_gather x1, blocking collectives, dense_local(): everyone = lax.all_gather(terms, BOTH, axis=0)  40 us
    ppermute x31, waiting for transfers between devices, send(): return lax.ppermute(value, BOTH, pairs)  39 us
    all_gather x1, blocking collectives, dense_local(): lax.all_gather(jnp.stack([slot_of.astype(F32), gate_of], axis=1), 'expert...  32.6 us
    ppermute x31, starting transfers between devices, send(): return lax.ppermute(value, BOTH, pairs)  27.6 us
    slice x24, local copies, waits for them, and re-layouts, dense_local(): factors[dy][d][i][lo:hi]  16.8 us
    unnamed x123, local copies, waits for them, and re-layouts  8.82 us
  transfers between devices with their start and end apart: 31, of which 9 were waited for; matrix products, arithmetic and copies ran while one was open for 45% of the time, Pallas kernels for 0%

profile of v1, /device:TPU:0, one launch (start us, length us, event | category | flops | bytes accessed | tf_op | source)
XLA Modules:
  0.0 267.9 jit_solution(1975998342890564821)
XLA Ops:
  1.8 3.1 %collective-permute-start = (bf16[64,1024]{1,0:T(8,128)(2,1)S(1)}, bf16[64,1024]{1,0:T(8,128)(2,1)}, u32[]{:S(2)}, u32[]{:S(2)}) collective-permute-start(bf16[64,1024]{1,0:T(8,128)(2,1)S(1)} %get-tuple-element.38), channel_id=1, source_target_pairs={{0,8},{1,9},{2,10},{3,11},{4,12},{5,13},{6,14},{7,15},{8,16},{9,17... | collective-permute-start | bytes 393224 | tf_op jit(solution)/shard_map/ppermute | solution.py:111
  4.9 2.6 collective-permute-start.1
  9.9 4.6 %copy.22 = bf16[1,384,4096]{1,2,0:T(8,128)(2,1)} copy(bf16[1,384,4096]{2,1,0:T(8,128)(2,1)} %param.15) | data formatting | bytes 6291456 | tf_op args[7]
  15.0 32.6 %all-gather = f32[64,2,128]{2,1,0:T(2,128)S(1)} all-gather(f32[8,2,128]{2,1,0:T(2,128)S(1)} %copy.26), channel_id=2, replica_groups=mesh['expert'=8,'tensor'=4] {'expert'}, dimensions={0}, use_global_device_ids=true | all-gather | bytes 73728 | tf_op jit(solution)/shard_map/all_gather | solution.py:148
  74.3 2.1 collective-permute-start.5
  76.4 2.7 %constant_dynamic-slice_fusion.8 = bf16[384,2,1,1024]{0,3,2,1:T(8,128)(2,1)} fusion(bf16[384,2,2,1024]{0,3,2,1:T(8,128)(2,1)} %bitcast.303, s32[]{:T(128)S(6)} %select_n.244), kind=kLoop, calls=%fused_computation.422 | loop fusion | bytes 3145732 | tf_op jit(solution)/shard_map/jit(dynamic_index_in_dim)/dynamic_slice | solution.py:155
  79.1 2.6 copy.25
  81.7 1.9 pad_maximum_fusion.3
  89.9 8.3 %collective-permute-done.20 = bf16[256,1024]{1,0:T(8,128)(2,1)} collective-permute-done((bf16[256,1024]{1,0:T(8,128)(2,1)}, bf16[256,1024]{1,0:T(8,128)(2,1)}, u32[]{:S(2)}, u32[]{:S(2)}) %collective-permute-start.20) | collective-permute-done | bytes 524320 | tf_op jit(solution)/shard_map/ppermute | solution.py:111
  102.9 2.3 fusion.28
  105.2 2.2 collective-permute-done.6
  107.8 5.2 %collective-permute-done.22 = bf16[256,1024]{1,0:T(8,128)(2,1)S(1)} collective-permute-done((bf16[256,1024]{1,0:T(8,128)(2,1)S(1)}, bf16[256,1024]{1,0:T(8,128)(2,1)S(1)}, u32[]{:S(2)}, u32[]{:S(2)}) %collective-permute-start.22) | collective-permute-done | bytes 524320 | tf_op jit(solution)/shard_map/ppermute | solution.py:111
  126.6 1.9 convolution_add_fusion.17
  132.0 2.8 %fusion.155 = (f32[256]{0:T(256)}, bf16[256,384]{1,0:T(8,128)(2,1)S(1)}, bf16[256,384]{1,0:T(8,128)(2,1)}) fusion(f32[64,384]{1,0:T(8,128)S(1)} %copy-done.55, f32[64,384]{1,0:T(8,128)S(1)} %copy-done.52, f32[64,384]{1,0:T(8,128)S(1)} %copy-done.49, f32[64,384]{1,0:T(8,128)S(1)} %copy-done.46, f32[64,384]{1,0:T(8,128)S(1)} %copy-done.57, ...), kind=kOutput, calls=%fused_computation.206 | convolution fusion | flops 202997504 | bytes 3671048 | tf_op jit(solution)/shard_map/dot_general | solution.py:115
  137.8 2.4 fusion.56
  143.3 3.2 %fusion.156 = (f32[256]{0:T(256)}, bf16[256,384]{1,0:T(8,128)(2,1)}, bf16[256,384]{1,0:T(8,128)(2,1)}) fusion(f32[64,384]{1,0:T(8,128)S(1)} %copy-done.33, f32[64,384]{1,0:T(8,128)S(1)} %copy-done.28, f32[64,384]{1,0:T(8,128)S(1)} %copy-done.25, f32[64,384]{1,0:T(8,128)S(1)} %copy-done.22, f32[64,384]{1,0:T(8,128)S(1)} %copy-done.36, ...), kind=kOutput, calls=%fused_computation.208 | convolution fusion | flops 205094656 | bytes 3671048 | tf_op jit(solution)/shard_map/dot_general | solution.py:115
  147.8 3.6 %fusion.157 = (f32[256]{0:T(256)}, bf16[256,384]{1,0:T(8,128)(2,1)}, bf16[256,384]{1,0:T(8,128)(2,1)}) fusion(f32[64,384]{1,0:T(8,128)} %get-tuple-element.63, f32[64,384]{1,0:T(8,128)} %get-tuple-element.61, f32[64,384]{1,0:T(8,128)} %get-tuple-element.59, f32[64,384]{1,0:T(8,128)} %get-tuple-element.57, f32[64,384]{1,0:T(8,128)} %get-tuple-element.95, ...), kind=kOutput, calls=%fused_computation.210 | convolution fusion | flops 202997504 | bytes 3671048 | tf_op jit(solution)/shard_map/dot_general | solution.py:115
  153.5 40.0 %all-gather.1 = f32[64,4,128]{2,1,0:T(4,128)} all-gather(f32[2,4,128]{2,1,0:T(4,128)S(1)} %maximum_maximum_fusion.2), channel_id=3, replica_groups=mesh['expert'=8,'tensor'=4] {'expert','tensor'}, dimensions={0}, use_global_device_ids=true | all-gather | bytes 135168 | tf_op jit(solution)/shard_map/all_gather | solution.py:226
  196.6 2.1 convolution_add_fusion.15
  232.0 2.1 collective-permute-start.26
  236.3 5.7 %collective-permute-done.12 = bf16[256,1024]{1,0:T(8,128)(2,1)S(1)} collective-permute-done((bf16[256,1024]{1,0:T(8,128)(2,1)S(1)}, bf16[256,1024]{1,0:T(8,128)(2,1)S(1)}, u32[]{:S(2)}, u32[]{:S(2)}) %collective-permute-start.12) | collective-permute-done | bytes 524320 | tf_op jit(solution)/shard_map/ppermute | solution.py:111
  247.5 4.3 %collective-permute-done.26 = bf16[256,1024]{1,0:T(8,128)(2,1)S(1)} collective-permute-done((bf16[256,1024]{1,0:T(8,128)(2,1)S(1)}, bf16[256,1024]{1,0:T(8,128)(2,1)S(1)}, u32[]{:S(2)}, u32[]{:S(2)}) %collective-permute-start.26) | collective-permute-done | bytes 524320 | tf_op jit(solution)/shard_map/ppermute | solution.py:111
  257.4 2.9 %collective-permute-done.28 = bf16[64,1024]{1,0:T(8,128)(2,1)S(1)} collective-permute-done((bf16[64,1024]{1,0:T(8,128)(2,1)S(1)}, bf16[64,1024]{1,0:T(8,128)(2,1)S(1)}, u32[]{:S(2)}, u32[]{:S(2)}) %collective-permute-start.28) | collective-permute-done | bytes 131104 | tf_op jit(solution)/shard_map/ppermute | solution.py:111
  260.3 6.8 %collective-permute-done.29 = bf16[64,1024]{1,0:T(8,128)(2,1)S(1)} collective-permute-done((bf16[64,1024]{1,0:T(8,128)(2,1)S(1)}, bf16[64,1024]{1,0:T(8,128)(2,1)S(1)}, u32[]{:S(2)}, u32[]{:S(2)}) %collective-permute-start.29) | collective-permute-done | bytes 131104 | tf_op jit(solution)/shard_map/ppermute | solution.py:111
  (292 shorter events, 117.9 us)
Async XLA Ops:
  1.8 68.3 %collective-permute-start = (bf16[64,1024]{1,0:T(8,128)(2,1)S(1)}, bf16[64,1024]{1,0:T(8,128)(2,1)}, u32[]{:S(2)}, u32[]{:S(2)}) collective-permute-start(bf16[64,1024]{1,0:T(8,128)(2,1)S(1)} %get-tuple-element.38), channel_id=1, source_target_pairs={{0,8},{1,9},{2,10},{3,11},{4,12},{5,13},{6,14},{7,15},{8,16},{9,17... | collective-permute-start | bytes 393224 | tf_op jit(solution)/shard_map/ppermute | solution.py:111
  4.9 66.0 %collective-permute-start.1 = (bf16[64,1024]{1,0:T(8,128)(2,1)S(1)}, bf16[64,1024]{1,0:T(8,128)(2,1)}, u32[]{:S(2)}, u32[]{:S(2)}) collective-permute-start(bf16[64,1024]{1,0:T(8,128)(2,1)S(1)} %get-tuple-element.38), channel_id=1, source_target_pairs={{0,16},{1,17},{2,18},{3,19},{4,20},{5,21},{6,22},{7,23},{8,24},{9,... | collective-permute-start | bytes 393224 | tf_op jit(solution)/shard_map/ppermute | solution.py:111
  7.5 63.4 %collective-permute-start.2 = (bf16[64,1024]{1,0:T(8,128)(2,1)S(1)}, bf16[64,1024]{1,0:T(8,128)(2,1)}, u32[]{:S(2)}, u32[]{:S(2)}) collective-permute-start(bf16[64,1024]{1,0:T(8,128)(2,1)S(1)} %get-tuple-element.38), channel_id=1, source_target_pairs={{0,24},{1,25},{2,26},{3,27},{4,28},{5,29},{6,30},{7,31},{8,0},{9,1... | collective-permute-start | bytes 393224 | tf_op jit(solution)/shard_map/ppermute | solution.py:111
  8.8 72.9 %collective-permute-start.17 = (bf16[64,1024]{1,0:T(8,128)(2,1)S(1)}, bf16[64,1024]{1,0:T(8,128)(2,1)S(1)}, u32[]{:S(2)}, u32[]{:S(2)}) collective-permute-start(bf16[64,1024]{1,0:T(8,128)(2,1)S(1)} %get-tuple-element.39), channel_id=1, source_target_pairs={{0,8},{1,9},{2,10},{3,11},{4,12},{5,13},{6,14},{7,15},{8,16},{9,17... | collective-permute-start | bytes 393224 | tf_op jit(solution)/shard_map/ppermute | solution.py:111
  9.5 72.2 %collective-permute-start.18 = (bf16[64,1024]{1,0:T(8,128)(2,1)S(1)}, bf16[64,1024]{1,0:T(8,128)(2,1)}, u32[]{:S(2)}, u32[]{:S(2)}) collective-permute-start(bf16[64,1024]{1,0:T(8,128)(2,1)S(1)} %get-tuple-element.39), channel_id=1, source_target_pairs={{0,16},{1,17},{2,18},{3,19},{4,20},{5,21},{6,22},{7,23},{8,24},{9,... | collective-permute-start | bytes 393224 | tf_op jit(solution)/shard_map/ppermute | solution.py:111
  70.1 11.6 %collective-permute-start.19 = (bf16[64,1024]{1,0:T(8,128)(2,1)S(1)}, bf16[64,1024]{1,0:T(8,128)(2,1)}, u32[]{:S(2)}, u32[]{:S(2)}) collective-permute-start(bf16[64,1024]{1,0:T(8,128)(2,1)S(1)} %get-tuple-element.39), channel_id=1, source_target_pairs={{0,24},{1,25},{2,26},{3,27},{4,28},{5,29},{6,30},{7,31},{8,0},{9,1... | collective-permute-start | bytes 393224 | tf_op jit(solution)/shard_map/ppermute | solution.py:111
  72.8 15.3 %collective-permute-start.3 = (bf16[256,1024]{1,0:T(8,128)(2,1)}, bf16[256,1024]{1,0:T(8,128)(2,1)}, u32[]{:S(2)}, u32[]{:S(2)}) collective-permute-start(bf16[256,1024]{1,0:T(8,128)(2,1)} %pad_maximum_fusion.2), channel_id=1, source_target_pairs={{0,2},{1,3},{2,0},{3,1},{4,6},{5,7},{6,4},{7,5},{8,10},{9,11},{10,... | collective-permute-start | bytes 1572872 | tf_op jit(solution)/shard_map/ppermute | solution.py:111
  74.3 13.9 %collective-permute-start.5 = (bf16[256,1024]{1,0:T(8,128)(2,1)}, bf16[256,1024]{1,0:T(8,128)(2,1)}, u32[]{:S(2)}, u32[]{:S(2)}) collective-permute-start(bf16[256,1024]{1,0:T(8,128)(2,1)} %pad_maximum_fusion.2), channel_id=1, source_target_pairs={{0,4},{1,5},{2,6},{3,7},{4,0},{5,1},{6,2},{7,3},{8,12},{9,13},{10,... | collective-permute-start | bytes 1572872 | tf_op jit(solution)/shard_map/ppermute | solution.py:111
  81.7 32.5 %collective-permute-start.4 = (bf16[384,2,1024]{2,0,1:T(8,128)(2,1)}, bf16[384,2,1024]{2,0,1:T(8,128)(2,1)}, u32[]{:S(2)}, u32[]{:S(2)}) collective-permute-start(bf16[384,2,1024]{2,0,1:T(8,128)(2,1)} %bitcast.321), channel_id=1, source_target_pairs={{0,1},{1,0},{2,3},{3,2},{4,5},{5,4},{6,7},{7,6},{8,9},{9,8},{10,11... | collective-permute-start | bytes 4718600 | tf_op jit(solution)/shard_map/ppermute | solution.py:111
  83.6 14.6 %collective-permute-start.20 = (bf16[256,1024]{1,0:T(8,128)(2,1)}, bf16[256,1024]{1,0:T(8,128)(2,1)}, u32[]{:S(2)}, u32[]{:S(2)}) collective-permute-start(bf16[256,1024]{1,0:T(8,128)(2,1)} %pad_maximum_fusion.3), channel_id=1, source_target_pairs={{0,2},{1,3},{2,0},{3,1},{4,6},{5,7},{6,4},{7,5},{8,10},{9,11},{10,... | collective-permute-start | bytes 1572872 | tf_op jit(solution)/shard_map/ppermute | solution.py:111
  84.1 14.6 %collective-permute-start.21 = (bf16[256,1024]{1,0:T(8,128)(2,1)}, bf16[256,1024]{1,0:T(8,128)(2,1)}, u32[]{:S(2)}, u32[]{:S(2)}) collective-permute-start(bf16[256,1024]{1,0:T(8,128)(2,1)} %pad_maximum_fusion.3), channel_id=1, source_target_pairs={{0,4},{1,5},{2,6},{3,7},{4,0},{5,1},{6,2},{7,3},{8,12},{9,13},{10,... | collective-permute-start | bytes 1572872 | tf_op jit(solution)/shard_map/ppermute | solution.py:111
  88.0 119.1 %collective-permute-start.10 = (bf16[2,1024,384]{2,1,0:T(8,128)(2,1)}, bf16[2,1024,384]{2,1,0:T(8,128)(2,1)}, u32[]{:S(2)}, u32[]{:S(2)}) collective-permute-start(bf16[2,1024,384]{2,1,0:T(8,128)(2,1)} %dynamic-slice_bitcast_fusion), channel_id=1, source_target_pairs={{0,1},{1,0},{2,3},{3,2},{4,5},{5,4},{6,7},{7,6},{8,9},{9,8},{10,11... | collective-permute-start | bytes 4718600 | tf_op jit(solution)/shard_map/ppermute | solution.py:111
  88.2 120.5 %collective-permute-start.9 = (bf16[2,1024,384]{2,1,0:T(8,128)(2,1)}, bf16[2,1024,384]{2,1,0:T(8,128)(2,1)}, u32[]{:S(2)}, u32[]{:S(2)}) collective-permute-start(bf16[2,1024,384]{2,1,0:T(8,128)(2,1)} %dynamic-slice_bitcast_fusion.1), channel_id=1, source_target_pairs={{0,1},{1,0},{2,3},{3,2},{4,5},{5,4},{6,7},{7,6},{8,9},{9,8},{10,11... | collective-permute-start | bytes 4718600 | tf_op jit(solution)/shard_map/ppermute | solution.py:111
  99.9 13.2 %collective-permute-start.22 = (bf16[256,1024]{1,0:T(8,128)(2,1)S(1)}, bf16[256,1024]{1,0:T(8,128)(2,1)S(1)}, u32[]{:S(2)}, u32[]{:S(2)}) collective-permute-start(bf16[256,1024]{1,0:T(8,128)(2,1)S(1)} %broadcast_select_fusion), channel_id=1, source_target_pairs={{0,2},{1,5},{2,0},{3,7},{4,6},{5,1},{6,4},{7,3},{8,10},{9,13},{10,... | collective-permute-start | bytes 1572872 | tf_op jit(solution)/shard_map/ppermute | solution.py:111
  129.4 13.8 %collective-permute-start.23 = (f32[512,384]{1,0:T(8,128)}, f32[512,384]{1,0:T(8,128)}, u32[]{:S(2)}, u32[]{:S(2)}) collective-permute-start(f32[512,384]{1,0:T(8,128)} %pad_maximum_fusion.1), channel_id=1, source_target_pairs={{0,1},{1,0},{2,3},{3,2},{4,5},{5,4},{6,7},{7,6},{8,9},{9,8},{10,11... | collective-permute-start | bytes 2359304 | tf_op jit(solution)/shard_map/ppermute | solution.py:111
  210.4 15.0 %collective-permute-start.11 = (bf16[256,1024]{1,0:T(8,128)(2,1)S(1)}, bf16[256,1024]{1,0:T(8,128)(2,1)S(1)}, u32[]{:S(2)}, u32[]{:S(2)}) collective-permute-start(bf16[256,1024]{1,0:T(8,128)(2,1)S(1)} %fusion.16), channel_id=1, source_target_pairs={{0,2},{1,5},{2,0},{3,7},{4,6},{5,1},{6,4},{7,3},{8,10},{9,13},{10,... | collective-permute-start | bytes 1572872 | tf_op jit(solution)/shard_map/ppermute | solution.py:111
  215.1 15.2 %collective-permute-start.25 = (bf16[256,1024]{1,0:T(8,128)(2,1)S(1)}, bf16[256,1024]{1,0:T(8,128)(2,1)S(1)}, u32[]{:S(2)}, u32[]{:S(2)}) collective-permute-start(bf16[256,1024]{1,0:T(8,128)(2,1)S(1)} %fusion.17), channel_id=1, source_target_pairs={{0,2},{1,5},{2,0},{3,7},{4,6},{5,1},{6,4},{7,3},{8,10},{9,13},{10,... | collective-permute-start | bytes 1572872 | tf_op jit(solution)/shard_map/ppermute | solution.py:111
  227.0 14.9 %collective-permute-start.12 = (bf16[256,1024]{1,0:T(8,128)(2,1)S(1)}, bf16[256,1024]{1,0:T(8,128)(2,1)S(1)}, u32[]{:S(2)}, u32[]{:S(2)}) collective-permute-start(bf16[256,1024]{1,0:T(8,128)(2,1)S(1)} %fusion.18), channel_id=1, source_target_pairs={{0,4},{1,5},{2,6},{3,7},{4,0},{5,1},{6,2},{7,3},{8,12},{9,13},{10,... | collective-permute-start | bytes 1572872 | tf_op jit(solution)/shard_map/ppermute | solution.py:111
  228.8 14.9 %collective-permute-start.13 = (bf16[256,1024]{1,0:T(8,128)(2,1)S(1)}, bf16[256,1024]{1,0:T(8,128)(2,1)S(1)}, u32[]{:S(2)}, u32[]{:S(2)}) collective-permute-start(bf16[256,1024]{1,0:T(8,128)(2,1)S(1)} %fusion.19), channel_id=1, source_target_pairs={{0,2},{1,3},{2,0},{3,1},{4,6},{5,7},{6,4},{7,5},{8,10},{9,11},{10,... | collective-permute-start | bytes 1572872 | tf_op jit(solution)/shard_map/ppermute | solution.py:111
  232.0 19.8 %collective-permute-start.26 = (bf16[256,1024]{1,0:T(8,128)(2,1)S(1)}, bf16[256,1024]{1,0:T(8,128)(2,1)S(1)}, u32[]{:S(2)}, u32[]{:S(2)}) collective-permute-start(bf16[256,1024]{1,0:T(8,128)(2,1)S(1)} %fusion.20), channel_id=1, source_target_pairs={{0,4},{1,5},{2,6},{3,7},{4,0},{5,1},{6,2},{7,3},{8,12},{9,13},{10,... | collective-permute-start | bytes 1572872 | tf_op jit(solution)/shard_map/ppermute | solution.py:111
  235.7 17.8 %collective-permute-start.27 = (bf16[256,1024]{1,0:T(8,128)(2,1)S(1)}, bf16[256,1024]{1,0:T(8,128)(2,1)S(1)}, u32[]{:S(2)}, u32[]{:S(2)}) collective-permute-start(bf16[256,1024]{1,0:T(8,128)(2,1)S(1)} %fusion.21), channel_id=1, source_target_pairs={{0,2},{1,3},{2,0},{3,1},{4,6},{5,7},{6,4},{7,5},{8,10},{9,11},{10,... | collective-permute-start | bytes 1572872 | tf_op jit(solution)/shard_map/ppermute | solution.py:111
  246.0 11.3 %collective-permute-start.15 = (bf16[64,1024]{1,0:T(8,128)(2,1)S(1)}, bf16[64,1024]{1,0:T(8,128)(2,1)S(1)}, u32[]{:S(2)}, u32[]{:S(2)}) collective-permute-start(bf16[64,1024]{1,0:T(8,128)(2,1)S(1)} %get-tuple-element.6), channel_id=1, source_target_pairs={{0,16},{1,17},{2,18},{3,19},{4,20},{5,21},{6,22},{7,23},{8,24},{9,... | collective-permute-start | bytes 393224 | tf_op jit(solution)/shard_map/ppermute | solution.py:111
  246.0 11.3 %collective-permute-start.16 = (bf16[64,1024]{1,0:T(8,128)(2,1)S(1)}, bf16[64,1024]{1,0:T(8,128)(2,1)S(1)}, u32[]{:S(2)}, u32[]{:S(2)}) collective-permute-start(bf16[64,1024]{1,0:T(8,128)(2,1)S(1)} %get-tuple-element.5), channel_id=1, source_target_pairs={{0,8},{1,9},{2,10},{3,11},{4,12},{5,13},{6,14},{7,15},{8,16},{9,17... | collective-permute-start | bytes 393224 | tf_op jit(solution)/shard_map/ppermute | solution.py:111
  255.8 11.3 %collective-permute-start.29 = (bf16[64,1024]{1,0:T(8,128)(2,1)S(1)}, bf16[64,1024]{1,0:T(8,128)(2,1)S(1)}, u32[]{:S(2)}, u32[]{:S(2)}) collective-permute-start(bf16[64,1024]{1,0:T(8,128)(2,1)S(1)} %get-tuple-element.9), channel_id=1, source_target_pairs={{0,16},{1,17},{2,18},{3,19},{4,20},{5,21},{6,22},{7,23},{8,24},{9,... | collective-permute-start | bytes 393224 | tf_op jit(solution)/shard_map/ppermute | solution.py:111
  (68 other events, 622.9 us)

commit v2 on v0

--- a/solution.py
+++ b/solution.py
@@ -1,7 +1,13 @@
 import jax
 import jax.numpy as jnp
 from jax import lax
+from jax.experimental import pallas as pl
+from jax.experimental.pallas import tpu as pltpu
 from jax.sharding import PartitionSpec as P
+
+BOTH = ("expert", "tensor")
+F32 = jnp.float32
+BF16 = jnp.bfloat16
 
 
 def silu_pair(pre_act):
@@ -9,7 +15,7 @@
     return (pre_act * sigma, sigma * (1.0 + pre_act * (1.0 - sigma)))
 
 
-def local(grad_out, gate_weights, slot_lists, saved_gate, saved_up, w_gate, w_up, w_down):
+def routed_local(grad_out, gate_weights, slot_lists, saved_gate, saved_up, w_gate, w_up, w_down):
     slot_table = slot_lists[0]
     experts, capacity = slot_table.shape
     tok_count, quarter = grad_out.shape
@@ -82,6 +88,415 @@
     return (grad_in, grad_gate)
 
 
+NZ, NY, NX, NC = 4, 2, 2, 2
+
+
+def _pairs(move):
+    pairs = []
+    for z in range(NZ):
+        for y in range(NY):
+            for x in range(NX):
+                for c in range(NC):
+                    tz, ty, tx, tc = move(z, y, x, c)
+                    pairs.append((((z * NY + y) * NX + x) * NC + c, ((tz * NY + ty) * NX + tx) * NC + tc))
+    return pairs
+
+
+TO_X = _pairs(lambda z, y, x, c: (z, y, 1 - x, c))
+TO_Y = _pairs(lambda z, y, x, c: (z, 1 - y, x, c))
+TO_CORE = _pairs(lambda z, y, x, c: (z, y, x, 1 - c))
+LEFT = _pairs(lambda z, y, x, c: (z, y, 1 - x, c) if c == 0 else (z, 1 - y, x, c))
+RIGHT = _pairs(lambda z, y, x, c: (z, 1 - y, x, c) if c == 0 else (z, y, 1 - x, c))
+TO_Z = [_pairs(lambda z, y, x, c, d=d: (z ^ d, y, x, c)) for d in range(NZ)]
+CHUNKS = ((0, 2), (1, 3))
+
+
+def send(value, pairs, name="send"):
+    with jax.named_scope(name):
+        return lax.ppermute(value, BOTH, pairs)
+
+
+def after(value, *first):
+    return lax.optimization_barrier((value, *first))[0]
+
+
+def dot_nt(a, b):
+    return lax.dot_general(a, b, (((1,), (1,)), ((), ())), preferred_element_type=F32)
+
+
+def shape_of(shape, dtype):
+    return jax.ShapeDtypeStruct(shape, dtype)
+
+
+HINT = pl.CostEstimate(flops=0, transcendentals=0, bytes_accessed=0)
+LARGE = pltpu.CompilerParams(vmem_limit_bytes=48 << 20)
+
+
+def kernel(name, body, outs, grid, in_specs, out_specs, *args, scratch=()):
+    return pl.pallas_call(
+        body,
+        out_shape=outs,
+        grid_spec=pltpu.PrefetchScalarGridSpec(
+            num_scalar_prefetch=1, grid=grid, in_specs=in_specs, out_specs=out_specs, scratch_shapes=scratch
+        ),
+        compiler_params=LARGE,
+        cost_estimate=HINT,
+        name=name,
+    )(*args)
+
+
+def prepare(expert, table, saved_gate, saved_up):
+    groups, _, tokens = table.shape
+    hid = saved_gate.shape[1]
+
+    def spot(i):
+        return (i // 2) % NY, i // 4 + 2 * (i % 2)
+
+    def group(i, s):
+        dy, d = spot(i)
+        return ((s[0] // NY) ^ d) * NY + ((s[0] % NY) ^ dy)
+
+    def body(s_ref, t_ref, g_ref, u_ref, *outs):
+        slots = lax.broadcasted_iota(jnp.int32, (tokens, tokens), 0).astype(F32)
+        pick = jnp.where(slots == t_ref[0, 0:1, :], 1.0, 0.0).astype(BF16)
+        flip = (((0,), (0,)), ((), ()))
+        gate_pre = lax.dot_general(pick, g_ref[...], flip, preferred_element_type=F32)
+        up_pre = lax.dot_general(pick, u_ref[...], flip, preferred_element_type=F32)
+        scale = jnp.transpose(jnp.broadcast_to(t_ref[0, 1:2, :], (tokens, tokens)))[:, 0:1]
+        activated, derivative = silu_pair(gate_pre)
+        outs[0][...] = activated * up_pre
+        outs[1][...] = scale * up_pre * derivative
+        outs[2][...] = scale * activated
+
+    out = shape_of((groups * tokens, hid), F32)
+    saved = pl.BlockSpec((tokens, hid), lambda i, s: (group(i, s), 0))
+    row = pl.BlockSpec((1, 2, tokens), lambda i, s: (spot(i)[0] * NZ + spot(i)[1], 0, 0))
+    spec = pl.BlockSpec((tokens, hid), lambda i, s: (i, 0))
+    return kernel(
+        "prepare", body, [out] * 3, (groups,), [row, saved, saved], [spec] * 3, expert, table, saved_gate, saved_up
+    )
+
+
+def hidden_parts(block, pieces, down, got):
+    tokens, quarter = pieces[0][0].shape
+    hid = down.shape[0]
+    count = len(pieces)
+    half = count * tokens
+    rows = NY * half
+
+    def body(s_ref, *refs):
+        near = refs[: 4 * count]
+        d_ref, o_ref, mine, theirs, rows_v, w_v, row_sem, w_sem = refs[4 * count :]
+        x, c = s_ref[0] // NC, s_ref[0] % NC
+
+        def columns(q):
+            return pl.ds(pl.multiple_of(q * quarter, quarter), quarter)
+
+        def weight(dx, k):
+            source = (d_ref, o_ref)[k].at[:, columns(2 * (x ^ dx) + c)]
+            return pltpu.make_async_copy(source, w_v.at[dx, k], w_sem.at[dx, k])
+
+        def piece(i, j, dx, dy):
+            target = rows_v.at[dx, pl.ds(dy * half + i * tokens, tokens), :]
+            return pltpu.make_async_copy(near[4 * i + j], target, row_sem.at[i, dx, dy])
+
+        for dx in range(NX):
+            for k in (1, 0):
+                weight(dx, k).start()
+            for i in range(count):
+                piece(i, 0 if dx == 0 else 3, dx, dx).start()
+
+                @pl.when(c == dx)
+                def _(i=i, dx=dx):
+                    piece(i, 1, dx, 1 - dx).start()
+
+                @pl.when(c != dx)
+                def _(i=i, dx=dx):
+                    piece(i, 2, dx, 1 - dx).start()
+
+        total = [None, None]
+        for dx in range(NX):
+            for i in range(count):
+                for dy in range(NY):
+                    piece(i, 0, dx, dy).wait()
+            for k in (1, 0):
+                weight(dx, k).wait()
+                part = dot_nt(rows_v[dx], w_v[dx, k])
+                total[k] = part if dx == 0 else total[k] + part
+        theirs[...] = total[1].astype(BF16)
+        mine[...] = total[0]
+
+    flat = [p for four in pieces for p in four]
+    spec = lambda cols: pl.BlockSpec((rows, cols), lambda i, s: (0, 0))
+    return kernel(
+        "hidden",
+        body,
+        [shape_of((rows, hid), F32), shape_of((rows, hid), BF16)],
+        (1,),
+        [pl.BlockSpec(memory_space=pl.ANY)] * (len(flat) + 2),
+        [spec(hid)] * 2,
+        block,
+        *flat,
+        down,
+        got,
+        scratch=[
+            pltpu.VMEM((NX, rows, quarter), BF16),
+            pltpu.VMEM((NX, 2, hid, quarter), BF16),
+            pltpu.SemaphoreType.DMA((count, NX, NY)),
+            pltpu.SemaphoreType.DMA((NX, 2)),
+        ],
+    )
+
+
+def pre_grads(block, mine, back, factors, number):
+    rows, hid = mine.shape
+    half = rows // NY
+    tokens = factors[0].shape[0] // (NY * NZ)
+    count = half // tokens
+
+    def body(s_ref, m_ref, b_ref, f0, f1, f2, h_ref, t_ref):
+        bh = m_ref[...] + b_ref[...].astype(F32)
+        h_ref[:, :hid] = (bh * f1[...]).astype(BF16)
+        h_ref[:, hid:] = (bh * f2[...]).astype(BF16)
+        term = jnp.sum(bh * f0[...], axis=1, keepdims=True)
+        flat = jnp.transpose(jnp.broadcast_to(term, (half, 128)))
+        for i in range(count):
+            t_ref[0, i : i + 1, :] = flat[0:1, i * tokens : (i + 1) * tokens]
+
+    outs = [shape_of((rows, 2 * hid), BF16), shape_of((NY, count, tokens), F32)]
+    spec = lambda cols, first=0: pl.BlockSpec((half, cols), lambda i, s: (first + i, 0))
+    return kernel(
+        "pre_grads",
+        body,
+        outs,
+        (NY,),
+        [spec(hid)] * 2 + [spec(hid, NY * number)] * 3,
+        [spec(2 * hid), pl.BlockSpec((1, count, tokens), lambda i, s: (i, 0, 0))],
+        block,
+        mine,
+        back,
+        *factors,
+    )
+
+
+def input_parts(block, mine, theirs, weights, got, spots, types):
+    rows = mine.shape[0] // NY
+    hid = mine.shape[1] // 2
+    quarter = weights[0].shape[0] // (NX * NC)
+    steps = 2
+    wide = quarter // steps
+
+    def place(i, s):
+        c = s[0] % NC
+        pairs = [spot(c) for spot in spots]
+        dy = jnp.where(i == 0, pairs[0][0], pairs[1][0])
+        dx = jnp.where(i == 0, pairs[0][1], pairs[1][1])
+        return dy, 2 * ((s[0] // NC) ^ dx) + c
+
+    def body(s_ref, m_ref, t_ref, wg, wu, og, ou, *outs):
+        total = dot_nt(m_ref[:, :hid], wg[...]) + dot_nt(m_ref[:, hid:], wu[...])
+        total = total + dot_nt(t_ref[:, :hid], og[...]) + dot_nt(t_ref[:, hid:], ou[...])
+        for k, out in enumerate(outs):
+
+            @pl.when(pl.program_id(0) == k)
+            def _(out=out):
+                out[...] = total.astype(out.dtype)
+
+    half = pl.BlockSpec((rows, 2 * hid), lambda i, j, s: (place(i, s)[0], 0))
+    weight = pl.BlockSpec((wide, hid), lambda i, j, s: (place(i, s)[1] * steps + j, 0))
+    outs = [
+        pl.BlockSpec((rows, wide), lambda i, j, s: (0, jnp.where(i == 0, j, steps - 1))),
+        pl.BlockSpec((rows, wide), lambda i, j, s: (0, jnp.where(i == 0, 0, j))),
+    ]
+    return kernel(
+        "input",
+        body,
+        [shape_of((rows, quarter), t) for t in types],
+        (2, steps),
+        [half, half] + [weight] * 4,
+        outs,
+        block,
+        mine,
+        theirs,
+        *weights,
+        *got,
+    )
+
+
+def add_pieces(block, base, first, second, types):
+    rows, cols = base.shape
+    part = rows // len(types)
+    wide = cols // 2
+
+    def body(s_ref, b_ref, f_ref, g_ref, *outs):
+        for i, out in enumerate(outs):
+            s = slice(i * part, (i + 1) * part)
+            out[...] = (b_ref[s] + f_ref[s].astype(F32) + g_ref[s].astype(F32)).astype(out.dtype)
+
+    spec = lambda n: pl.BlockSpec((n, wide), lambda i, s: (0, i))
+    outs = [shape_of((part, cols), t) for t in types]
+    return kernel("add", body, outs, (2,), [spec(rows)] * 3, [spec(part)] * len(outs), block, base, first, second)
+
+
+def add_corner(block, base, corner):
+    rows, cols = base.shape
+
+    def body(s_ref, b_ref, c_ref, out):
+        out[...] = (b_ref[...].astype(F32) + c_ref[...].astype(F32)).astype(BF16)
+
+    spec = pl.BlockSpec((rows, cols // 2), lambda i, s: (0, i))
+    return kernel("corner", body, shape_of(base.shape, BF16), (2,), [spec] * 2, spec, block, base, corner)
+
+
+def last_sum(block, keep, parts):
+    def body(s_ref, k_ref, *refs):
+        total = k_ref[...]
+        for ref in refs[:-1]:
+            total = total + ref[...].astype(F32)
+        refs[-1][...] = total.astype(BF16)
+
+    spec = pl.BlockSpec(keep.shape, lambda i, s: (0, 0))
+    return kernel(
+        "last", body, shape_of(keep.shape, BF16), (1,), [spec] * (1 + len(parts)), spec, block, keep, *parts
+    )
+
+
+def dense_local(grad_out, gate_weights, slot_lists, saved_gate, saved_up, w_gate, w_up, w_down):
+    tokens, quarter = grad_out.shape
+    experts = slot_lists.shape[1]
+    top_count = gate_weights.shape[1]
+    expert = lax.axis_index("expert")
+    block = lax.axis_index("tensor")
+    z, y = expert // NY, expert % NY
+    at_expert, at_block = expert.reshape(1), block.reshape(1)
+
+    down, gate_w, up_w = w_down[0], w_gate[0], w_up[0]
+
+    entries = slot_lists[0]
+    owner, choice = entries // top_count, entries % top_count
+    token_ids = jnp.arange(tokens, dtype=jnp.int32)
+    hit = owner[:, :, None] == token_ids[None, None, :]
+    choice_of = jnp.sum(jnp.where(hit, choice[:, :, None], 0), axis=1)
+    slot_of = jnp.sum(jnp.where(hit, token_ids[None, :, None], 0), axis=1)
+    choice_ids = jnp.arange(top_count, dtype=jnp.int32)
+    chosen = choice_of[:, :, None] == choice_ids[None, None, :]
+    gate_of = jnp.sum(jnp.where(chosen, gate_weights[None].astype(F32), 0.0), axis=2)
+    table = jnp.stack([slot_of.astype(F32), gate_of], axis=1).reshape(NZ, NY, 2, tokens)
+
+    own = grad_out
+    z2, z1 = send(own, TO_Z[2], "z2"), send(own, TO_Z[1], "z1")
+    first0, second0 = send(own, RIGHT, "first0"), send(own, LEFT, "second0")
+    got_down = send(down, TO_CORE, "weights")
+
+    own_, z2, z1, first0, second0, got_down, table = lax.optimization_barrier(
+        (own, z2, z1, first0, second0, got_down, table)
+    )
+    z3 = send(own_, TO_Z[3], "z3")
+    first2, second2 = send(z2, RIGHT, "first2"), send(z2, LEFT, "second2")
+    third0 = send(first0, LEFT, "third0")
+    line = []
+    for d in range(NZ):
+        part = lax.dynamic_index_in_dim(table, z ^ d, axis=0, keepdims=False)
+        line.append(part if d == 0 else send(part, TO_Z[d], "meta"))
+    line = jnp.stack(line)
+    gate_w_, up_w_ = after(gate_w, table), after(up_w, table)
+    got_gate, got_up = send(gate_w_, TO_CORE, "weights"), send(up_w_, TO_CORE, "weights")
+
+    z1, z3, first2, second2, third0, line, got_gate, got_up = lax.optimization_barrier(
+        (z1, z3, first2, second2, third0, line, got_gate, got_up)
+    )
+    first1, second1 = send(z1, RIGHT, "first1"), send(z1, LEFT, "second1")
+    third2 = send(first2, LEFT, "third2")
+    near = lax.dynamic_index_in_dim(line, y, axis=1, keepdims=False)
+    far = send(lax.dynamic_index_in_dim(line, 1 - y, axis=1, keepdims=False), TO_Y, "meta_y")
+    table = jnp.concatenate([near, far], axis=0)
+
+    z3, first1, second1, third2, table = lax.optimization_barrier((z3, first1, second1, third2, table))
+    first3, second3 = send(z3, RIGHT, "first3"), send(z3, LEFT, "second3")
+    third1 = send(first1, LEFT, "third1")
+    factors = prepare(at_expert, table, saved_gate[0], saved_up[0])
+
+    pieces = {0: (own, first0, second0, third0), 2: (z2, first2, second2, third2)}
+
+    weights, got = (gate_w, up_w), (got_gate, got_up)
+    near, far = CHUNKS
+
+    def stage_hidden(place, chunk):
+        mine, theirs = hidden_parts(place, [pieces[d] for d in chunk], down, got_down)
+        return mine, send(theirs, TO_CORE, f"swap_bh{chunk[0]}"), after(at_block, mine)
+
+    def stage_pre(place, chunk, mine, back):
+        mine, term = pre_grads(place, mine, back, factors, CHUNKS.index(chunk))
+        return mine, send(mine, TO_CORE, f"swap_h{chunk[0]}"), term, after(at_block, mine)
+
+    def stage_out(place, chunk, mine, theirs):
+        a, b = input_parts(
+            place, mine, theirs, weights, got, (lambda c: (1, 1), lambda c: (c, 1 - c)), (BF16, BF16)
+        )
+        corner = send(a, LEFT, f"r_corner{chunk[0]}")
+        right = send(b, LEFT, f"r_right{chunk[0]}")
+        return corner, right, after(at_block, a)
+
+    def stage_keep(place, mine, theirs):
+        base, left = input_parts(
+            place, mine, theirs, weights, got, (lambda c: (0, 0), lambda c: (1 - c, c)), (F32, BF16)
+        )
+        return base, left, after(at_block, base)
+
+    def stage_corner(place, chunk, left, corner):
+        value = add_corner(place, left, corner)
+        return send(value, RIGHT, f"r_left{chunk[0]}"), after(at_block, value)
+
+    def stage_add(place, chunk, base, right, left):
+        types = [F32 if d == 0 else BF16 for d in chunk]
+        totals = add_pieces(place, base, right, left, types)
+        sums = {d: t if d == 0 else send(t, TO_Z[d], f"r_z{d}") for d, t in zip(chunk, totals)}
+        return sums, after(at_block, totals[0])
+
+    place = after(at_block, factors[0])
+    mine_a, back, place = stage_hidden(place, near)
+    mine_a, theirs_a, term_a, place = stage_pre(place, near, mine_a, back)
+    theirs_a, first3, second3, third1 = lax.optimization_barrier((theirs_a, first3, second3, third1))
+    third3 = send(first3, LEFT, "third3")
+    pieces |= {1: (z1, first1, second1, third1), 3: (z3, first3, second3, third3)}
+    corner_a, right_a, place = stage_out(place, near, mine_a, theirs_a)
+    base_a, left_a, place = stage_keep(place, mine_a, theirs_a)
+    mine_b, back, place = stage_hidden(place, far)
+    left_a, place = stage_corner(place, near, left_a, corner_a)
+    mine_b, theirs_b, term_b, place = stage_pre(place, far, mine_b, back)
+    corner_b, right_b, place = stage_out(place, far, mine_b, theirs_b)
+    base_b, left_b, place = stage_keep(place, mine_b, theirs_b)
+    sums, place = stage_add(place, near, base_a, right_a, left_a)
+    left_b, place = stage_corner(place, far, left_b, corner_b)
+    more, place = stage_add(place, far, base_b, right_b, left_b)
+    sums.update(more)
+    grad_in = last_sum(place, sums[0], [sums[d] for d in (2, 1, 3)])
+
+    terms = {d: t[:, i] for c, t in ((near, term_a), (far, term_b)) for i, d in enumerate(c)}
+    term = jnp.stack([terms[d] for d in range(NZ)], axis=1)
+    term = term + send(term, TO_CORE, "t_core")
+    term = term + send(term, TO_X, "t_x")
+    term = jnp.stack([term[0], send(term[1], TO_Y, "t_y")], axis=1)
+    slots = [term[0]] + [send(term[d], TO_Z[d], f"t_z{d}") for d in range(1, NZ)]
+    slot_grad = jnp.zeros((experts, tokens), F32)
+    ids = jnp.arange(experts, dtype=jnp.int32)
+    for d in range(NZ):
+        for dy in range(NY):
+            source = (z ^ d) * NY + (y ^ dy)
+            slot_grad = jnp.where((ids == source)[:, None], slots[d][dy][None], slot_grad)
+    grad_gate = jnp.sum(jnp.where(chosen, slot_grad[:, :, None], 0.0), axis=0)
+    return (grad_in, grad_gate)
+
+
+def local(grad_out, gate_weights, slot_lists, *rest):
+    tokens = grad_out.shape[0]
+    _, experts, capacity = slot_lists.shape
+    dense = experts == gate_weights.shape[1] == NZ * NY and capacity == tokens
+    dense = dense and lax.axis_size("expert") == NZ * NY and lax.axis_size("tensor") == NX * NC
+    program = dense_local if dense else routed_local
+    return program(grad_out, gate_weights, slot_lists, *rest)
+
+
 def solution(mesh):
     in_specs = (
         P("expert", "tensor"),

time: 379 us -> 158 us (0.42)
  blocking collectives: 260 us -> 0 us
  starting transfers between devices: 3.66 us -> 49.7 us
  Pallas kernels: 0 us -> 40.9 us
  matrix products: 36.7 us -> 0 us
  between operations: 14.1 us -> 0.99 us
  waiting for transfers between devices: 40.9 us -> 53.5 us
  other arithmetic: 8.5 us -> 2.51 us
  local copies, waits for them, and re-layouts: 14.9 us -> 9.93 us
    all_to_all x3 -> x0, blocking collectives: 254 us -> none  [the longest x1 189 us: local(): lax.all_to_all(partial_rows, 'expert', split_axis=1, concat_axis=1, tiled...]
    ppermute x0 -> x41, waiting for transfers between devices: none -> 53.5 us  [send(): return lax.ppermute(value, BOTH, pairs)]
    ppermute x0 -> x41, starting transfers between devices: none -> 49.7 us  [send(): return lax.ppermute(value, BOTH, pairs)]
    pallas_call x0 -> x14, Pallas kernels: none -> 40.9 us  [kernel(): pl.pallas_call(body, out_shape=outs, grid_spec=pltpu.PrefetchScalarGridSp...]
    all_gather x1 -> x0, waiting for transfers between devices: 39.1 us -> none  [local(): lax.all_gather(routed, 'tensor', axis=1, tiled=True)]
    dot_general x5 -> x0, matrix products: 36.7 us -> none  [the longest x1 15.3 us: local(): lax.dot_general(up_proj, grad_pre_up, contract, preferred_element_type=jn...]
    scatter-add x1 -> x0, other arithmetic: 7.62 us -> none  [local(): jnp.zeros((tok_count * top_count + 1,), jnp.float32).at[position]]
    gather x1 -> x0, local copies, waits for them, and re-layouts: 6.8 us -> none  [local(): gate_weights.reshape(-1)[jnp.maximum(entries, 0)]]
  transfers between devices with their start and end apart: 3 -> 41, of which waited for: 2 -> 21; matrix products, arithmetic and copies ran while one was open for 5% -> 2% of each run, Pallas kernels for 0% -> 18%
where the time goes in v2:
time: 158 us
  waiting for transfers between devices  53.5 us (34%)
  starting transfers between devices  49.7 us (31%)
  Pallas kernels  40.9 us (26%)
  local copies, waits for them, and re-layouts  9.93 us (6%)
  other arithmetic  2.51 us (2%)
    ppermute x41, waiting for transfers between devices, send(): return lax.ppermute(value, BOTH, pairs)  53.5 us
    ppermute x41, starting transfers between devices, send(): return lax.ppermute(value, BOTH, pairs)  49.7 us
    pallas_call x14, Pallas kernels, kernel(): pl.pallas_call(body, out_shape=outs, grid_spec=pltpu.PrefetchScalarGridSp...  40.9 us
    unnamed x36, local copies, waits for them, and re-layouts  9.88 us
  transfers between devices with their start and end apart: 41, of which 21 were waited for; matrix products, arithmetic and copies ran while one was open for 2% of the time, Pallas kernels for 18%

profile of v2, /device:TPU:0, one launch (start us, length us, event | category | flops | bytes accessed | tf_op | source)
XLA Modules:
  0.0 157.6 jit_solution(3204498763065575293)
XLA Ops:
  1.1 3.7 %collective-permute-start = (bf16[128,1024]{1,0:T(8,128)(2,1)}, bf16[128,1024]{1,0:T(8,128)(2,1)S(1)}, u32[]{:S(2)}, u32[]{:S(2)}) collective-permute-start(bf16[128,1024]{1,0:T(8,128)(2,1)} %refs_0_.1), channel_id=1, source_target_pairs={{0,16},{1,17},{2,18},{3,19},{4,20},{5,21},{6,22},{7,23},{8,24},{9,... | collective-permute-start | bytes 786440 | tf_op jit(solution)/shard_map/z2/ppermute | solution.py:116
  11.2 6.5 %collective-permute-done.refs_4_ = bf16[128,1024]{1,0:T(8,128)(2,1)S(1)} collective-permute-done((bf16[128,1024]{1,0:T(8,128)(2,1)}, bf16[128,1024]{1,0:T(8,128)(2,1)S(1)}, u32[]{:S(2)}, u32[]{:S(2)}) %collective-permute-start) | collective-permute-done | bytes 262176 | tf_op jit(solution)/shard_map/z2/ppermute | solution.py:116
  21.2 3.3 %collective-permute-start.11 = (f32[2,2,128]{2,0,1:T(2,128)S(1)}, f32[2,2,128]{2,0,1:T(2,128)S(1)}, u32[]{:S(2)}, u32[]{:S(2)}) collective-permute-start(f32[2,2,128]{2,0,1:T(2,128)S(1)} %get-tuple-element.131), channel_id=1, source_target_pairs={{0,24},{1,25},{2,26},{3,27},{4,28},{5,29},{6,30},{7,31},{8,16},{9,... | collective-permute-start | bytes 6152 | tf_op jit(solution)/shard_map/meta/ppermute | solution.py:116
  24.4 2.1 %collective-permute-done.11 = f32[2,2,128]{2,0,1:T(2,128)S(1)} collective-permute-done((f32[2,2,128]{2,0,1:T(2,128)S(1)}, f32[2,2,128]{2,0,1:T(2,128)S(1)}, u32[]{:S(2)}, u32[]{:S(2)}) %collective-permute-start.11) | collective-permute-done | bytes 2080 | tf_op jit(solution)/shard_map/meta/ppermute | solution.py:116
  32.5 3.3 %collective-permute-start.5 = (bf16[128,1024]{1,0:T(8,128)(2,1)}, bf16[128,1024]{1,0:T(8,128)(2,1)S(1)}, u32[]{:S(2)}, u32[]{:S(2)}) collective-permute-start(bf16[128,1024]{1,0:T(8,128)(2,1)} %refs_0_.1), channel_id=1, source_target_pairs={{0,24},{1,25},{2,26},{3,27},{4,28},{5,29},{6,30},{7,31},{8,16},{9,... | collective-permute-start | bytes 786440 | tf_op jit(solution)/shard_map/z3/ppermute | solution.py:116
  37.4 3.6 %collective-permute-done.5.refs_4_ = bf16[128,1024]{1,0:T(8,128)(2,1)S(1)} collective-permute-done((bf16[128,1024]{1,0:T(8,128)(2,1)}, bf16[128,1024]{1,0:T(8,128)(2,1)S(1)}, u32[]{:S(2)}, u32[]{:S(2)}) %collective-permute-start.5) | collective-permute-done | bytes 262176 | tf_op jit(solution)/shard_map/z3/ppermute | solution.py:116
  45.1 3.8 %collective-permute-done.17 = f32[4,2,128]{2,1,0:T(2,128)S(1)} collective-permute-done((f32[4,2,128]{2,1,0:T(2,128)S(1)}, f32[4,2,128]{2,1,0:T(2,128)S(1)}, u32[]{:S(2)}, u32[]{:S(2)}) %collective-permute-start.17) | collective-permute-done | bytes 4128 | tf_op jit(solution)/shard_map/meta_y/ppermute | solution.py:116
  52.9 4.1 %prepare.1 = (f32[1024,384]{1,0:T(8,128)S(1)}, f32[1024,384]{1,0:T(8,128)S(1)}, f32[1024,384]{1,0:T(8,128)}) custom-call(s32[1]{0:T(128)} %bitcast.1.s_ref, f32[8,2,128]{2,1,0:T(2,128)S(1)} %pad_maximum_fusion.2.t_ref, bf16[1024,384]{1,0:T(8,128)(2,1)S(1)} %bitcast.79, bf16[1024,384]{1,0:T(8,128)(2,1)S(1)} %bitcast.80), custom_call_target="tpu_custom_call" | custom-call | tf_op jit(solution)/shard_map/prepare/pallas_call | solution.py:136
  58.2 4.3 %hidden.2 = (f32[512,384]{1,0:T(8,128)S(1)}, bf16[512,384]{1,0:T(8,128)(2,1)S(1)}) custom-call(s32[1]{0:T(128)} %bitcast.s_ref, bf16[128,1024]{1,0:T(8,128)(2,1)S(1)} %copy-done.15, bf16[128,1024]{1,0:T(8,128)(2,1)S(1)} %collective-permute-done.2.refs_1_, bf16[128,1024]{1,0:T(8,128)(2,1)S(1)} %collective-permute-done.3.refs_2_, ...), custom_call_target="tpu_custom_call" | custom-call | tf_op jit(solution)/shard_map/hidden/pallas_call | solution.py:136
  69.5 5.5 %collective-permute-done.20.refs_5_ = bf16[128,1024]{1,0:T(8,128)(2,1)S(1)} collective-permute-done((bf16[128,1024]{1,0:T(8,128)(2,1)S(1)}, bf16[128,1024]{1,0:T(8,128)(2,1)S(1)}, u32[]{:S(2)}, u32[]{:S(2)}) %collective-permute-start.20) | collective-permute-done | bytes 262176 | tf_op jit(solution)/shard_map/first3/ppermute | solution.py:116
  75.1 2.3 %collective-permute-done.22.refs_3_ = bf16[128,1024]{1,0:T(8,128)(2,1)S(1)} collective-permute-done((bf16[128,1024]{1,0:T(8,128)(2,1)S(1)}, bf16[128,1024]{1,0:T(8,128)(2,1)S(1)}, u32[]{:S(2)}, u32[]{:S(2)}) %collective-permute-start.22) | collective-permute-done | bytes 262176 | tf_op jit(solution)/shard_map/third1/ppermute | solution.py:116
  77.8 5.1 %input.4 = (bf16[256,1024]{1,0:T(8,128)(2,1)S(1)}, bf16[256,1024]{1,0:T(8,128)(2,1)S(1)}) custom-call(s32[1]{0:T(128)} %bitcast.s_ref, bf16[512,768]{1,0:T(8,128)(2,1)S(1)} %get-tuple-element.88.m_ref, bf16[512,768]{1,0:T(8,128)(2,1)S(1)} %collective-permute-done.19.t_ref, bf16[4096,384]{1,0:T(8,128)(2,1)S(1)} %bitcast.77, bf16[4096,384]{1,0:T(8,128)(2,1)} %bitcast.82, ...), custom_call_target="tpu_custom_call" | custom-call | tf_op jit(solution)/shard_map/input/pallas_call | solution.py:136
  87.6 5.4 %input.5 = (f32[256,1024]{1,0:T(8,128)S(1)}, bf16[256,1024]{1,0:T(8,128)(2,1)S(1)}) custom-call(s32[1]{0:T(128)} %bitcast.s_ref, bf16[512,768]{1,0:T(8,128)(2,1)S(1)} %copy-done.7, bf16[512,768]{1,0:T(8,128)(2,1)S(1)} %copy-done.9, bf16[4096,384]{1,0:T(8,128)(2,1)} %bitcast.75, bf16[4096,384]{1,0:T(8,128)(2,1)} %bitcast.83, ...), custom_call_target="tpu_custom_call" | custom-call | tf_op jit(solution)/shard_map/input/pallas_call | solution.py:136
  94.0 4.5 %hidden.3 = (f32[512,384]{1,0:T(8,128)S(1)}, bf16[512,384]{1,0:T(8,128)(2,1)S(1)}) custom-call(s32[1]{0:T(128)} %bitcast.s_ref, bf16[128,1024]{1,0:T(8,128)(2,1)S(1)} %collective-permute-done.1.refs_0_, bf16[128,1024]{1,0:T(8,128)(2,1)S(1)} %collective-permute-done.14.refs_1_, bf16[128,1024]{1,0:T(8,128)(2,1)S(1)} %collective-permute-done.15.refs_2_, ...), custom_call_target="tpu_custom_call" | custom-call | tf_op jit(solution)/shard_map/hidden/pallas_call | solution.py:136
  100.3 2.3 %pre_grads.3 = (bf16[512,768]{1,0:T(8,128)(2,1)}, f32[2,2,128]{2,1,0:T(2,128)S(1)}) custom-call(s32[1]{0:T(128)} %bitcast.s_ref, f32[512,384]{1,0:T(8,128)S(1)} %get-tuple-element.103.m_ref, bf16[512,384]{1,0:T(8,128)(2,1)S(1)} %collective-permute-done.25.b_ref, f32[1024,384]{1,0:T(8,128)S(1)} %copy-done.3, f32[1024,384]{1,0:T(8,128)S(1)} %copy-done.5, ...), custom_call_target="tpu_custom_call" | custom-call | tf_op jit(solution)/shard_map/pre_grads/pallas_call | solution.py:136
  109.2 5.6 %input.6 = (bf16[256,1024]{1,0:T(8,128)(2,1)S(1)}, bf16[256,1024]{1,0:T(8,128)(2,1)S(1)}) custom-call(s32[1]{0:T(128)} %bitcast.s_ref, bf16[512,768]{1,0:T(8,128)(2,1)} %get-tuple-element.108.m_ref, bf16[512,768]{1,0:T(8,128)(2,1)} %collective-permute-done.26.t_ref, bf16[4096,384]{1,0:T(8,128)(2,1)S(1)} %bitcast.78, bf16[4096,384]{1,0:T(8,128)(2,1)} %bitcast.84, ...), custom_call_target="tpu_custom_call" | custom-call | tf_op jit(solution)/shard_map/input/pallas_call | solution.py:136
  115.4 5.3 %collective-permute-done.37 = f32[4,128]{1,0:T(4,128)S(1)} collective-permute-done((f32[4,128]{1,0:T(4,128)S(1)}, f32[4,128]{1,0:T(4,128)S(1)}, u32[]{:S(2)}, u32[]{:S(2)}) %collective-permute-start.37) | collective-permute-done | bytes 2080 | tf_op jit(solution)/shard_map/t_y/ppermute | solution.py:116
  120.7 3.5 %collective-permute-start.38 = (f32[2,128]{1,0:T(2,128)S(1)}, f32[2,128]{1,0:T(2,128)S(1)}, u32[]{:S(2)}, u32[]{:S(2)}) collective-permute-start(f32[2,128]{1,0:T(2,128)S(1)} %bitcast.99), channel_id=1, source_target_pairs={{0,24},{1,25},{2,26},{3,27},{4,28},{5,29},{6,30},{7,31},{8,16},{9,... | collective-permute-start | bytes 3080 | tf_op jit(solution)/shard_map/t_z3/ppermute | solution.py:116
  124.2 3.2 %collective-permute-start.39 = (f32[2,128]{1,0:T(2,128)S(1)}, f32[2,128]{1,0:T(2,128)S(1)}, u32[]{:S(2)}, u32[]{:S(2)}) collective-permute-start(f32[2,128]{1,0:T(2,128)S(1)} %bitcast.98), channel_id=1, source_target_pairs={{0,16},{1,17},{2,18},{3,19},{4,20},{5,21},{6,22},{7,23},{8,24},{9,... | collective-permute-start | bytes 3080 | tf_op jit(solution)/shard_map/t_z2/ppermute | solution.py:116
  127.3 6.0 %input.7 = (f32[256,1024]{1,0:T(8,128)S(1)}, bf16[256,1024]{1,0:T(8,128)(2,1)S(1)}) custom-call(s32[1]{0:T(128)} %bitcast.s_ref, bf16[512,768]{1,0:T(8,128)(2,1)} %get-tuple-element.108.m_ref, bf16[512,768]{1,0:T(8,128)(2,1)} %collective-permute-done.26.t_ref, bf16[4096,384]{1,0:T(8,128)(2,1)} %bitcast.76, bf16[4096,384]{1,0:T(8,128)(2,1)} %bitcast.85, ...), custom_call_target="tpu_custom_call" | custom-call | tf_op jit(solution)/shard_map/input/pallas_call | solution.py:136
  138.1 6.0 %collective-permute-done.30.f_ref = bf16[256,1024]{1,0:T(8,128)(2,1)S(1)} collective-permute-done((bf16[256,1024]{1,0:T(8,128)(2,1)S(1)}, bf16[256,1024]{1,0:T(8,128)(2,1)S(1)}, u32[]{:S(2)}, u32[]{:S(2)}) %collective-permute-start.30) | collective-permute-done | bytes 524320 | tf_op jit(solution)/shard_map/r_right1/ppermute | solution.py:116
  145.0 2.0 %collective-permute-start.33 = (bf16[128,1024]{1,0:T(8,128)(2,1)S(1)}, bf16[128,1024]{1,0:T(8,128)(2,1)S(1)}, u32[]{:S(2)}, u32[]{:S(2)}) collective-permute-start(bf16[128,1024]{1,0:T(8,128)(2,1)S(1)} %get-tuple-element.120), channel_id=1, source_target_pairs={{0,8},{1,9},{2,10},{3,11},{4,12},{5,13},{6,14},{7,15},{8,0},{9,1},... | collective-permute-start | bytes 786440 | tf_op jit(solution)/shard_map/r_z1/ppermute | solution.py:116
  150.2 4.3 %collective-permute-done.33.refs_1_ = bf16[128,1024]{1,0:T(8,128)(2,1)S(1)} collective-permute-done((bf16[128,1024]{1,0:T(8,128)(2,1)S(1)}, bf16[128,1024]{1,0:T(8,128)(2,1)S(1)}, u32[]{:S(2)}, u32[]{:S(2)}) %collective-permute-start.33) | collective-permute-done | bytes 262176 | tf_op jit(solution)/shard_map/r_z1/ppermute | solution.py:116
  154.4 2.3 %collective-permute-done.34.refs_2_ = bf16[128,1024]{1,0:T(8,128)(2,1)S(1)} collective-permute-done((bf16[128,1024]{1,0:T(8,128)(2,1)S(1)}, bf16[128,1024]{1,0:T(8,128)(2,1)S(1)}, u32[]{:S(2)}, u32[]{:S(2)}) %collective-permute-start.34) | collective-permute-done | bytes 262176 | tf_op jit(solution)/shard_map/r_z3/ppermute | solution.py:116
  (138 shorter events, 58.7 us)
Async XLA Ops:
  0.6 17.2 %collective-permute-start.4 = (bf16[384,4096]{1,0:T(8,128)(2,1)}, bf16[384,4096]{1,0:T(8,128)(2,1)S(1)}, u32[]{:S(2)}, u32[]{:S(2)}) collective-permute-start(bf16[384,4096]{1,0:T(8,128)(2,1)} %bitcast.86), channel_id=1, source_target_pairs={{0,1},{1,0},{2,3},{3,2},{4,5},{5,4},{6,7},{7,6},{8,9},{9,8},{10,11... | collective-permute-start | bytes 9437192 | tf_op jit(solution)/shard_map/weights/ppermute | solution.py:116
  1.1 16.5 %collective-permute-start = (bf16[128,1024]{1,0:T(8,128)(2,1)}, bf16[128,1024]{1,0:T(8,128)(2,1)S(1)}, u32[]{:S(2)}, u32[]{:S(2)}) collective-permute-start(bf16[128,1024]{1,0:T(8,128)(2,1)} %refs_0_.1), channel_id=1, source_target_pairs={{0,16},{1,17},{2,18},{3,19},{4,20},{5,21},{6,22},{7,23},{8,24},{9,... | collective-permute-start | bytes 786440 | tf_op jit(solution)/shard_map/z2/ppermute | solution.py:116
  4.8 13.0 %collective-permute-start.1 = (bf16[128,1024]{1,0:T(8,128)(2,1)}, bf16[128,1024]{1,0:T(8,128)(2,1)S(1)}, u32[]{:S(2)}, u32[]{:S(2)}) collective-permute-start(bf16[128,1024]{1,0:T(8,128)(2,1)} %refs_0_.1), channel_id=1, source_target_pairs={{0,8},{1,9},{2,10},{3,11},{4,12},{5,13},{6,14},{7,15},{8,0},{9,1},... | collective-permute-start | bytes 786440 | tf_op jit(solution)/shard_map/z1/ppermute | solution.py:116
  6.4 11.4 %collective-permute-start.2 = (bf16[128,1024]{1,0:T(8,128)(2,1)}, bf16[128,1024]{1,0:T(8,128)(2,1)S(1)}, u32[]{:S(2)}, u32[]{:S(2)}) collective-permute-start(bf16[128,1024]{1,0:T(8,128)(2,1)} %refs_0_.1), channel_id=1, source_target_pairs={{0,4},{1,3},{2,6},{3,1},{4,0},{5,7},{6,2},{7,5},{8,12},{9,11},{10,... | collective-permute-start | bytes 786440 | tf_op jit(solution)/shard_map/first0/ppermute | solution.py:116
  7.9 9.9 %collective-permute-start.3 = (bf16[128,1024]{1,0:T(8,128)(2,1)}, bf16[128,1024]{1,0:T(8,128)(2,1)S(1)}, u32[]{:S(2)}, u32[]{:S(2)}) collective-permute-start(bf16[128,1024]{1,0:T(8,128)(2,1)} %refs_0_.1), channel_id=1, source_target_pairs={{0,2},{1,5},{2,0},{3,7},{4,6},{5,1},{6,4},{7,3},{8,10},{9,13},{10,... | collective-permute-start | bytes 786440 | tf_op jit(solution)/shard_map/second0/ppermute | solution.py:116
  17.9 23.1 %collective-permute-start.12 = (bf16[4096,384]{1,0:T(8,128)(2,1)}, bf16[4096,384]{1,0:T(8,128)(2,1)}, u32[]{:S(2)}, u32[]{:S(2)}) collective-permute-start(bf16[4096,384]{1,0:T(8,128)(2,1)} %bitcast.74), channel_id=1, source_target_pairs={{0,1},{1,0},{2,3},{3,2},{4,5},{5,4},{6,7},{7,6},{8,9},{9,8},{10,11... | collective-permute-start | bytes 9437192 | tf_op jit(solution)/shard_map/weights/ppermute | solution.py:116
  19.6 21.4 %collective-permute-start.13 = (bf16[4096,384]{1,0:T(8,128)(2,1)}, bf16[4096,384]{1,0:T(8,128)(2,1)}, u32[]{:S(2)}, u32[]{:S(2)}) collective-permute-start(bf16[4096,384]{1,0:T(8,128)(2,1)} %bitcast.81), channel_id=1, source_target_pairs={{0,1},{1,0},{2,3},{3,2},{4,5},{5,4},{6,7},{7,6},{8,9},{9,8},{10,11... | collective-permute-start | bytes 9437192 | tf_op jit(solution)/shard_map/weights/ppermute | solution.py:116
  19.6 13.0 %collective-permute-start.6 = (bf16[128,1024]{1,0:T(8,128)(2,1)S(1)}, bf16[128,1024]{1,0:T(8,128)(2,1)S(1)}, u32[]{:S(2)}, u32[]{:S(2)}) collective-permute-start(bf16[128,1024]{1,0:T(8,128)(2,1)S(1)} %collective-permute-done.refs_4_), channel_id=1, source_target_pairs={{0,4},{1,3},{2,6},{3,1},{4,0},{5,7},{6,2},{7,5},{8,12},{9,11},{10,... | collective-permute-start | bytes 786440 | tf_op jit(solution)/shard_map/first2/ppermute | solution.py:116
  65.8 11.6 %collective-permute-start.19 = (bf16[512,768]{1,0:T(8,128)(2,1)S(1)}, bf16[512,768]{1,0:T(8,128)(2,1)S(1)}, u32[]{:S(2)}, u32[]{:S(2)}) collective-permute-start(bf16[512,768]{1,0:T(8,128)(2,1)S(1)} %get-tuple-element.88.m_ref), channel_id=1, source_target_pairs={{0,1},{1,0},{2,3},{3,2},{4,5},{5,4},{6,7},{7,6},{8,9},{9,8},{10,11... | collective-permute-start | bytes 2359304 | tf_op jit(solution)/shard_map/swap_h0/ppermute | solution.py:116
  66.0 9.1 %collective-permute-start.20 = (bf16[128,1024]{1,0:T(8,128)(2,1)S(1)}, bf16[128,1024]{1,0:T(8,128)(2,1)S(1)}, u32[]{:S(2)}, u32[]{:S(2)}) collective-permute-start(bf16[128,1024]{1,0:T(8,128)(2,1)S(1)} %collective-permute-done.5.refs_4_), channel_id=1, source_target_pairs={{0,4},{1,3},{2,6},{3,1},{4,0},{5,7},{6,2},{7,5},{8,12},{9,11},{10,... | collective-permute-start | bytes 786440 | tf_op jit(solution)/shard_map/first3/ppermute | solution.py:116
  68.0 9.3 %collective-permute-start.22 = (bf16[128,1024]{1,0:T(8,128)(2,1)S(1)}, bf16[128,1024]{1,0:T(8,128)(2,1)S(1)}, u32[]{:S(2)}, u32[]{:S(2)}) collective-permute-start(bf16[128,1024]{1,0:T(8,128)(2,1)S(1)} %collective-permute-done.14.refs_1_), channel_id=1, source_target_pairs={{0,2},{1,5},{2,0},{3,7},{4,6},{5,1},{6,4},{7,3},{8,10},{9,13},{10,... | collective-permute-start | bytes 786440 | tf_op jit(solution)/shard_map/third1/ppermute | solution.py:116
  77.4 16.6 %collective-permute-start.23 = (bf16[128,1024]{1,0:T(8,128)(2,1)S(1)}, bf16[128,1024]{1,0:T(8,128)(2,1)S(1)}, u32[]{:S(2)}, u32[]{:S(2)}) collective-permute-start(bf16[128,1024]{1,0:T(8,128)(2,1)S(1)} %collective-permute-done.20.refs_5_), channel_id=1, source_target_pairs={{0,2},{1,5},{2,0},{3,7},{4,6},{5,1},{6,4},{7,3},{8,10},{9,13},{10,... | collective-permute-start | bytes 786440 | tf_op jit(solution)/shard_map/third3/ppermute | solution.py:116
  83.7 14.8 %collective-permute-start.24 = (bf16[256,1024]{1,0:T(8,128)(2,1)S(1)}, bf16[256,1024]{1,0:T(8,128)(2,1)S(1)}, u32[]{:S(2)}, u32[]{:S(2)}) collective-permute-start(bf16[256,1024]{1,0:T(8,128)(2,1)S(1)} %get-tuple-element.95), channel_id=1, source_target_pairs={{0,2},{1,5},{2,0},{3,7},{4,6},{5,1},{6,4},{7,3},{8,10},{9,13},{10,... | collective-permute-start | bytes 1572872 | tf_op jit(solution)/shard_map/r_corner0/ppermute | solution.py:116
  104.4 28.9 %collective-permute-start.27 = (bf16[256,1024]{1,0:T(8,128)(2,1)}, bf16[256,1024]{1,0:T(8,128)(2,1)S(1)}, u32[]{:S(2)}, u32[]{:S(2)}) collective-permute-start(bf16[256,1024]{1,0:T(8,128)(2,1)} %copy-done.16), channel_id=1, source_target_pairs={{0,2},{1,5},{2,0},{3,7},{4,6},{5,1},{6,4},{7,3},{8,10},{9,13},{10,... | collective-permute-start | bytes 1572872 | tf_op jit(solution)/shard_map/r_right0/ppermute | solution.py:116
  106.0 27.4 %collective-permute-start.28 = (bf16[256,1024]{1,0:T(8,128)(2,1)}, bf16[256,1024]{1,0:T(8,128)(2,1)S(1)}, u32[]{:S(2)}, u32[]{:S(2)}) collective-permute-start(bf16[256,1024]{1,0:T(8,128)(2,1)} %copy-done.14), channel_id=1, source_target_pairs={{0,4},{1,3},{2,6},{3,1},{4,0},{5,7},{6,2},{7,5},{8,12},{9,11},{10,... | collective-permute-start | bytes 1572872 | tf_op jit(solution)/shard_map/r_left0/ppermute | solution.py:116
  107.6 13.1 %collective-permute-start.37 = (f32[4,128]{1,0:T(4,128)S(1)}, f32[4,128]{1,0:T(4,128)S(1)}, u32[]{:S(2)}, u32[]{:S(2)}) collective-permute-start(f32[4,128]{1,0:T(4,128)S(1)} %get-tuple-element.138), channel_id=1, source_target_pairs={{0,4},{1,5},{2,6},{3,7},{4,0},{5,1},{6,2},{7,3},{8,12},{9,13},{10,... | collective-permute-start | bytes 6152 | tf_op jit(solution)/shard_map/t_y/ppermute | solution.py:116
  114.8 20.3 %collective-permute-start.29 = (bf16[256,1024]{1,0:T(8,128)(2,1)S(1)}, bf16[256,1024]{1,0:T(8,128)(2,1)S(1)}, u32[]{:S(2)}, u32[]{:S(2)}) collective-permute-start(bf16[256,1024]{1,0:T(8,128)(2,1)S(1)} %get-tuple-element.110), channel_id=1, source_target_pairs={{0,2},{1,5},{2,0},{3,7},{4,6},{5,1},{6,4},{7,3},{8,10},{9,13},{10,... | collective-permute-start | bytes 1572872 | tf_op jit(solution)/shard_map/r_corner1/ppermute | solution.py:116
  120.7 15.8 %collective-permute-start.38 = (f32[2,128]{1,0:T(2,128)S(1)}, f32[2,128]{1,0:T(2,128)S(1)}, u32[]{:S(2)}, u32[]{:S(2)}) collective-permute-start(f32[2,128]{1,0:T(2,128)S(1)} %bitcast.99), channel_id=1, source_target_pairs={{0,24},{1,25},{2,26},{3,27},{4,28},{5,29},{6,30},{7,31},{8,16},{9,... | collective-permute-start | bytes 3080 | tf_op jit(solution)/shard_map/t_z3/ppermute | solution.py:116
  124.2 12.4 %collective-permute-start.39 = (f32[2,128]{1,0:T(2,128)S(1)}, f32[2,128]{1,0:T(2,128)S(1)}, u32[]{:S(2)}, u32[]{:S(2)}) collective-permute-start(f32[2,128]{1,0:T(2,128)S(1)} %bitcast.98), channel_id=1, source_target_pairs={{0,16},{1,17},{2,18},{3,19},{4,20},{5,21},{6,22},{7,23},{8,24},{9,... | collective-permute-start | bytes 3080 | tf_op jit(solution)/shard_map/t_z2/ppermute | solution.py:116
  133.8 10.3 %collective-permute-start.30 = (bf16[256,1024]{1,0:T(8,128)(2,1)S(1)}, bf16[256,1024]{1,0:T(8,128)(2,1)S(1)}, u32[]{:S(2)}, u32[]{:S(2)}) collective-permute-start(bf16[256,1024]{1,0:T(8,128)(2,1)S(1)} %get-tuple-element.119), channel_id=1, source_target_pairs={{0,2},{1,5},{2,0},{3,7},{4,6},{5,1},{6,4},{7,3},{8,10},{9,13},{10,... | collective-permute-start | bytes 1572872 | tf_op jit(solution)/shard_map/r_right1/ppermute | solution.py:116
  135.4 9.2 %collective-permute-start.31 = (bf16[256,1024]{1,0:T(8,128)(2,1)S(1)}, bf16[256,1024]{1,0:T(8,128)(2,1)S(1)}, u32[]{:S(2)}, u32[]{:S(2)}) collective-permute-start(bf16[256,1024]{1,0:T(8,128)(2,1)S(1)} %corner.3), channel_id=1, source_target_pairs={{0,4},{1,3},{2,6},{3,1},{4,0},{5,7},{6,2},{7,5},{8,12},{9,11},{10,... | collective-permute-start | bytes 1572872 | tf_op jit(solution)/shard_map/r_left1/ppermute | solution.py:116
  136.9 13.2 %collective-permute-start.32 = (bf16[128,1024]{1,0:T(8,128)(2,1)S(1)}, bf16[128,1024]{1,0:T(8,128)(2,1)S(1)}, u32[]{:S(2)}, u32[]{:S(2)}) collective-permute-start(bf16[128,1024]{1,0:T(8,128)(2,1)S(1)} %get-tuple-element.122), channel_id=1, source_target_pairs={{0,16},{1,17},{2,18},{3,19},{4,20},{5,21},{6,22},{7,23},{8,24},{9,... | collective-permute-start | bytes 786440 | tf_op jit(solution)/shard_map/r_z2/ppermute | solution.py:116
  145.0 9.4 %collective-permute-start.33 = (bf16[128,1024]{1,0:T(8,128)(2,1)S(1)}, bf16[128,1024]{1,0:T(8,128)(2,1)S(1)}, u32[]{:S(2)}, u32[]{:S(2)}) collective-permute-start(bf16[128,1024]{1,0:T(8,128)(2,1)S(1)} %get-tuple-element.120), channel_id=1, source_target_pairs={{0,8},{1,9},{2,10},{3,11},{4,12},{5,13},{6,14},{7,15},{8,0},{9,1},... | collective-permute-start | bytes 786440 | tf_op jit(solution)/shard_map/r_z1/ppermute | solution.py:116
  147.1 9.7 %collective-permute-start.34 = (bf16[128,1024]{1,0:T(8,128)(2,1)S(1)}, bf16[128,1024]{1,0:T(8,128)(2,1)S(1)}, u32[]{:S(2)}, u32[]{:S(2)}) collective-permute-start(bf16[128,1024]{1,0:T(8,128)(2,1)S(1)} %get-tuple-element.123), channel_id=1, source_target_pairs={{0,24},{1,25},{2,26},{3,27},{4,28},{5,29},{6,30},{7,31},{8,16},{9,... | collective-permute-start | bytes 786440 | tf_op jit(solution)/shard_map/r_z3/ppermute | solution.py:116
  (35 other events, 182.3 us)

commit v3 on v2

--- a/solution.py
+++ b/solution.py
@@ -145,40 +145,99 @@
     )(*args)
 
 
-def prepare(expert, table, saved_gate, saved_up):
-    groups, _, tokens = table.shape
+META = 8
+
+
+def pack_rows(grad_out, slots, gates):
+    tokens, quarter = grad_out.shape
+    experts = slots.shape[0]
+    top_count = gates.shape[0]
+
+    def body(g_ref, s_ref, w_ref, out, choice_ref):
+        out[:tokens] = g_ref[...]
+        entries = s_ref[...]
+        owner = lax.div(entries, top_count)
+        choice = (entries - owner * top_count).astype(F32)
+        owner = owner.astype(F32)
+        gate = w_ref[...].astype(F32)
+        square = lax.broadcasted_iota(jnp.int32, (tokens, tokens), 0).astype(F32)
+        row = lax.broadcasted_iota(jnp.int32, (META, tokens), 0)
+        lane = lax.broadcasted_iota(jnp.int32, (META, tokens), 1).astype(F32)
+        number = lax.broadcasted_iota(jnp.int32, (top_count, tokens), 0).astype(F32)
+        for e in range(experts):
+            hit = jnp.where(square == owner[e : e + 1], 1.0, 0.0).astype(BF16)
+            value = jnp.where(row == 0, lane, choice[e : e + 1]).astype(BF16)
+            found = dot_nt(value, hit)
+            chosen = found[1:2]
+            weight = jnp.sum(jnp.where(number == chosen, gate, 0.0), axis=0, keepdims=True)
+            choice_ref[e : e + 1, :] = chosen
+            out[tokens:, e * tokens : (e + 1) * tokens] = jnp.where(row == 0, found, weight).astype(BF16)
+
+    full = lambda shape: pl.BlockSpec(shape, lambda i: (0, 0))
+    return pl.pallas_call(
+        body,
+        out_shape=[shape_of((tokens + META, quarter), BF16), shape_of((experts, tokens), F32)],
+        grid=(1,),
+        in_specs=[full(grad_out.shape), full(slots.shape), full(gates.shape)],
+        out_specs=[full((tokens + META, quarter)), full((experts, tokens))],
+        compiler_params=pltpu.CompilerParams(vmem_limit_bytes=60 << 20),
+        cost_estimate=HINT,
+        name="pack",
+    )(grad_out, slots, gates)
+
+
+def prepare(expert, block, near, saved_gate, saved_up, chunk):
+    tokens = near[0][0].shape[0] - META
     hid = saved_gate.shape[1]
-
-    def spot(i):
-        return (i // 2) % NY, i // 4 + 2 * (i % 2)
-
-    def group(i, s):
-        dy, d = spot(i)
-        return ((s[0] // NY) ^ d) * NY + ((s[0] % NY) ^ dy)
-
-    def body(s_ref, t_ref, g_ref, u_ref, *outs):
+    count = len(chunk)
+    low, step = chunk[0], chunk[1] - chunk[0]
+
+    def group(i, e, s):
+        return ((e[0] // NY) ^ (low + step * (i % count))) * NY + ((e[0] % NY) ^ (i // count))
+
+    def body(e_ref, s_ref, *refs):
+        metas = refs[: 3 * count]
+        g_ref, u_ref = refs[3 * count : 3 * count + 2]
+        outs = refs[3 * count + 2 :]
+        i, c = pl.program_id(0), s_ref[0] % NC
+        meta = None
+        for k in range(count):
+            own, first, second = (m[...].astype(F32) for m in metas[3 * k : 3 * k + 3])
+            mine = jnp.where(i // count == 0, own, jnp.where(c == 0, first, second))
+            meta = mine if meta is None else jnp.where(i % count == k, mine, meta)
         slots = lax.broadcasted_iota(jnp.int32, (tokens, tokens), 0).astype(F32)
-        pick = jnp.where(slots == t_ref[0, 0:1, :], 1.0, 0.0).astype(BF16)
+        pick = jnp.where(slots == meta[0:1], 1.0, 0.0).astype(BF16)
         flip = (((0,), (0,)), ((), ()))
         gate_pre = lax.dot_general(pick, g_ref[...], flip, preferred_element_type=F32)
         up_pre = lax.dot_general(pick, u_ref[...], flip, preferred_element_type=F32)
-        scale = jnp.transpose(jnp.broadcast_to(t_ref[0, 1:2, :], (tokens, tokens)))[:, 0:1]
+        scale = jnp.transpose(jnp.broadcast_to(meta[1:2], (tokens, tokens)))[:, 0:1]
         activated, derivative = silu_pair(gate_pre)
         outs[0][...] = activated * up_pre
         outs[1][...] = scale * up_pre * derivative
         outs[2][...] = scale * activated
 
-    out = shape_of((groups * tokens, hid), F32)
-    saved = pl.BlockSpec((tokens, hid), lambda i, s: (group(i, s), 0))
-    row = pl.BlockSpec((1, 2, tokens), lambda i, s: (spot(i)[0] * NZ + spot(i)[1], 0, 0))
-    spec = pl.BlockSpec((tokens, hid), lambda i, s: (i, 0))
-    return kernel(
-        "prepare", body, [out] * 3, (groups,), [row, saved, saved], [spec] * 3, expert, table, saved_gate, saved_up
-    )
+    out = shape_of((NY * count * tokens, hid), F32)
+    meta = pl.BlockSpec((META, tokens), lambda i, e, s: (tokens // META, e[0]))
+    saved = pl.BlockSpec((tokens, hid), lambda i, e, s: (group(i, e, s), 0))
+    spec = pl.BlockSpec((tokens, hid), lambda i, e, s: (i, 0))
+    flat = [p for three in near for p in three]
+    return pl.pallas_call(
+        body,
+        out_shape=[out] * 3,
+        grid_spec=pltpu.PrefetchScalarGridSpec(
+            num_scalar_prefetch=2,
+            grid=(NY * count,),
+            in_specs=[meta] * len(flat) + [saved, saved],
+            out_specs=[spec] * 3,
+        ),
+        compiler_params=LARGE,
+        cost_estimate=HINT,
+        name="prepare",
+    )(expert, block, *flat, saved_gate, saved_up)
 
 
 def hidden_parts(block, pieces, down, got):
-    tokens, quarter = pieces[0][0].shape
+    tokens, quarter = pieces[0][0].shape[0] - META, pieces[0][0].shape[1]
     hid = down.shape[0]
     count = len(pieces)
     half = count * tokens
@@ -198,9 +257,10 @@
 
         def piece(i, j, dx, dy):
             target = rows_v.at[dx, pl.ds(dy * half + i * tokens, tokens), :]
-            return pltpu.make_async_copy(near[4 * i + j], target, row_sem.at[i, dx, dy])
-
-        for dx in range(NX):
+            source = near[4 * i + j].at[pl.ds(0, tokens), :]
+            return pltpu.make_async_copy(source, target, row_sem.at[i, dx, dy])
+
+        def begin(dx):
             for k in (1, 0):
                 weight(dx, k).start()
             for i in range(count):
@@ -215,12 +275,16 @@
                     piece(i, 2, dx, 1 - dx).start()
 
         total = [None, None]
+        begin(0)
         for dx in range(NX):
             for i in range(count):
                 for dy in range(NY):
                     piece(i, 0, dx, dy).wait()
             for k in (1, 0):
                 weight(dx, k).wait()
+            if dx + 1 < NX:
+                begin(dx + 1)
+            for k in (1, 0):
                 part = dot_nt(rows_v[dx], w_v[dx, k])
                 total[k] = part if dx == 0 else total[k] + part
         theirs[...] = total[1].astype(BF16)
@@ -248,11 +312,11 @@
     )
 
 
-def pre_grads(block, mine, back, factors, number):
+def pre_grads(block, mine, back, factors):
     rows, hid = mine.shape
     half = rows // NY
-    tokens = factors[0].shape[0] // (NY * NZ)
-    count = half // tokens
+    count = len(CHUNKS[0])
+    tokens = half // count
 
     def body(s_ref, m_ref, b_ref, f0, f1, f2, h_ref, t_ref):
         bh = m_ref[...] + b_ref[...].astype(F32)
@@ -264,13 +328,13 @@
             t_ref[0, i : i + 1, :] = flat[0:1, i * tokens : (i + 1) * tokens]
 
     outs = [shape_of((rows, 2 * hid), BF16), shape_of((NY, count, tokens), F32)]
-    spec = lambda cols, first=0: pl.BlockSpec((half, cols), lambda i, s: (first + i, 0))
+    spec = lambda cols: pl.BlockSpec((half, cols), lambda i, s: (i, 0))
     return kernel(
         "pre_grads",
         body,
         outs,
         (NY,),
-        [spec(hid)] * 2 + [spec(hid, NY * number)] * 3,
+        [spec(hid)] * 5,
         [spec(2 * hid), pl.BlockSpec((1, count, tokens), lambda i, s: (i, 0, 0))],
         block,
         mine,
@@ -279,47 +343,86 @@
     )
 
 
-def input_parts(block, mine, theirs, weights, got, spots, types):
+def input_parts(block, mine, theirs, weights, got):
     rows = mine.shape[0] // NY
     hid = mine.shape[1] // 2
     quarter = weights[0].shape[0] // (NX * NC)
     steps = 2
     wide = quarter // steps
-
-    def place(i, s):
-        c = s[0] % NC
-        pairs = [spot(c) for spot in spots]
-        dy = jnp.where(i == 0, pairs[0][0], pairs[1][0])
-        dx = jnp.where(i == 0, pairs[0][1], pairs[1][1])
-        return dy, 2 * ((s[0] // NC) ^ dx) + c
-
-    def body(s_ref, m_ref, t_ref, wg, wu, og, ou, *outs):
-        total = dot_nt(m_ref[:, :hid], wg[...]) + dot_nt(m_ref[:, hid:], wu[...])
-        total = total + dot_nt(t_ref[:, :hid], og[...]) + dot_nt(t_ref[:, hid:], ou[...])
-        for k, out in enumerate(outs):
-
-            @pl.when(pl.program_id(0) == k)
-            def _(out=out):
-                out[...] = total.astype(out.dtype)
-
-    half = pl.BlockSpec((rows, 2 * hid), lambda i, j, s: (place(i, s)[0], 0))
-    weight = pl.BlockSpec((wide, hid), lambda i, j, s: (place(i, s)[1] * steps + j, 0))
-    outs = [
-        pl.BlockSpec((rows, wide), lambda i, j, s: (0, jnp.where(i == 0, j, steps - 1))),
-        pl.BlockSpec((rows, wide), lambda i, j, s: (0, jnp.where(i == 0, 0, j))),
-    ]
+    order = [(dx, h) for dx in (1, 0) for h in range(steps)]
+
+    def body(s_ref, m_ref, t_ref, *refs):
+        sources = refs[:4]
+        outs = refs[4:8]
+        side_v, w_v, o_v, side_sem, sem, out_sem = refs[8:]
+        x, c = s_ref[0] // NC, s_ref[0] % NC
+
+        def weight(n, j):
+            dx, h = order[n]
+            first = pl.multiple_of((2 * (x ^ dx) + c) * quarter + h * wide, wide)
+            return pltpu.make_async_copy(sources[j].at[pl.ds(first, wide), :], w_v.at[n, j], sem.at[n, j])
+
+        def side(k):
+            return pltpu.make_async_copy((m_ref, t_ref)[k], side_v.at[k], side_sem.at[k])
+
+        def give(which, n, dy):
+            cols = pl.ds(order[n][1] * wide, wide)
+            return pltpu.make_async_copy(o_v.at[n, dy], outs[which].at[:, cols], out_sem.at[n, dy])
+
+        side(0).start()
+        for j in range(4):
+            weight(0, j).start()
+        side(1).start()
+        for j in range(4):
+            weight(1, j).start()
+        side(0).wait()
+        for n, (dx, h) in enumerate(order):
+            total = None
+            for j in range(4):
+                weight(n, j).wait()
+                if n == 0 and j == 2:
+                    side(1).wait()
+                part = dot_nt(side_v[j // 2, :, (j % 2) * hid : (j % 2 + 1) * hid], w_v[n, j])
+                total = part if j == 0 else total + part
+                if n + 2 < len(order):
+                    weight(n + 2, j).start()
+            o_v[n, 0] = total[:rows].astype(BF16)
+            o_v[n, 1] = total[rows:].astype(BF16)
+            give(0 if dx == 1 else 3, n, dx).start()
+
+            @pl.when(c == 1 - dx)
+            def _(n=n, dx=dx):
+                give(1, n, 1 - dx).start()
+
+            @pl.when(c != 1 - dx)
+            def _(n=n, dx=dx):
+                give(2, n, 1 - dx).start()
+
+        for n in range(len(order)):
+            for dy in range(NY):
+                give(0, n, dy).wait()
+
+    far = pl.BlockSpec(memory_space=pl.ANY)
     return kernel(
         "input",
         body,
-        [shape_of((rows, quarter), t) for t in types],
-        (2, steps),
-        [half, half] + [weight] * 4,
-        outs,
+        [shape_of((rows, quarter), BF16)] * 4,
+        (1,),
+        [far] * 6,
+        [far] * 4,
         block,
         mine,
         theirs,
         *weights,
         *got,
+        scratch=[
+            pltpu.VMEM((2,) + mine.shape, BF16),
+            pltpu.VMEM((len(order), 4, wide, hid), BF16),
+            pltpu.VMEM((len(order), NY, rows, wide), BF16),
+            pltpu.SemaphoreType.DMA((2,)),
+            pltpu.SemaphoreType.DMA((len(order), 4)),
+            pltpu.SemaphoreType.DMA((len(order), NY)),
+        ],
     )
 
 
@@ -331,7 +434,7 @@
     def body(s_ref, b_ref, f_ref, g_ref, *outs):
         for i, out in enumerate(outs):
             s = slice(i * part, (i + 1) * part)
-            out[...] = (b_ref[s] + f_ref[s].astype(F32) + g_ref[s].astype(F32)).astype(out.dtype)
+            out[...] = (b_ref[s].astype(F32) + f_ref[s].astype(F32) + g_ref[s].astype(F32)).astype(out.dtype)
 
     spec = lambda n: pl.BlockSpec((n, wide), lambda i, s: (0, i))
     outs = [shape_of((part, cols), t) for t in types]
@@ -348,16 +451,16 @@
     return kernel("corner", body, shape_of(base.shape, BF16), (2,), [spec] * 2, spec, block, base, corner)
 
 
-def last_sum(block, keep, parts):
+def last_sum(block, keep, parts, out_type):
     def body(s_ref, k_ref, *refs):
         total = k_ref[...]
         for ref in refs[:-1]:
             total = total + ref[...].astype(F32)
-        refs[-1][...] = total.astype(BF16)
+        refs[-1][...] = total.astype(out_type)
 
     spec = pl.BlockSpec(keep.shape, lambda i, s: (0, 0))
     return kernel(
-        "last", body, shape_of(keep.shape, BF16), (1,), [spec] * (1 + len(parts)), spec, block, keep, *parts
+        "last", body, shape_of(keep.shape, out_type), (1,), [spec] * (1 + len(parts)), spec, block, keep, *parts
     )
 
 
@@ -371,112 +474,89 @@
     at_expert, at_block = expert.reshape(1), block.reshape(1)
 
     down, gate_w, up_w = w_down[0], w_gate[0], w_up[0]
-
-    entries = slot_lists[0]
-    owner, choice = entries // top_count, entries % top_count
-    token_ids = jnp.arange(tokens, dtype=jnp.int32)
-    hit = owner[:, :, None] == token_ids[None, None, :]
-    choice_of = jnp.sum(jnp.where(hit, choice[:, :, None], 0), axis=1)
-    slot_of = jnp.sum(jnp.where(hit, token_ids[None, :, None], 0), axis=1)
-    choice_ids = jnp.arange(top_count, dtype=jnp.int32)
-    chosen = choice_of[:, :, None] == choice_ids[None, None, :]
-    gate_of = jnp.sum(jnp.where(chosen, gate_weights[None].astype(F32), 0.0), axis=2)
-    table = jnp.stack([slot_of.astype(F32), gate_of], axis=1).reshape(NZ, NY, 2, tokens)
-
-    own = grad_out
+    near, far = CHUNKS
+    own, choice_of = pack_rows(grad_out, slot_lists[0], gate_weights.T)
+
     z2, z1 = send(own, TO_Z[2], "z2"), send(own, TO_Z[1], "z1")
     first0, second0 = send(own, RIGHT, "first0"), send(own, LEFT, "second0")
     got_down = send(down, TO_CORE, "weights")
 
-    own_, z2, z1, first0, second0, got_down, table = lax.optimization_barrier(
-        (own, z2, z1, first0, second0, got_down, table)
-    )
-    z3 = send(own_, TO_Z[3], "z3")
+    z2, z1, first0, second0, got_down, gate_w_, up_w_ = lax.optimization_barrier(
+        (z2, z1, first0, second0, got_down, gate_w, up_w)
+    )
     first2, second2 = send(z2, RIGHT, "first2"), send(z2, LEFT, "second2")
     third0 = send(first0, LEFT, "third0")
-    line = []
-    for d in range(NZ):
-        part = lax.dynamic_index_in_dim(table, z ^ d, axis=0, keepdims=False)
-        line.append(part if d == 0 else send(part, TO_Z[d], "meta"))
-    line = jnp.stack(line)
-    gate_w_, up_w_ = after(gate_w, table), after(up_w, table)
+    z3 = send(z2, TO_Z[1], "z3")
     got_gate, got_up = send(gate_w_, TO_CORE, "weights"), send(up_w_, TO_CORE, "weights")
 
-    z1, z3, first2, second2, third0, line, got_gate, got_up = lax.optimization_barrier(
-        (z1, z3, first2, second2, third0, line, got_gate, got_up)
-    )
+    z1, z3, first2, second2, third0, got_gate, got_up = lax.optimization_barrier(
+        (z1, z3, first2, second2, third0, got_gate, got_up)
+    )
+    third2 = send(first2, LEFT, "third2")
     first1, second1 = send(z1, RIGHT, "first1"), send(z1, LEFT, "second1")
-    third2 = send(first2, LEFT, "third2")
-    near = lax.dynamic_index_in_dim(line, y, axis=1, keepdims=False)
-    far = send(lax.dynamic_index_in_dim(line, 1 - y, axis=1, keepdims=False), TO_Y, "meta_y")
-    table = jnp.concatenate([near, far], axis=0)
-
-    z3, first1, second1, third2, table = lax.optimization_barrier((z3, first1, second1, third2, table))
-    first3, second3 = send(z3, RIGHT, "first3"), send(z3, LEFT, "second3")
-    third1 = send(first1, LEFT, "third1")
-    factors = prepare(at_expert, table, saved_gate[0], saved_up[0])
-
-    pieces = {0: (own, first0, second0, third0), 2: (z2, first2, second2, third2)}
+    saved = saved_gate[0], saved_up[0]
+    factors_a = prepare(
+        at_expert, at_block, [(own, first0, second0), (z2, first2, second2)], *saved, near
+    )
+    place = after(at_block, factors_a[0])
 
     weights, got = (gate_w, up_w), (got_gate, got_up)
-    near, far = CHUNKS
-
-    def stage_hidden(place, chunk):
-        mine, theirs = hidden_parts(place, [pieces[d] for d in chunk], down, got_down)
-        return mine, send(theirs, TO_CORE, f"swap_bh{chunk[0]}"), after(at_block, mine)
-
-    def stage_pre(place, chunk, mine, back):
-        mine, term = pre_grads(place, mine, back, factors, CHUNKS.index(chunk))
-        return mine, send(mine, TO_CORE, f"swap_h{chunk[0]}"), term, after(at_block, mine)
-
-    def stage_out(place, chunk, mine, theirs):
-        a, b = input_parts(
-            place, mine, theirs, weights, got, (lambda c: (1, 1), lambda c: (c, 1 - c)), (BF16, BF16)
-        )
-        corner = send(a, LEFT, f"r_corner{chunk[0]}")
-        right = send(b, LEFT, f"r_right{chunk[0]}")
-        return corner, right, after(at_block, a)
-
-    def stage_keep(place, mine, theirs):
-        base, left = input_parts(
-            place, mine, theirs, weights, got, (lambda c: (0, 0), lambda c: (1 - c, c)), (F32, BF16)
-        )
-        return base, left, after(at_block, base)
 
     def stage_corner(place, chunk, left, corner):
         value = add_corner(place, left, corner)
-        return send(value, RIGHT, f"r_left{chunk[0]}"), after(at_block, value)
+        return send(value, RIGHT, f"r_left{chunk[0]}"), value
 
     def stage_add(place, chunk, base, right, left):
         types = [F32 if d == 0 else BF16 for d in chunk]
         totals = add_pieces(place, base, right, left, types)
-        sums = {d: t if d == 0 else send(t, TO_Z[d], f"r_z{d}") for d, t in zip(chunk, totals)}
-        return sums, after(at_block, totals[0])
-
-    place = after(at_block, factors[0])
-    mine_a, back, place = stage_hidden(place, near)
-    mine_a, theirs_a, term_a, place = stage_pre(place, near, mine_a, back)
-    theirs_a, first3, second3, third1 = lax.optimization_barrier((theirs_a, first3, second3, third1))
+        return {d: t if d == 0 else send(t, TO_Z[d], f"r_z{d}") for d, t in zip(chunk, totals)}, totals[0]
+
+    mine, theirs = hidden_parts(
+        place, [(own, first0, second0, third0), (z2, first2, second2, third2)], down, got_down
+    )
+    theirs, first1, second1 = lax.optimization_barrier((theirs, first1, second1))
+    back = send(theirs, TO_CORE, "swap_bh0")
+    first3, second3 = send(z3, RIGHT, "first3"), send(z3, LEFT, "second3")
+    third1 = send(first1, LEFT, "third1")
+    mine, term_a = pre_grads(after(at_block, mine), mine, back, factors_a)
+    theirs = send(mine, TO_CORE, "swap_h0")
+    place = at_block
+    corner_a, right_a, left_a, base_a = input_parts(place, mine, theirs, weights, got)
+    place = after(at_block, base_a)
+    corner_a, right_a = send(corner_a, LEFT, "r_corner0"), send(right_a, LEFT, "r_right0")
+
+    first3, _ = lax.optimization_barrier((first3, base_a))
     third3 = send(first3, LEFT, "third3")
-    pieces |= {1: (z1, first1, second1, third1), 3: (z3, first3, second3, third3)}
-    corner_a, right_a, place = stage_out(place, near, mine_a, theirs_a)
-    base_a, left_a, place = stage_keep(place, mine_a, theirs_a)
-    mine_b, back, place = stage_hidden(place, far)
-    left_a, place = stage_corner(place, near, left_a, corner_a)
-    mine_b, theirs_b, term_b, place = stage_pre(place, far, mine_b, back)
-    corner_b, right_b, place = stage_out(place, far, mine_b, theirs_b)
-    base_b, left_b, place = stage_keep(place, mine_b, theirs_b)
-    sums, place = stage_add(place, near, base_a, right_a, left_a)
-    left_b, place = stage_corner(place, far, left_b, corner_b)
-    more, place = stage_add(place, far, base_b, right_b, left_b)
+    factors_b = prepare(
+        at_expert, place, [(z1, first1, second1), (z3, first3, second3)], *saved, far
+    )
+    place = after(at_block, factors_b[0])
+    mine, theirs = hidden_parts(
+        place, [(z1, first1, second1, third1), (z3, first3, second3, third3)], down, got_down
+    )
+    back = send(theirs, TO_CORE, "swap_bh1")
+    place = after(at_block, mine)
+    left_a, value = stage_corner(place, near, left_a, corner_a)
+    place = after(at_block, value)
+    mine, term_b = pre_grads(place, mine, back, factors_b)
+    theirs = send(mine, TO_CORE, "swap_h1")
+    place = at_block
+    corner_b, right_b, left_b, base_b = input_parts(place, mine, theirs, weights, got)
+    place = after(at_block, base_b)
+    corner_b, right_b = send(corner_b, LEFT, "r_corner1"), send(right_b, LEFT, "r_right1")
+    sums, value = stage_add(place, near, base_a, right_a, left_a)
+    left_b, value = stage_corner(after(at_block, value), far, left_b, corner_b)
+    more, _ = stage_add(after(at_block, value, sums[2]), far, base_b, right_b, left_b)
     sums.update(more)
-    grad_in = last_sum(place, sums[0], [sums[d] for d in (2, 1, 3)])
+    grad_in = last_sum(at_block, sums[0], [sums[d] for d in (2, 1, 3)], BF16)
 
     terms = {d: t[:, i] for c, t in ((near, term_a), (far, term_b)) for i, d in enumerate(c)}
     term = jnp.stack([terms[d] for d in range(NZ)], axis=1)
     term = term + send(term, TO_CORE, "t_core")
-    term = term + send(term, TO_X, "t_x")
+    term = term + send(after(term, base_b), TO_X, "t_x")
+    term = after(term, value)
     term = jnp.stack([term[0], send(term[1], TO_Y, "t_y")], axis=1)
+    term = after(term, right_b)
     slots = [term[0]] + [send(term[d], TO_Z[d], f"t_z{d}") for d in range(1, NZ)]
     slot_grad = jnp.zeros((experts, tokens), F32)
     ids = jnp.arange(experts, dtype=jnp.int32)
@@ -484,6 +564,8 @@
         for dy in range(NY):
             source = (z ^ d) * NY + (y ^ dy)
             slot_grad = jnp.where((ids == source)[:, None], slots[d][dy][None], slot_grad)
+    choice_ids = jnp.arange(top_count, dtype=F32)
+    chosen = choice_of[:, :, None] == choice_ids[None, None, :]
     grad_gate = jnp.sum(jnp.where(chosen, slot_grad[:, :, None], 0.0), axis=0)
     return (grad_in, grad_gate)
 

time: 158 us -> 137 us (0.87)
  waiting for transfers between devices: 53.5 us -> 45.8 us
  starting transfers between devices: 49.7 us -> 43.5 us
  Pallas kernels: 40.9 us -> 34.7 us
  other arithmetic: 2.51 us -> 0.75 us
    pallas_call x14 -> x11, Pallas kernels: 40.9 us -> 30.2 us  [kernel(): pl.pallas_call(body, out_shape=outs, grid_spec=pltpu.PrefetchScalarGridSp...]
    ppermute x41 -> x37, waiting for transfers between devices: 53.5 us -> 45.8 us  [send(): return lax.ppermute(value, BOTH, pairs)]
    ppermute x41 -> x37, starting transfers between devices: 49.7 us -> 43.5 us  [send(): return lax.ppermute(value, BOTH, pairs)]
    pallas_call x0 -> x3, Pallas kernels: none -> 4.49 us  [the longest x2 2.53 us: prepare(): pl.pallas_call(body, out_shape=[out] * 3, grid_spec=pltpu.PrefetchScalarG...]
    unnamed x36 -> x42, local copies, waits for them, and re-layouts: 9.88 us -> 10.9 us
  transfers between devices with their start and end apart: 41 -> 37, of which waited for: 21 -> 15; matrix products, arithmetic and copies ran while one was open for 2% -> 1% of each run, Pallas kernels for 18% -> 24%
where the time goes in v3:
time: 137 us
  waiting for transfers between devices  45.8 us (33%)
  starting transfers between devices  43.5 us (32%)
  Pallas kernels  34.7 us (25%)
  local copies, waits for them, and re-layouts  10.9 us (8%)
    ppermute x37, waiting for transfers between devices, send(): return lax.ppermute(value, BOTH, pairs)  45.8 us
    ppermute x37, starting transfers between devices, send(): return lax.ppermute(value, BOTH, pairs)  43.5 us
    pallas_call x11, Pallas kernels, kernel(): pl.pallas_call(body, out_shape=outs, grid_spec=pltpu.PrefetchScalarGridSp...  30.2 us
    unnamed x42, local copies, waits for them, and re-layouts  10.9 us
  transfers between devices with their start and end apart: 37, of which 15 were waited for; matrix products, arithmetic and copies ran while one was open for 1% of the time, Pallas kernels for 24%

profile of v3, /device:TPU:0, one launch (start us, length us, event | category | flops | bytes accessed | tf_op | source)
XLA Modules:
  0.0 136.7 jit_solution(4721257325321238353)
XLA Ops:
  1.1 2.0 %pack.1 = (bf16[136,1024]{1,0:T(8,128)(2,1)}, f32[8,128]{1,0:T(8,128)}) custom-call(bf16[128,1024]{1,0:T(8,128)(2,1)} %g_ref.1, s32[8,128]{1,0:T(8,128)} %bitcast.46, bf16[8,128]{1,0:T(8,128)(2,1)} %bitcast.47), custom_call_target="tpu_custom_call" | custom-call | tf_op jit(solution)/shard_map/pack/pallas_call | solution.py:177
  3.1 3.6 %collective-permute-start = (bf16[136,1024]{1,0:T(8,128)(2,1)}, bf16[136,1024]{1,0:T(8,128)(2,1)S(1)}, u32[]{:S(2)}, u32[]{:S(2)}) collective-permute-start(bf16[136,1024]{1,0:T(8,128)(2,1)} %get-tuple-element.60.refs_0_), channel_id=1, source_target_pairs={{0,16},{1,17},{2,18},{3,19},{4,20},{5,21},{6,22},{7,23},{8,24},{9,... | collective-permute-start | bytes 835592 | tf_op jit(solution)/shard_map/z2/ppermute | solution.py:116
  6.7 1.6 %collective-permute-start.1 = (bf16[136,1024]{1,0:T(8,128)(2,1)}, bf16[136,1024]{1,0:T(8,128)(2,1)S(1)}, u32[]{:S(2)}, u32[]{:S(2)}) collective-permute-start(bf16[136,1024]{1,0:T(8,128)(2,1)} %get-tuple-element.60.refs_0_), channel_id=1, source_target_pairs={{0,8},{1,9},{2,10},{3,11},{4,12},{5,13},{6,14},{7,15},{8,0},{9,1},... | collective-permute-start | bytes 835592 | tf_op jit(solution)/shard_map/z1/ppermute | solution.py:116
  8.3 1.5 %collective-permute-start.2 = (bf16[136,1024]{1,0:T(8,128)(2,1)}, bf16[136,1024]{1,0:T(8,128)(2,1)S(1)}, u32[]{:S(2)}, u32[]{:S(2)}) collective-permute-start(bf16[136,1024]{1,0:T(8,128)(2,1)} %get-tuple-element.60.refs_0_), channel_id=1, source_target_pairs={{0,4},{1,3},{2,6},{3,1},{4,0},{5,7},{6,2},{7,5},{8,12},{9,11},{10,... | collective-permute-start | bytes 835592 | tf_op jit(solution)/shard_map/first0/ppermute | solution.py:116
  11.3 9.0 %collective-permute-done.refs_3_.refs_4_ = bf16[136,1024]{1,0:T(8,128)(2,1)S(1)} collective-permute-done((bf16[136,1024]{1,0:T(8,128)(2,1)}, bf16[136,1024]{1,0:T(8,128)(2,1)S(1)}, u32[]{:S(2)}, u32[]{:S(2)}) %collective-permute-start) | collective-permute-done | bytes 278560 | tf_op jit(solution)/shard_map/z2/ppermute | solution.py:116
  22.6 1.5 %collective-permute-start.6 = (bf16[136,1024]{1,0:T(8,128)(2,1)S(1)}, bf16[136,1024]{1,0:T(8,128)(2,1)S(1)}, u32[]{:S(2)}, u32[]{:S(2)}) collective-permute-start(bf16[136,1024]{1,0:T(8,128)(2,1)S(1)} %collective-permute-done.refs_3_.refs_4_), channel_id=1, source_target_pairs={{0,4},{1,3},{2,6},{3,1},{4,0},{5,7},{6,2},{7,5},{8,12},{9,11},{10,... | collective-permute-start | bytes 835592 | tf_op jit(solution)/shard_map/first2/ppermute | solution.py:116
  25.6 4.1 %collective-permute-done.5.refs_3_.refs_4_ = bf16[136,1024]{1,0:T(8,128)(2,1)S(1)} collective-permute-done((bf16[136,1024]{1,0:T(8,128)(2,1)S(1)}, bf16[136,1024]{1,0:T(8,128)(2,1)S(1)}, u32[]{:S(2)}, u32[]{:S(2)}) %collective-permute-start.5) | collective-permute-done | bytes 278560 | tf_op jit(solution)/shard_map/z3/ppermute | solution.py:116
  29.7 1.5 %collective-permute-start.8 = (bf16[136,1024]{1,0:T(8,128)(2,1)S(1)}, bf16[136,1024]{1,0:T(8,128)(2,1)S(1)}, u32[]{:S(2)}, u32[]{:S(2)}) collective-permute-start(bf16[136,1024]{1,0:T(8,128)(2,1)S(1)} %collective-permute-done.2.refs_1_), channel_id=1, source_target_pairs={{0,2},{1,5},{2,0},{3,7},{4,6},{5,1},{6,4},{7,3},{8,10},{9,13},{10,... | collective-permute-start | bytes 835592 | tf_op jit(solution)/shard_map/third0/ppermute | solution.py:116
  32.1 4.2 %collective-permute-done.8.refs_3_ = bf16[136,1024]{1,0:T(8,128)(2,1)S(1)} collective-permute-done((bf16[136,1024]{1,0:T(8,128)(2,1)S(1)}, bf16[136,1024]{1,0:T(8,128)(2,1)S(1)}, u32[]{:S(2)}, u32[]{:S(2)}) %collective-permute-start.8) | collective-permute-done | bytes 278560 | tf_op jit(solution)/shard_map/third0/ppermute | solution.py:116
  36.3 1.6 %collective-permute-start.11 = (bf16[136,1024]{1,0:T(8,128)(2,1)S(1)}, bf16[136,1024]{1,0:T(8,128)(2,1)S(1)}, u32[]{:S(2)}, u32[]{:S(2)}) collective-permute-start(bf16[136,1024]{1,0:T(8,128)(2,1)S(1)} %collective-permute-done.6.refs_4_.refs_5_), channel_id=1, source_target_pairs={{0,2},{1,5},{2,0},{3,7},{4,6},{5,1},{6,4},{7,3},{8,10},{9,13},{10,... | collective-permute-start | bytes 835592 | tf_op jit(solution)/shard_map/third2/ppermute | solution.py:116
  38.0 1.6 %collective-permute-start.12 = (bf16[136,1024]{1,0:T(8,128)(2,1)S(1)}, bf16[136,1024]{1,0:T(8,128)(2,1)S(1)}, u32[]{:S(2)}, u32[]{:S(2)}) collective-permute-start(bf16[136,1024]{1,0:T(8,128)(2,1)S(1)} %collective-permute-done.1.refs_0_), channel_id=1, source_target_pairs={{0,4},{1,3},{2,6},{3,1},{4,0},{5,7},{6,2},{7,5},{8,12},{9,11},{10,... | collective-permute-start | bytes 835592 | tf_op jit(solution)/shard_map/first1/ppermute | solution.py:116
  45.5 5.2 %hidden.2 = (f32[512,384]{1,0:T(8,128)S(1)}, bf16[512,384]{1,0:T(8,128)(2,1)S(1)}) custom-call(s32[1]{0:T(128)} %bitcast.s_ref, bf16[136,1024]{1,0:T(8,128)(2,1)S(1)} %copy-done.4, bf16[136,1024]{1,0:T(8,128)(2,1)S(1)} %collective-permute-done.2.refs_1_, bf16[136,1024]{1,0:T(8,128)(2,1)S(1)} %collective-permute-done.3.refs_2_, ...), custom_call_target="tpu_custom_call" | custom-call | tf_op jit(solution)/shard_map/hidden/pallas_call | solution.py:136
  50.8 1.7 %collective-permute-done.14.b_ref = bf16[512,384]{1,0:T(8,128)(2,1)S(1)} collective-permute-done((bf16[512,384]{1,0:T(8,128)(2,1)S(1)}, bf16[512,384]{1,0:T(8,128)(2,1)S(1)}, u32[]{:S(2)}, u32[]{:S(2)}) %collective-permute-start.14) | collective-permute-done | bytes 393248 | tf_op jit(solution)/shard_map/swap_bh0/ppermute | solution.py:116
  56.7 7.5 %input.2 = (bf16[256,1024]{1,0:T(8,128)(2,1)}, bf16[256,1024]{1,0:T(8,128)(2,1)S(1)}, bf16[256,1024]{1,0:T(8,128)(2,1)S(1)}, bf16[256,1024]{1,0:T(8,128)(2,1)S(1)}) custom-call(s32[1]{0:T(128)} %bitcast.s_ref, bf16[512,768]{1,0:T(8,128)(2,1)S(1)} %get-tuple-element.80.m_ref, bf16[512,768]{1,0:T(8,128)(2,1)S(1)} %collective-permute-done.15.t_ref, ...), custom_call_target="tpu_custom_call" | custom-call | tf_op jit(solution)/shard_map/input/pallas_call | solution.py:136
  67.7 3.2 %collective-permute-done.19.refs_7_ = bf16[136,1024]{1,0:T(8,128)(2,1)S(1)} collective-permute-done((bf16[136,1024]{1,0:T(8,128)(2,1)S(1)}, bf16[136,1024]{1,0:T(8,128)(2,1)S(1)}, u32[]{:S(2)}, u32[]{:S(2)}) %collective-permute-start.19) | collective-permute-done | bytes 278560 | tf_op jit(solution)/shard_map/third3/ppermute | solution.py:116
  70.9 5.2 %hidden.3 = (f32[512,384]{1,0:T(8,128)S(1)}, bf16[512,384]{1,0:T(8,128)(2,1)}) custom-call(s32[1]{0:T(128)} %bitcast.s_ref, bf16[136,1024]{1,0:T(8,128)(2,1)S(1)} %collective-permute-done.1.refs_0_, bf16[136,1024]{1,0:T(8,128)(2,1)S(1)} %collective-permute-done.12.refs_1_, bf16[136,1024]{1,0:T(8,128)(2,1)S(1)} %collective-permute-done.13.refs_2_, ...), custom_call_target="tpu_custom_call" | custom-call | tf_op jit(solution)/shard_map/hidden/pallas_call | solution.py:136
  85.1 7.5 %input.3 = (bf16[256,1024]{1,0:T(8,128)(2,1)}, bf16[256,1024]{1,0:T(8,128)(2,1)S(1)}, bf16[256,1024]{1,0:T(8,128)(2,1)S(1)}, bf16[256,1024]{1,0:T(8,128)(2,1)S(1)}) custom-call(s32[1]{0:T(128)} %bitcast.s_ref, bf16[512,768]{1,0:T(8,128)(2,1)S(1)} %get-tuple-element.99.m_ref, bf16[512,768]{1,0:T(8,128)(2,1)S(1)} %collective-permute-done.22.t_ref, ...), custom_call_target="tpu_custom_call" | custom-call | tf_op jit(solution)/shard_map/input/pallas_call | solution.py:136
  99.9 2.3 %collective-permute-start.25 = (bf16[128,1024]{1,0:T(8,128)(2,1)S(1)}, bf16[128,1024]{1,0:T(8,128)(2,1)S(1)}, u32[]{:S(2)}, u32[]{:S(2)}) collective-permute-start(bf16[128,1024]{1,0:T(8,128)(2,1)S(1)} %get-tuple-element.104), channel_id=1, source_target_pairs={{0,16},{1,17},{2,18},{3,19},{4,20},{5,21},{6,22},{7,23},{8,24},{9,... | collective-permute-start | bytes 786440 | tf_op jit(solution)/shard_map/r_z2/ppermute | solution.py:116
  107.2 7.4 %collective-permute-done.25.refs_0_ = bf16[128,1024]{1,0:T(8,128)(2,1)S(1)} collective-permute-done((bf16[128,1024]{1,0:T(8,128)(2,1)S(1)}, bf16[128,1024]{1,0:T(8,128)(2,1)S(1)}, u32[]{:S(2)}, u32[]{:S(2)}) %collective-permute-start.25) | collective-permute-done | bytes 262176 | tf_op jit(solution)/shard_map/r_z2/ppermute | solution.py:116
  114.6 3.0 %collective-permute-start.34 = (f32[2,128]{1,0:T(2,128)S(1)}, f32[2,128]{1,0:T(2,128)S(1)}, u32[]{:S(2)}, u32[]{:S(2)}) collective-permute-start(f32[2,128]{1,0:T(2,128)S(1)} %bitcast.51), channel_id=1, source_target_pairs={{0,24},{1,25},{2,26},{3,27},{4,28},{5,29},{6,30},{7,31},{8,16},{9,... | collective-permute-start | bytes 3080 | tf_op jit(solution)/shard_map/t_z3/ppermute | solution.py:116
  120.1 2.0 %collective-permute-done.35 = f32[2,128]{1,0:T(2,128)S(1)} collective-permute-done((f32[2,128]{1,0:T(2,128)S(1)}, f32[2,128]{1,0:T(2,128)S(1)}, u32[]{:S(2)}, u32[]{:S(2)}) %collective-permute-start.35) | collective-permute-done | bytes 1056 | tf_op jit(solution)/shard_map/t_z2/ppermute | solution.py:116
  123.1 2.9 %collective-permute-start.30 = (bf16[128,1024]{1,0:T(8,128)(2,1)S(1)}, bf16[128,1024]{1,0:T(8,128)(2,1)S(1)}, u32[]{:S(2)}, u32[]{:S(2)}) collective-permute-start(bf16[128,1024]{1,0:T(8,128)(2,1)S(1)} %get-tuple-element.111), channel_id=1, source_target_pairs={{0,24},{1,25},{2,26},{3,27},{4,28},{5,29},{6,30},{7,31},{8,16},{9,... | collective-permute-start | bytes 786440 | tf_op jit(solution)/shard_map/r_z3/ppermute | solution.py:116
  126.7 4.0 %collective-permute-done.29.refs_1_ = bf16[128,1024]{1,0:T(8,128)(2,1)S(1)} collective-permute-done((bf16[128,1024]{1,0:T(8,128)(2,1)S(1)}, bf16[128,1024]{1,0:T(8,128)(2,1)S(1)}, u32[]{:S(2)}, u32[]{:S(2)}) %collective-permute-start.29) | collective-permute-done | bytes 262176 | tf_op jit(solution)/shard_map/r_z1/ppermute | solution.py:116
  130.7 5.2 %collective-permute-done.30.refs_2_ = bf16[128,1024]{1,0:T(8,128)(2,1)S(1)} collective-permute-done((bf16[128,1024]{1,0:T(8,128)(2,1)S(1)}, bf16[128,1024]{1,0:T(8,128)(2,1)S(1)}, u32[]{:S(2)}, u32[]{:S(2)}) %collective-permute-start.30) | collective-permute-done | bytes 262176 | tf_op jit(solution)/shard_map/r_z3/ppermute | solution.py:116
  (124 shorter events, 46.3 us)
Async XLA Ops:
  0.6 19.9 %collective-permute-start.4 = (bf16[384,4096]{1,0:T(8,128)(2,1)}, bf16[384,4096]{1,0:T(8,128)(2,1)}, u32[]{:S(2)}, u32[]{:S(2)}) collective-permute-start(bf16[384,4096]{1,0:T(8,128)(2,1)} %bitcast.37), channel_id=1, source_target_pairs={{0,1},{1,0},{2,3},{3,2},{4,5},{5,4},{6,7},{7,6},{8,9},{9,8},{10,11... | collective-permute-start | bytes 9437192 | tf_op jit(solution)/shard_map/weights/ppermute | solution.py:116
  3.1 17.2 %collective-permute-start = (bf16[136,1024]{1,0:T(8,128)(2,1)}, bf16[136,1024]{1,0:T(8,128)(2,1)S(1)}, u32[]{:S(2)}, u32[]{:S(2)}) collective-permute-start(bf16[136,1024]{1,0:T(8,128)(2,1)} %get-tuple-element.60.refs_0_), channel_id=1, source_target_pairs={{0,16},{1,17},{2,18},{3,19},{4,20},{5,21},{6,22},{7,23},{8,24},{9,... | collective-permute-start | bytes 835592 | tf_op jit(solution)/shard_map/z2/ppermute | solution.py:116
  6.7 13.8 %collective-permute-start.1 = (bf16[136,1024]{1,0:T(8,128)(2,1)}, bf16[136,1024]{1,0:T(8,128)(2,1)S(1)}, u32[]{:S(2)}, u32[]{:S(2)}) collective-permute-start(bf16[136,1024]{1,0:T(8,128)(2,1)} %get-tuple-element.60.refs_0_), channel_id=1, source_target_pairs={{0,8},{1,9},{2,10},{3,11},{4,12},{5,13},{6,14},{7,15},{8,0},{9,1},... | collective-permute-start | bytes 835592 | tf_op jit(solution)/shard_map/z1/ppermute | solution.py:116
  8.3 12.2 %collective-permute-start.2 = (bf16[136,1024]{1,0:T(8,128)(2,1)}, bf16[136,1024]{1,0:T(8,128)(2,1)S(1)}, u32[]{:S(2)}, u32[]{:S(2)}) collective-permute-start(bf16[136,1024]{1,0:T(8,128)(2,1)} %get-tuple-element.60.refs_0_), channel_id=1, source_target_pairs={{0,4},{1,3},{2,6},{3,1},{4,0},{5,7},{6,2},{7,5},{8,12},{9,11},{10,... | collective-permute-start | bytes 835592 | tf_op jit(solution)/shard_map/first0/ppermute | solution.py:116
  9.8 10.7 %collective-permute-start.3 = (bf16[136,1024]{1,0:T(8,128)(2,1)}, bf16[136,1024]{1,0:T(8,128)(2,1)S(1)}, u32[]{:S(2)}, u32[]{:S(2)}) collective-permute-start(bf16[136,1024]{1,0:T(8,128)(2,1)} %get-tuple-element.60.refs_0_), channel_id=1, source_target_pairs={{0,2},{1,5},{2,0},{3,7},{4,6},{5,1},{6,4},{7,3},{8,10},{9,13},{10,... | collective-permute-start | bytes 835592 | tf_op jit(solution)/shard_map/second0/ppermute | solution.py:116
  20.5 15.8 %collective-permute-start.10 = (bf16[4096,384]{1,0:T(8,128)(2,1)}, bf16[4096,384]{1,0:T(8,128)(2,1)S(1)}, u32[]{:S(2)}, u32[]{:S(2)}) collective-permute-start(bf16[4096,384]{1,0:T(8,128)(2,1)} %bitcast.43), channel_id=1, source_target_pairs={{0,1},{1,0},{2,3},{3,2},{4,5},{5,4},{6,7},{7,6},{8,9},{9,8},{10,11... | collective-permute-start | bytes 9437192 | tf_op jit(solution)/shard_map/weights/ppermute | solution.py:116
  20.6 15.7 %collective-permute-start.9 = (bf16[4096,384]{1,0:T(8,128)(2,1)}, bf16[4096,384]{1,0:T(8,128)(2,1)S(1)}, u32[]{:S(2)}, u32[]{:S(2)}) collective-permute-start(bf16[4096,384]{1,0:T(8,128)(2,1)} %bitcast.40), channel_id=1, source_target_pairs={{0,1},{1,0},{2,3},{3,2},{4,5},{5,4},{6,7},{7,6},{8,9},{9,8},{10,11... | collective-permute-start | bytes 9437192 | tf_op jit(solution)/shard_map/weights/ppermute | solution.py:116
  22.6 9.5 %collective-permute-start.6 = (bf16[136,1024]{1,0:T(8,128)(2,1)S(1)}, bf16[136,1024]{1,0:T(8,128)(2,1)S(1)}, u32[]{:S(2)}, u32[]{:S(2)}) collective-permute-start(bf16[136,1024]{1,0:T(8,128)(2,1)S(1)} %collective-permute-done.refs_3_.refs_4_), channel_id=1, source_target_pairs={{0,4},{1,3},{2,6},{3,1},{4,0},{5,7},{6,2},{7,5},{8,12},{9,11},{10,... | collective-permute-start | bytes 835592 | tf_op jit(solution)/shard_map/first2/ppermute | solution.py:116
  36.3 9.2 %collective-permute-start.11 = (bf16[136,1024]{1,0:T(8,128)(2,1)S(1)}, bf16[136,1024]{1,0:T(8,128)(2,1)S(1)}, u32[]{:S(2)}, u32[]{:S(2)}) collective-permute-start(bf16[136,1024]{1,0:T(8,128)(2,1)S(1)} %collective-permute-done.6.refs_4_.refs_5_), channel_id=1, source_target_pairs={{0,2},{1,5},{2,0},{3,7},{4,6},{5,1},{6,4},{7,3},{8,10},{9,13},{10,... | collective-permute-start | bytes 835592 | tf_op jit(solution)/shard_map/third2/ppermute | solution.py:116
  38.0 12.8 %collective-permute-start.12 = (bf16[136,1024]{1,0:T(8,128)(2,1)S(1)}, bf16[136,1024]{1,0:T(8,128)(2,1)S(1)}, u32[]{:S(2)}, u32[]{:S(2)}) collective-permute-start(bf16[136,1024]{1,0:T(8,128)(2,1)S(1)} %collective-permute-done.1.refs_0_), channel_id=1, source_target_pairs={{0,4},{1,3},{2,6},{3,1},{4,0},{5,7},{6,2},{7,5},{8,12},{9,11},{10,... | collective-permute-start | bytes 835592 | tf_op jit(solution)/shard_map/first1/ppermute | solution.py:116
  39.6 11.2 %collective-permute-start.13 = (bf16[136,1024]{1,0:T(8,128)(2,1)S(1)}, bf16[136,1024]{1,0:T(8,128)(2,1)S(1)}, u32[]{:S(2)}, u32[]{:S(2)}) collective-permute-start(bf16[136,1024]{1,0:T(8,128)(2,1)S(1)} %collective-permute-done.1.refs_0_), channel_id=1, source_target_pairs={{0,2},{1,5},{2,0},{3,7},{4,6},{5,1},{6,4},{7,3},{8,10},{9,13},{10,... | collective-permute-start | bytes 835592 | tf_op jit(solution)/shard_map/second1/ppermute | solution.py:116
  53.2 11.0 %collective-permute-start.16 = (bf16[136,1024]{1,0:T(8,128)(2,1)S(1)}, bf16[136,1024]{1,0:T(8,128)(2,1)S(1)}, u32[]{:S(2)}, u32[]{:S(2)}) collective-permute-start(bf16[136,1024]{1,0:T(8,128)(2,1)S(1)} %collective-permute-done.5.refs_3_.refs_4_), channel_id=1, source_target_pairs={{0,4},{1,3},{2,6},{3,1},{4,0},{5,7},{6,2},{7,5},{8,12},{9,11},{10,... | collective-permute-start | bytes 835592 | tf_op jit(solution)/shard_map/first3/ppermute | solution.py:116
  54.7 11.7 %collective-permute-start.17 = (bf16[136,1024]{1,0:T(8,128)(2,1)S(1)}, bf16[136,1024]{1,0:T(8,128)(2,1)S(1)}, u32[]{:S(2)}, u32[]{:S(2)}) collective-permute-start(bf16[136,1024]{1,0:T(8,128)(2,1)S(1)} %collective-permute-done.5.refs_3_.refs_4_), channel_id=1, source_target_pairs={{0,2},{1,5},{2,0},{3,7},{4,6},{5,1},{6,4},{7,3},{8,10},{9,13},{10,... | collective-permute-start | bytes 835592 | tf_op jit(solution)/shard_map/second3/ppermute | solution.py:116
  55.7 12.0 %collective-permute-start.18 = (bf16[136,1024]{1,0:T(8,128)(2,1)S(1)}, bf16[136,1024]{1,0:T(8,128)(2,1)S(1)}, u32[]{:S(2)}, u32[]{:S(2)}) collective-permute-start(bf16[136,1024]{1,0:T(8,128)(2,1)S(1)} %collective-permute-done.12.refs_1_), channel_id=1, source_target_pairs={{0,2},{1,5},{2,0},{3,7},{4,6},{5,1},{6,4},{7,3},{8,10},{9,13},{10,... | collective-permute-start | bytes 835592 | tf_op jit(solution)/shard_map/third1/ppermute | solution.py:116
  65.3 11.7 %collective-permute-start.20 = (bf16[256,1024]{1,0:T(8,128)(2,1)}, bf16[256,1024]{1,0:T(8,128)(2,1)}, u32[]{:S(2)}, u32[]{:S(2)}) collective-permute-start(bf16[256,1024]{1,0:T(8,128)(2,1)} %get-tuple-element.94), channel_id=1, source_target_pairs={{0,2},{1,5},{2,0},{3,7},{4,6},{5,1},{6,4},{7,3},{8,10},{9,13},{10,... | collective-permute-start | bytes 1572872 | tf_op jit(solution)/shard_map/r_corner0/ppermute | solution.py:116
  83.2 14.5 %collective-permute-start.23 = (bf16[256,1024]{1,0:T(8,128)(2,1)}, bf16[256,1024]{1,0:T(8,128)(2,1)S(1)}, u32[]{:S(2)}, u32[]{:S(2)}) collective-permute-start(bf16[256,1024]{1,0:T(8,128)(2,1)} %copy-done.16), channel_id=1, source_target_pairs={{0,2},{1,5},{2,0},{3,7},{4,6},{5,1},{6,4},{7,3},{8,10},{9,13},{10,... | collective-permute-start | bytes 1572872 | tf_op jit(solution)/shard_map/r_right0/ppermute | solution.py:116
  84.3 13.4 %collective-permute-start.24 = (bf16[256,1024]{1,0:T(8,128)(2,1)}, bf16[256,1024]{1,0:T(8,128)(2,1)}, u32[]{:S(2)}, u32[]{:S(2)}) collective-permute-start(bf16[256,1024]{1,0:T(8,128)(2,1)} %copy-done.9), channel_id=1, source_target_pairs={{0,4},{1,3},{2,6},{3,1},{4,0},{5,7},{6,2},{7,5},{8,12},{9,11},{10,... | collective-permute-start | bytes 1572872 | tf_op jit(solution)/shard_map/r_left0/ppermute | solution.py:116
  84.8 10.5 %collective-permute-start.31 = (f32[2,4,128]{2,1,0:T(4,128)S(1)}, f32[2,4,128]{2,1,0:T(4,128)S(1)}, u32[]{:S(2)}, u32[]{:S(2)}) collective-permute-start(f32[2,4,128]{2,1,0:T(4,128)S(1)} %pad_maximum_fusion), channel_id=1, source_target_pairs={{0,1},{1,0},{2,3},{3,2},{4,5},{5,4},{6,7},{7,6},{8,9},{9,8},{10,11... | collective-permute-start | bytes 12296 | tf_op jit(solution)/shard_map/t_core/ppermute | solution.py:116
  94.2 9.5 %collective-permute-start.26 = (bf16[256,1024]{1,0:T(8,128)(2,1)}, bf16[256,1024]{1,0:T(8,128)(2,1)S(1)}, u32[]{:S(2)}, u32[]{:S(2)}) collective-permute-start(bf16[256,1024]{1,0:T(8,128)(2,1)} %get-tuple-element.107), channel_id=1, source_target_pairs={{0,2},{1,5},{2,0},{3,7},{4,6},{5,1},{6,4},{7,3},{8,10},{9,13},{10,... | collective-permute-start | bytes 1572872 | tf_op jit(solution)/shard_map/r_corner1/ppermute | solution.py:116
  99.0 15.6 %collective-permute-start.27 = (bf16[256,1024]{1,0:T(8,128)(2,1)}, bf16[256,1024]{1,0:T(8,128)(2,1)S(1)}, u32[]{:S(2)}, u32[]{:S(2)}) collective-permute-start(bf16[256,1024]{1,0:T(8,128)(2,1)} %copy-done.17), channel_id=1, source_target_pairs={{0,2},{1,5},{2,0},{3,7},{4,6},{5,1},{6,4},{7,3},{8,10},{9,13},{10,... | collective-permute-start | bytes 1572872 | tf_op jit(solution)/shard_map/r_right1/ppermute | solution.py:116
  99.9 14.6 %collective-permute-start.25 = (bf16[128,1024]{1,0:T(8,128)(2,1)S(1)}, bf16[128,1024]{1,0:T(8,128)(2,1)S(1)}, u32[]{:S(2)}, u32[]{:S(2)}) collective-permute-start(bf16[128,1024]{1,0:T(8,128)(2,1)S(1)} %get-tuple-element.104), channel_id=1, source_target_pairs={{0,16},{1,17},{2,18},{3,19},{4,20},{5,21},{6,22},{7,23},{8,24},{9,... | collective-permute-start | bytes 786440 | tf_op jit(solution)/shard_map/r_z2/ppermute | solution.py:116
  105.1 9.5 %collective-permute-start.33 = (f32[4,128]{1,0:T(4,128)S(1)}, f32[4,128]{1,0:T(4,128)S(1)}, u32[]{:S(2)}, u32[]{:S(2)}) collective-permute-start(f32[4,128]{1,0:T(4,128)S(1)} %get-tuple-element.124), channel_id=1, source_target_pairs={{0,4},{1,5},{2,6},{3,7},{4,0},{5,1},{6,2},{7,3},{8,12},{9,13},{10,... | collective-permute-start | bytes 6152 | tf_op jit(solution)/shard_map/t_y/ppermute | solution.py:116
  106.5 15.6 %collective-permute-start.28 = (bf16[256,1024]{1,0:T(8,128)(2,1)S(1)}, bf16[256,1024]{1,0:T(8,128)(2,1)S(1)}, u32[]{:S(2)}, u32[]{:S(2)}) collective-permute-start(bf16[256,1024]{1,0:T(8,128)(2,1)S(1)} %corner.3), channel_id=1, source_target_pairs={{0,4},{1,3},{2,6},{3,1},{4,0},{5,7},{6,2},{7,5},{8,12},{9,11},{10,... | collective-permute-start | bytes 1572872 | tf_op jit(solution)/shard_map/r_left1/ppermute | solution.py:116
  123.1 12.8 %collective-permute-start.30 = (bf16[128,1024]{1,0:T(8,128)(2,1)S(1)}, bf16[128,1024]{1,0:T(8,128)(2,1)S(1)}, u32[]{:S(2)}, u32[]{:S(2)}) collective-permute-start(bf16[128,1024]{1,0:T(8,128)(2,1)S(1)} %get-tuple-element.111), channel_id=1, source_target_pairs={{0,24},{1,25},{2,26},{3,27},{4,28},{5,29},{6,30},{7,31},{8,16},{9,... | collective-permute-start | bytes 786440 | tf_op jit(solution)/shard_map/r_z3/ppermute | solution.py:116
  (34 other events, 171.9 us)

commit v4 on v3

--- a/solution.py
+++ b/solution.py
@@ -253,7 +253,7 @@
 
         def weight(dx, k):
             source = (d_ref, o_ref)[k].at[:, columns(2 * (x ^ dx) + c)]
-            return pltpu.make_async_copy(source, w_v.at[dx, k], w_sem.at[dx, k])
+            return pltpu.make_async_copy(source, w_v.at[dx, pl.ds(k * hid, hid), :], w_sem.at[dx, k])
 
         def piece(i, j, dx, dy):
             target = rows_v.at[dx, pl.ds(dy * half + i * tokens, tokens), :]
@@ -274,7 +274,7 @@
                 def _(i=i, dx=dx):
                     piece(i, 2, dx, 1 - dx).start()
 
-        total = [None, None]
+        total = None
         begin(0)
         for dx in range(NX):
             for i in range(count):
@@ -284,11 +284,10 @@
                 weight(dx, k).wait()
             if dx + 1 < NX:
                 begin(dx + 1)
-            for k in (1, 0):
-                part = dot_nt(rows_v[dx], w_v[dx, k])
-                total[k] = part if dx == 0 else total[k] + part
-        theirs[...] = total[1].astype(BF16)
-        mine[...] = total[0]
+            part = dot_nt(rows_v[dx], w_v[dx])
+            total = part if dx == 0 else total + part
+        mine[...] = total[:, :hid]
+        theirs[...] = total[:, hid:].astype(BF16)
 
     flat = [p for four in pieces for p in four]
     spec = lambda cols: pl.BlockSpec((rows, cols), lambda i, s: (0, 0))
@@ -305,7 +304,7 @@
         got,
         scratch=[
             pltpu.VMEM((NX, rows, quarter), BF16),
-            pltpu.VMEM((NX, 2, hid, quarter), BF16),
+            pltpu.VMEM((NX, 2 * hid, quarter), BF16),
             pltpu.SemaphoreType.DMA((count, NX, NY)),
             pltpu.SemaphoreType.DMA((NX, 2)),
         ],
@@ -360,7 +359,8 @@
         def weight(n, j):
             dx, h = order[n]
             first = pl.multiple_of((2 * (x ^ dx) + c) * quarter + h * wide, wide)
-            return pltpu.make_async_copy(sources[j].at[pl.ds(first, wide), :], w_v.at[n, j], sem.at[n, j])
+            target = w_v.at[n, j // 2, :, pl.ds((j % 2) * hid, hid)]
+            return pltpu.make_async_copy(sources[j].at[pl.ds(first, wide), :], target, sem.at[n, j])
 
         def side(k):
             return pltpu.make_async_copy((m_ref, t_ref)[k], side_v.at[k], side_sem.at[k])
@@ -378,14 +378,16 @@
         side(0).wait()
         for n, (dx, h) in enumerate(order):
             total = None
-            for j in range(4):
-                weight(n, j).wait()
-                if n == 0 and j == 2:
+            for k in range(2):
+                for j in (2 * k, 2 * k + 1):
+                    weight(n, j).wait()
+                if n == 0 and k == 1:
                     side(1).wait()
-                part = dot_nt(side_v[j // 2, :, (j % 2) * hid : (j % 2 + 1) * hid], w_v[n, j])
-                total = part if j == 0 else total + part
-                if n + 2 < len(order):
-                    weight(n + 2, j).start()
+                part = dot_nt(side_v[k], w_v[n, k])
+                total = part if k == 0 else total + part
+                for j in (2 * k, 2 * k + 1):
+                    if n + 2 < len(order):
+                        weight(n + 2, j).start()
             o_v[n, 0] = total[:rows].astype(BF16)
             o_v[n, 1] = total[rows:].astype(BF16)
             give(0 if dx == 1 else 3, n, dx).start()
@@ -417,7 +419,7 @@
         *got,
         scratch=[
             pltpu.VMEM((2,) + mine.shape, BF16),
-            pltpu.VMEM((len(order), 4, wide, hid), BF16),
+            pltpu.VMEM((len(order), 2, wide, 2 * hid), BF16),
             pltpu.VMEM((len(order), NY, rows, wide), BF16),
             pltpu.SemaphoreType.DMA((2,)),
             pltpu.SemaphoreType.DMA((len(order), 4)),
@@ -487,13 +489,15 @@
     first2, second2 = send(z2, RIGHT, "first2"), send(z2, LEFT, "second2")
     third0 = send(first0, LEFT, "third0")
     z3 = send(z2, TO_Z[1], "z3")
-    got_gate, got_up = send(gate_w_, TO_CORE, "weights"), send(up_w_, TO_CORE, "weights")
-
-    z1, z3, first2, second2, third0, got_gate, got_up = lax.optimization_barrier(
-        (z1, z3, first2, second2, third0, got_gate, got_up)
-    )
+    got_gate = send(gate_w_, TO_CORE, "weights")
+
+    z1, z3, first2, second2, third0, got_gate, up_w_ = lax.optimization_barrier(
+        (z1, z3, first2, second2, third0, got_gate, up_w_)
+    )
+    got_up = send(up_w_, TO_CORE, "weights")
     third2 = send(first2, LEFT, "third2")
     first1, second1 = send(z1, RIGHT, "first1"), send(z1, LEFT, "second1")
+    first3 = send(z3, RIGHT, "first3")
     saved = saved_gate[0], saved_up[0]
     factors_a = prepare(
         at_expert, at_block, [(own, first0, second0), (z2, first2, second2)], *saved, near
@@ -514,9 +518,10 @@
     mine, theirs = hidden_parts(
         place, [(own, first0, second0, third0), (z2, first2, second2, third2)], down, got_down
     )
-    theirs, first1, second1 = lax.optimization_barrier((theirs, first1, second1))
+    theirs, first1, second1, got_up, first3 = lax.optimization_barrier((theirs, first1, second1, got_up, first3))
     back = send(theirs, TO_CORE, "swap_bh0")
-    first3, second3 = send(z3, RIGHT, "first3"), send(z3, LEFT, "second3")
+    second3 = send(z3, LEFT, "second3")
+    third3 = send(first3, LEFT, "third3")
     third1 = send(first1, LEFT, "third1")
     mine, term_a = pre_grads(after(at_block, mine), mine, back, factors_a)
     theirs = send(mine, TO_CORE, "swap_h0")
@@ -525,8 +530,6 @@
     place = after(at_block, base_a)
     corner_a, right_a = send(corner_a, LEFT, "r_corner0"), send(right_a, LEFT, "r_right0")
 
-    first3, _ = lax.optimization_barrier((first3, base_a))
-    third3 = send(first3, LEFT, "third3")
     factors_b = prepare(
         at_expert, place, [(z1, first1, second1), (z3, first3, second3)], *saved, far
     )
@@ -546,7 +549,7 @@
     corner_b, right_b = send(corner_b, LEFT, "r_corner1"), send(right_b, LEFT, "r_right1")
     sums, value = stage_add(place, near, base_a, right_a, left_a)
     left_b, value = stage_corner(after(at_block, value), far, left_b, corner_b)
-    more, _ = stage_add(after(at_block, value, sums[2]), far, base_b, right_b, left_b)
+    more, kept = stage_add(after(at_block, value, sums[2]), far, base_b, right_b, left_b)
     sums.update(more)
     grad_in = last_sum(at_block, sums[0], [sums[d] for d in (2, 1, 3)], BF16)
 
@@ -556,7 +559,7 @@
     term = term + send(after(term, base_b), TO_X, "t_x")
     term = after(term, value)
     term = jnp.stack([term[0], send(term[1], TO_Y, "t_y")], axis=1)
-    term = after(term, right_b)
+    term = after(term, kept)
     slots = [term[0]] + [send(term[d], TO_Z[d], f"t_z{d}") for d in range(1, NZ)]
     slot_grad = jnp.zeros((experts, tokens), F32)
     ids = jnp.arange(experts, dtype=jnp.int32)

time: 137 us -> 124 us (0.905)
  local copies, waits for them, and re-layouts: 10.9 us -> 5.93 us
  Pallas kernels: 34.7 us -> 30.3 us
  starting transfers between devices: 43.5 us -> 39.5 us
    unnamed x42 -> x20, local copies, waits for them, and re-layouts: 10.9 us -> 5.9 us
    pallas_call x11, Pallas kernels: 30.2 us -> 25.8 us  [kernel(): pl.pallas_call(body, out_shape=outs, grid_spec=pltpu.PrefetchScalarGridSp...]
    ppermute x37, starting transfers between devices: 43.5 us -> 39.5 us  [send(): return lax.ppermute(value, BOTH, pairs)]
  transfers between devices with their start and end apart: 37 -> 37, of which waited for: 15 -> 20; matrix products, arithmetic and copies ran while one was open for 1% -> 1% of each run, Pallas kernels for 24% -> 23%
where the time goes in v4:
time: 124 us; the launch traced here: 123 us
  waiting for transfers between devices  45.9 us (37%)
  starting transfers between devices  39.5 us (32%)
  Pallas kernels  30.3 us (24%)
  local copies, waits for them, and re-layouts  5.93 us (5%)
    ppermute x37, waiting for transfers between devices, send(): return lax.ppermute(value, BOTH, pairs)  45.9 us
    ppermute x37, starting transfers between devices, send(): return lax.ppermute(value, BOTH, pairs)  39.5 us
    pallas_call x11, Pallas kernels, kernel(): pl.pallas_call(body, out_shape=outs, grid_spec=pltpu.PrefetchScalarGridSp...  25.8 us
    unnamed x20, local copies, waits for them, and re-layouts  5.9 us
    pallas_call x2, Pallas kernels, prepare(): pl.pallas_call(body, out_shape=[out] * 3, grid_spec=pltpu.PrefetchScalarG...  2.53 us
  transfers between devices with their start and end apart: 37, of which 20 were waited for; matrix products, arithmetic and copies ran while one was open for 1% of the time, Pallas kernels for 23%

profile of v4, /device:TPU:0, one launch (start us, length us, event | category | flops | bytes accessed | tf_op | source)
XLA Modules:
  0.0 123.3 jit_solution(1287753249733324357)
XLA Ops:
  1.1 2.0 %pack.1 = (bf16[136,1024]{1,0:T(8,128)(2,1)}, f32[8,128]{1,0:T(8,128)}) custom-call(bf16[128,1024]{1,0:T(8,128)(2,1)} %g_ref.1, s32[8,128]{1,0:T(8,128)} %bitcast.46, bf16[8,128]{1,0:T(8,128)(2,1)} %bitcast.47), custom_call_target="tpu_custom_call" | custom-call | tf_op jit(solution)/shard_map/pack/pallas_call | solution.py:177
  3.1 3.6 %collective-permute-start = (bf16[136,1024]{1,0:T(8,128)(2,1)}, bf16[136,1024]{1,0:T(8,128)(2,1)S(1)}, u32[]{:S(2)}, u32[]{:S(2)}) collective-permute-start(bf16[136,1024]{1,0:T(8,128)(2,1)} %get-tuple-element.60.refs_0_), channel_id=1, source_target_pairs={{0,16},{1,17},{2,18},{3,19},{4,20},{5,21},{6,22},{7,23},{8,24},{9,... | collective-permute-start | bytes 835592 | tf_op jit(solution)/shard_map/z2/ppermute | solution.py:116
  6.7 1.6 %collective-permute-start.1 = (bf16[136,1024]{1,0:T(8,128)(2,1)}, bf16[136,1024]{1,0:T(8,128)(2,1)S(1)}, u32[]{:S(2)}, u32[]{:S(2)}) collective-permute-start(bf16[136,1024]{1,0:T(8,128)(2,1)} %get-tuple-element.60.refs_0_), channel_id=1, source_target_pairs={{0,8},{1,9},{2,10},{3,11},{4,12},{5,13},{6,14},{7,15},{8,0},{9,1},... | collective-permute-start | bytes 835592 | tf_op jit(solution)/shard_map/z1/ppermute | solution.py:116
  8.3 1.5 %collective-permute-start.2 = (bf16[136,1024]{1,0:T(8,128)(2,1)}, bf16[136,1024]{1,0:T(8,128)(2,1)S(1)}, u32[]{:S(2)}, u32[]{:S(2)}) collective-permute-start(bf16[136,1024]{1,0:T(8,128)(2,1)} %get-tuple-element.60.refs_0_), channel_id=1, source_target_pairs={{0,4},{1,3},{2,6},{3,1},{4,0},{5,7},{6,2},{7,5},{8,12},{9,11},{10,... | collective-permute-start | bytes 835592 | tf_op jit(solution)/shard_map/first0/ppermute | solution.py:116
  9.8 1.5 %collective-permute-start.3 = (bf16[136,1024]{1,0:T(8,128)(2,1)}, bf16[136,1024]{1,0:T(8,128)(2,1)S(1)}, u32[]{:S(2)}, u32[]{:S(2)}) collective-permute-start(bf16[136,1024]{1,0:T(8,128)(2,1)} %get-tuple-element.60.refs_0_), channel_id=1, source_target_pairs={{0,2},{1,5},{2,0},{3,7},{4,6},{5,1},{6,4},{7,3},{8,10},{9,13},{10,... | collective-permute-start | bytes 835592 | tf_op jit(solution)/shard_map/second0/ppermute | solution.py:116
  11.3 9.0 %collective-permute-done.refs_3_.refs_4_ = bf16[136,1024]{1,0:T(8,128)(2,1)S(1)} collective-permute-done((bf16[136,1024]{1,0:T(8,128)(2,1)}, bf16[136,1024]{1,0:T(8,128)(2,1)S(1)}, u32[]{:S(2)}, u32[]{:S(2)}) %collective-permute-start) | collective-permute-done | bytes 278560 | tf_op jit(solution)/shard_map/z2/ppermute | solution.py:116
  20.6 1.6 %collective-permute-start.5 = (bf16[136,1024]{1,0:T(8,128)(2,1)S(1)}, bf16[136,1024]{1,0:T(8,128)(2,1)S(1)}, u32[]{:S(2)}, u32[]{:S(2)}) collective-permute-start(bf16[136,1024]{1,0:T(8,128)(2,1)S(1)} %collective-permute-done.refs_3_.refs_4_), channel_id=1, source_target_pairs={{0,8},{1,9},{2,10},{3,11},{4,12},{5,13},{6,14},{7,15},{8,0},{9,1},... | collective-permute-start | bytes 835592 | tf_op jit(solution)/shard_map/z3/ppermute | solution.py:116
  22.1 1.5 %collective-permute-start.6 = (bf16[136,1024]{1,0:T(8,128)(2,1)S(1)}, bf16[136,1024]{1,0:T(8,128)(2,1)S(1)}, u32[]{:S(2)}, u32[]{:S(2)}) collective-permute-start(bf16[136,1024]{1,0:T(8,128)(2,1)S(1)} %collective-permute-done.refs_3_.refs_4_), channel_id=1, source_target_pairs={{0,4},{1,3},{2,6},{3,1},{4,0},{5,7},{6,2},{7,5},{8,12},{9,11},{10,... | collective-permute-start | bytes 835592 | tf_op jit(solution)/shard_map/first2/ppermute | solution.py:116
  23.7 1.5 %collective-permute-start.7 = (bf16[136,1024]{1,0:T(8,128)(2,1)S(1)}, bf16[136,1024]{1,0:T(8,128)(2,1)S(1)}, u32[]{:S(2)}, u32[]{:S(2)}) collective-permute-start(bf16[136,1024]{1,0:T(8,128)(2,1)S(1)} %collective-permute-done.refs_3_.refs_4_), channel_id=1, source_target_pairs={{0,2},{1,5},{2,0},{3,7},{4,6},{5,1},{6,4},{7,3},{8,10},{9,13},{10,... | collective-permute-start | bytes 835592 | tf_op jit(solution)/shard_map/second2/ppermute | solution.py:116
  25.7 4.0 %collective-permute-done.5.refs_3_.refs_4_ = bf16[136,1024]{1,0:T(8,128)(2,1)S(1)} collective-permute-done((bf16[136,1024]{1,0:T(8,128)(2,1)S(1)}, bf16[136,1024]{1,0:T(8,128)(2,1)S(1)}, u32[]{:S(2)}, u32[]{:S(2)}) %collective-permute-start.5) | collective-permute-done | bytes 278560 | tf_op jit(solution)/shard_map/z3/ppermute | solution.py:116
  29.7 1.7 %collective-permute-done.6.refs_4_.refs_5_ = bf16[136,1024]{1,0:T(8,128)(2,1)S(1)} collective-permute-done((bf16[136,1024]{1,0:T(8,128)(2,1)S(1)}, bf16[136,1024]{1,0:T(8,128)(2,1)S(1)}, u32[]{:S(2)}, u32[]{:S(2)}) %collective-permute-start.6) | collective-permute-done | bytes 278560 | tf_op jit(solution)/shard_map/first2/ppermute | solution.py:116
  31.4 2.5 %collective-permute-done.8.refs_3_ = bf16[136,1024]{1,0:T(8,128)(2,1)S(1)} collective-permute-done((bf16[136,1024]{1,0:T(8,128)(2,1)S(1)}, bf16[136,1024]{1,0:T(8,128)(2,1)S(1)}, u32[]{:S(2)}, u32[]{:S(2)}) %collective-permute-start.8) | collective-permute-done | bytes 278560 | tf_op jit(solution)/shard_map/third0/ppermute | solution.py:116
  35.5 1.5 %collective-permute-start.11 = (bf16[136,1024]{1,0:T(8,128)(2,1)S(1)}, bf16[136,1024]{1,0:T(8,128)(2,1)S(1)}, u32[]{:S(2)}, u32[]{:S(2)}) collective-permute-start(bf16[136,1024]{1,0:T(8,128)(2,1)S(1)} %collective-permute-done.1.refs_0_), channel_id=1, source_target_pairs={{0,4},{1,3},{2,6},{3,1},{4,0},{5,7},{6,2},{7,5},{8,12},{9,11},{10,... | collective-permute-start | bytes 835592 | tf_op jit(solution)/shard_map/first1/ppermute | solution.py:116
  43.7 4.7 %hidden.2 = (f32[512,384]{1,0:T(8,128)S(1)}, bf16[512,384]{1,0:T(8,128)(2,1)S(1)}) custom-call(s32[1]{0:T(128)} %bitcast.s_ref, bf16[136,1024]{1,0:T(8,128)(2,1)S(1)} %copy-done.4, bf16[136,1024]{1,0:T(8,128)(2,1)S(1)} %collective-permute-done.2.refs_1_, bf16[136,1024]{1,0:T(8,128)(2,1)S(1)} %collective-permute-done.3.refs_2_, ...), custom_call_target="tpu_custom_call" | custom-call | tf_op jit(solution)/shard_map/hidden/pallas_call | solution.py:136
  49.8 1.6 %collective-permute-done.15.b_ref = bf16[512,384]{1,0:T(8,128)(2,1)S(1)} collective-permute-done((bf16[512,384]{1,0:T(8,128)(2,1)S(1)}, bf16[512,384]{1,0:T(8,128)(2,1)S(1)}, u32[]{:S(2)}, u32[]{:S(2)}) %collective-permute-start.15) | collective-permute-done | bytes 393248 | tf_op jit(solution)/shard_map/swap_bh0/ppermute | solution.py:116
  55.1 6.1 %input.2 = (bf16[256,1024]{1,0:T(8,128)(2,1)S(1)}, bf16[256,1024]{1,0:T(8,128)(2,1)}, bf16[256,1024]{1,0:T(8,128)(2,1)S(1)}, bf16[256,1024]{1,0:T(8,128)(2,1)S(1)}) custom-call(s32[1]{0:T(128)} %bitcast.s_ref, bf16[512,768]{1,0:T(8,128)(2,1)S(1)} %get-tuple-element.82.m_ref, bf16[512,768]{1,0:T(8,128)(2,1)S(1)} %collective-permute-done.16.t_ref, ...), custom_call_target="tpu_custom_call" | custom-call | tf_op jit(solution)/shard_map/input/pallas_call | solution.py:136
  64.6 4.7 %hidden.3 = (f32[512,384]{1,0:T(8,128)S(1)}, bf16[512,384]{1,0:T(8,128)(2,1)S(1)}) custom-call(s32[1]{0:T(128)} %bitcast.s_ref, bf16[136,1024]{1,0:T(8,128)(2,1)S(1)} %collective-permute-done.1.refs_0_, bf16[136,1024]{1,0:T(8,128)(2,1)S(1)} %collective-permute-done.11.refs_1_, bf16[136,1024]{1,0:T(8,128)(2,1)S(1)} %collective-permute-done.12.refs_2_, ...), custom_call_target="tpu_custom_call" | custom-call | tf_op jit(solution)/shard_map/hidden/pallas_call | solution.py:136
  72.8 1.5 %collective-permute-start.24 = (bf16[256,1024]{1,0:T(8,128)(2,1)S(1)}, bf16[256,1024]{1,0:T(8,128)(2,1)}, u32[]{:S(2)}, u32[]{:S(2)}) collective-permute-start(bf16[256,1024]{1,0:T(8,128)(2,1)S(1)} %corner.2), channel_id=1, source_target_pairs={{0,4},{1,3},{2,6},{3,1},{4,0},{5,7},{6,2},{7,5},{8,12},{9,11},{10,... | collective-permute-start | bytes 1572872 | tf_op jit(solution)/shard_map/r_left0/ppermute | solution.py:116
  74.2 6.3 %input.3 = (bf16[256,1024]{1,0:T(8,128)(2,1)}, bf16[256,1024]{1,0:T(8,128)(2,1)S(1)}, bf16[256,1024]{1,0:T(8,128)(2,1)S(1)}, bf16[256,1024]{1,0:T(8,128)(2,1)S(1)}) custom-call(s32[1]{0:T(128)} %bitcast.s_ref, bf16[512,768]{1,0:T(8,128)(2,1)S(1)} %get-tuple-element.99.m_ref, bf16[512,768]{1,0:T(8,128)(2,1)S(1)} %collective-permute-done.22.t_ref, ...), custom_call_target="tpu_custom_call" | custom-call | tf_op jit(solution)/shard_map/input/pallas_call | solution.py:136
  89.0 2.4 %collective-permute-start.25 = (bf16[128,1024]{1,0:T(8,128)(2,1)S(1)}, bf16[128,1024]{1,0:T(8,128)(2,1)S(1)}, u32[]{:S(2)}, u32[]{:S(2)}) collective-permute-start(bf16[128,1024]{1,0:T(8,128)(2,1)S(1)} %get-tuple-element.104), channel_id=1, source_target_pairs={{0,16},{1,17},{2,18},{3,19},{4,20},{5,21},{6,22},{7,23},{8,24},{9,... | collective-permute-start | bytes 786440 | tf_op jit(solution)/shard_map/r_z2/ppermute | solution.py:116
  96.0 7.3 %collective-permute-done.25.refs_0_ = bf16[128,1024]{1,0:T(8,128)(2,1)S(1)} collective-permute-done((bf16[128,1024]{1,0:T(8,128)(2,1)S(1)}, bf16[128,1024]{1,0:T(8,128)(2,1)S(1)}, u32[]{:S(2)}, u32[]{:S(2)}) %collective-permute-start.25) | collective-permute-done | bytes 262176 | tf_op jit(solution)/shard_map/r_z2/ppermute | solution.py:116
  106.5 4.0 %collective-permute-start.35 = (f32[2,128]{1,0:T(2,128)S(1)}, f32[2,128]{1,0:T(2,128)S(1)}, u32[]{:S(2)}, u32[]{:S(2)}) collective-permute-start(f32[2,128]{1,0:T(2,128)S(1)} %bitcast.50), channel_id=1, source_target_pairs={{0,16},{1,17},{2,18},{3,19},{4,20},{5,21},{6,22},{7,23},{8,24},{9,... | collective-permute-start | bytes 3080 | tf_op jit(solution)/shard_map/t_z2/ppermute | solution.py:116
  113.1 2.1 %collective-permute-done.36 = f32[2,128]{1,0:T(2,128)S(1)} collective-permute-done((f32[2,128]{1,0:T(2,128)S(1)}, f32[2,128]{1,0:T(2,128)S(1)}, u32[]{:S(2)}, u32[]{:S(2)}) %collective-permute-start.36) | collective-permute-done | bytes 1056 | tf_op jit(solution)/shard_map/t_z1/ppermute | solution.py:116
  115.9 6.5 %collective-permute-done.30.refs_2_ = bf16[128,1024]{1,0:T(8,128)(2,1)S(1)} collective-permute-done((bf16[128,1024]{1,0:T(8,128)(2,1)S(1)}, bf16[128,1024]{1,0:T(8,128)(2,1)S(1)}, u32[]{:S(2)}, u32[]{:S(2)}) %collective-permute-start.30) | collective-permute-done | bytes 262176 | tf_op jit(solution)/shard_map/r_z3/ppermute | solution.py:116
  (102 shorter events, 41.8 us)
Async XLA Ops:
  0.6 19.9 %collective-permute-start.4 = (bf16[384,4096]{1,0:T(8,128)(2,1)}, bf16[384,4096]{1,0:T(8,128)(2,1)}, u32[]{:S(2)}, u32[]{:S(2)}) collective-permute-start(bf16[384,4096]{1,0:T(8,128)(2,1)} %bitcast.37), channel_id=1, source_target_pairs={{0,1},{1,0},{2,3},{3,2},{4,5},{5,4},{6,7},{7,6},{8,9},{9,8},{10,11... | collective-permute-start | bytes 9437192 | tf_op jit(solution)/shard_map/weights/ppermute | solution.py:116
  3.1 17.2 %collective-permute-start = (bf16[136,1024]{1,0:T(8,128)(2,1)}, bf16[136,1024]{1,0:T(8,128)(2,1)S(1)}, u32[]{:S(2)}, u32[]{:S(2)}) collective-permute-start(bf16[136,1024]{1,0:T(8,128)(2,1)} %get-tuple-element.60.refs_0_), channel_id=1, source_target_pairs={{0,16},{1,17},{2,18},{3,19},{4,20},{5,21},{6,22},{7,23},{8,24},{9,... | collective-permute-start | bytes 835592 | tf_op jit(solution)/shard_map/z2/ppermute | solution.py:116
  6.7 13.8 %collective-permute-start.1 = (bf16[136,1024]{1,0:T(8,128)(2,1)}, bf16[136,1024]{1,0:T(8,128)(2,1)S(1)}, u32[]{:S(2)}, u32[]{:S(2)}) collective-permute-start(bf16[136,1024]{1,0:T(8,128)(2,1)} %get-tuple-element.60.refs_0_), channel_id=1, source_target_pairs={{0,8},{1,9},{2,10},{3,11},{4,12},{5,13},{6,14},{7,15},{8,0},{9,1},... | collective-permute-start | bytes 835592 | tf_op jit(solution)/shard_map/z1/ppermute | solution.py:116
  8.3 12.2 %collective-permute-start.2 = (bf16[136,1024]{1,0:T(8,128)(2,1)}, bf16[136,1024]{1,0:T(8,128)(2,1)S(1)}, u32[]{:S(2)}, u32[]{:S(2)}) collective-permute-start(bf16[136,1024]{1,0:T(8,128)(2,1)} %get-tuple-element.60.refs_0_), channel_id=1, source_target_pairs={{0,4},{1,3},{2,6},{3,1},{4,0},{5,7},{6,2},{7,5},{8,12},{9,11},{10,... | collective-permute-start | bytes 835592 | tf_op jit(solution)/shard_map/first0/ppermute | solution.py:116
  9.8 10.7 %collective-permute-start.3 = (bf16[136,1024]{1,0:T(8,128)(2,1)}, bf16[136,1024]{1,0:T(8,128)(2,1)S(1)}, u32[]{:S(2)}, u32[]{:S(2)}) collective-permute-start(bf16[136,1024]{1,0:T(8,128)(2,1)} %get-tuple-element.60.refs_0_), channel_id=1, source_target_pairs={{0,2},{1,5},{2,0},{3,7},{4,6},{5,1},{6,4},{7,3},{8,10},{9,13},{10,... | collective-permute-start | bytes 835592 | tf_op jit(solution)/shard_map/second0/ppermute | solution.py:116
  20.5 13.4 %collective-permute-start.9 = (bf16[4096,384]{1,0:T(8,128)(2,1)}, bf16[4096,384]{1,0:T(8,128)(2,1)S(1)}, u32[]{:S(2)}, u32[]{:S(2)}) collective-permute-start(bf16[4096,384]{1,0:T(8,128)(2,1)} %bitcast.40), channel_id=1, source_target_pairs={{0,1},{1,0},{2,3},{3,2},{4,5},{5,4},{6,7},{7,6},{8,9},{9,8},{10,11... | collective-permute-start | bytes 9437192 | tf_op jit(solution)/shard_map/weights/ppermute | solution.py:116
  33.9 15.8 %collective-permute-start.13 = (bf16[4096,384]{1,0:T(8,128)(2,1)}, bf16[4096,384]{1,0:T(8,128)(2,1)}, u32[]{:S(2)}, u32[]{:S(2)}) collective-permute-start(bf16[4096,384]{1,0:T(8,128)(2,1)} %bitcast.43), channel_id=1, source_target_pairs={{0,1},{1,0},{2,3},{3,2},{4,5},{5,4},{6,7},{7,6},{8,9},{9,8},{10,11... | collective-permute-start | bytes 9437192 | tf_op jit(solution)/shard_map/weights/ppermute | solution.py:116
  35.5 12.9 %collective-permute-start.11 = (bf16[136,1024]{1,0:T(8,128)(2,1)S(1)}, bf16[136,1024]{1,0:T(8,128)(2,1)S(1)}, u32[]{:S(2)}, u32[]{:S(2)}) collective-permute-start(bf16[136,1024]{1,0:T(8,128)(2,1)S(1)} %collective-permute-done.1.refs_0_), channel_id=1, source_target_pairs={{0,4},{1,3},{2,6},{3,1},{4,0},{5,7},{6,2},{7,5},{8,12},{9,11},{10,... | collective-permute-start | bytes 835592 | tf_op jit(solution)/shard_map/first1/ppermute | solution.py:116
  37.0 12.7 %collective-permute-start.12 = (bf16[136,1024]{1,0:T(8,128)(2,1)S(1)}, bf16[136,1024]{1,0:T(8,128)(2,1)S(1)}, u32[]{:S(2)}, u32[]{:S(2)}) collective-permute-start(bf16[136,1024]{1,0:T(8,128)(2,1)S(1)} %collective-permute-done.1.refs_0_), channel_id=1, source_target_pairs={{0,2},{1,5},{2,0},{3,7},{4,6},{5,1},{6,4},{7,3},{8,10},{9,13},{10,... | collective-permute-start | bytes 835592 | tf_op jit(solution)/shard_map/second1/ppermute | solution.py:116
  38.0 11.6 %collective-permute-start.14 = (bf16[136,1024]{1,0:T(8,128)(2,1)S(1)}, bf16[136,1024]{1,0:T(8,128)(2,1)S(1)}, u32[]{:S(2)}, u32[]{:S(2)}) collective-permute-start(bf16[136,1024]{1,0:T(8,128)(2,1)S(1)} %collective-permute-done.5.refs_3_.refs_4_), channel_id=1, source_target_pairs={{0,4},{1,3},{2,6},{3,1},{4,0},{5,7},{6,2},{7,5},{8,12},{9,11},{10,... | collective-permute-start | bytes 835592 | tf_op jit(solution)/shard_map/first3/ppermute | solution.py:116
  52.1 10.3 %collective-permute-start.17 = (bf16[136,1024]{1,0:T(8,128)(2,1)S(1)}, bf16[136,1024]{1,0:T(8,128)(2,1)S(1)}, u32[]{:S(2)}, u32[]{:S(2)}) collective-permute-start(bf16[136,1024]{1,0:T(8,128)(2,1)S(1)} %collective-permute-done.5.refs_3_.refs_4_), channel_id=1, source_target_pairs={{0,2},{1,5},{2,0},{3,7},{4,6},{5,1},{6,4},{7,3},{8,10},{9,13},{10,... | collective-permute-start | bytes 835592 | tf_op jit(solution)/shard_map/second3/ppermute | solution.py:116
  53.0 10.6 %collective-permute-start.18 = (bf16[136,1024]{1,0:T(8,128)(2,1)S(1)}, bf16[136,1024]{1,0:T(8,128)(2,1)S(1)}, u32[]{:S(2)}, u32[]{:S(2)}) collective-permute-start(bf16[136,1024]{1,0:T(8,128)(2,1)S(1)} %collective-permute-done.11.refs_1_), channel_id=1, source_target_pairs={{0,2},{1,5},{2,0},{3,7},{4,6},{5,1},{6,4},{7,3},{8,10},{9,13},{10,... | collective-permute-start | bytes 835592 | tf_op jit(solution)/shard_map/third1/ppermute | solution.py:116
  54.1 10.5 %collective-permute-start.19 = (bf16[136,1024]{1,0:T(8,128)(2,1)S(1)}, bf16[136,1024]{1,0:T(8,128)(2,1)S(1)}, u32[]{:S(2)}, u32[]{:S(2)}) collective-permute-start(bf16[136,1024]{1,0:T(8,128)(2,1)S(1)} %collective-permute-done.14.refs_4_.refs_5_), channel_id=1, source_target_pairs={{0,2},{1,5},{2,0},{3,7},{4,6},{5,1},{6,4},{7,3},{8,10},{9,13},{10,... | collective-permute-start | bytes 835592 | tf_op jit(solution)/shard_map/third3/ppermute | solution.py:116
  61.2 9.2 %collective-permute-start.20 = (bf16[256,1024]{1,0:T(8,128)(2,1)S(1)}, bf16[256,1024]{1,0:T(8,128)(2,1)S(1)}, u32[]{:S(2)}, u32[]{:S(2)}) collective-permute-start(bf16[256,1024]{1,0:T(8,128)(2,1)S(1)} %get-tuple-element.94), channel_id=1, source_target_pairs={{0,2},{1,5},{2,0},{3,7},{4,6},{5,1},{6,4},{7,3},{8,10},{9,13},{10,... | collective-permute-start | bytes 1572872 | tf_op jit(solution)/shard_map/r_corner0/ppermute | solution.py:116
  71.7 15.1 %collective-permute-start.23 = (bf16[256,1024]{1,0:T(8,128)(2,1)}, bf16[256,1024]{1,0:T(8,128)(2,1)}, u32[]{:S(2)}, u32[]{:S(2)}) collective-permute-start(bf16[256,1024]{1,0:T(8,128)(2,1)} %get-tuple-element.102), channel_id=1, source_target_pairs={{0,2},{1,5},{2,0},{3,7},{4,6},{5,1},{6,4},{7,3},{8,10},{9,13},{10,... | collective-permute-start | bytes 1572872 | tf_op jit(solution)/shard_map/r_right0/ppermute | solution.py:116
  72.8 14.9 %collective-permute-start.24 = (bf16[256,1024]{1,0:T(8,128)(2,1)S(1)}, bf16[256,1024]{1,0:T(8,128)(2,1)}, u32[]{:S(2)}, u32[]{:S(2)}) collective-permute-start(bf16[256,1024]{1,0:T(8,128)(2,1)S(1)} %corner.2), channel_id=1, source_target_pairs={{0,4},{1,3},{2,6},{3,1},{4,0},{5,7},{6,2},{7,5},{8,12},{9,11},{10,... | collective-permute-start | bytes 1572872 | tf_op jit(solution)/shard_map/r_left0/ppermute | solution.py:116
  82.2 10.2 %collective-permute-start.26 = (bf16[256,1024]{1,0:T(8,128)(2,1)}, bf16[256,1024]{1,0:T(8,128)(2,1)S(1)}, u32[]{:S(2)}, u32[]{:S(2)}) collective-permute-start(bf16[256,1024]{1,0:T(8,128)(2,1)} %get-tuple-element.107), channel_id=1, source_target_pairs={{0,2},{1,5},{2,0},{3,7},{4,6},{5,1},{6,4},{7,3},{8,10},{9,13},{10,... | collective-permute-start | bytes 1572872 | tf_op jit(solution)/shard_map/r_corner1/ppermute | solution.py:116
  84.2 10.8 %collective-permute-start.32 = (f32[2,4,128]{2,1,0:T(4,128)S(1)}, f32[2,4,128]{2,1,0:T(4,128)S(1)}, u32[]{:S(2)}, u32[]{:S(2)}) collective-permute-start(f32[2,4,128]{2,1,0:T(4,128)S(1)} %fusion), channel_id=1, source_target_pairs={{0,2},{1,3},{2,0},{3,1},{4,6},{5,7},{6,4},{7,5},{8,10},{9,11},{10,... | collective-permute-start | bytes 12296 | tf_op jit(solution)/shard_map/t_x/ppermute | solution.py:116
  89.0 14.3 %collective-permute-start.25 = (bf16[128,1024]{1,0:T(8,128)(2,1)S(1)}, bf16[128,1024]{1,0:T(8,128)(2,1)S(1)}, u32[]{:S(2)}, u32[]{:S(2)}) collective-permute-start(bf16[128,1024]{1,0:T(8,128)(2,1)S(1)} %get-tuple-element.104), channel_id=1, source_target_pairs={{0,16},{1,17},{2,18},{3,19},{4,20},{5,21},{6,22},{7,23},{8,24},{9,... | collective-permute-start | bytes 786440 | tf_op jit(solution)/shard_map/r_z2/ppermute | solution.py:116
  91.4 14.3 %collective-permute-start.27 = (bf16[256,1024]{1,0:T(8,128)(2,1)}, bf16[256,1024]{1,0:T(8,128)(2,1)S(1)}, u32[]{:S(2)}, u32[]{:S(2)}) collective-permute-start(bf16[256,1024]{1,0:T(8,128)(2,1)} %copy-done.7), channel_id=1, source_target_pairs={{0,2},{1,5},{2,0},{3,7},{4,6},{5,1},{6,4},{7,3},{8,10},{9,13},{10,... | collective-permute-start | bytes 1572872 | tf_op jit(solution)/shard_map/r_right1/ppermute | solution.py:116
  93.8 11.9 %collective-permute-start.28 = (bf16[256,1024]{1,0:T(8,128)(2,1)S(1)}, bf16[256,1024]{1,0:T(8,128)(2,1)S(1)}, u32[]{:S(2)}, u32[]{:S(2)}) collective-permute-start(bf16[256,1024]{1,0:T(8,128)(2,1)S(1)} %corner.3), channel_id=1, source_target_pairs={{0,4},{1,3},{2,6},{3,1},{4,0},{5,7},{6,2},{7,5},{8,12},{9,11},{10,... | collective-permute-start | bytes 1572872 | tf_op jit(solution)/shard_map/r_left1/ppermute | solution.py:116
  95.0 9.6 %collective-permute-start.33 = (f32[4,128]{1,0:T(4,128)S(1)}, f32[4,128]{1,0:T(4,128)S(1)}, u32[]{:S(2)}, u32[]{:S(2)}) collective-permute-start(f32[4,128]{1,0:T(4,128)S(1)} %get-tuple-element.124), channel_id=1, source_target_pairs={{0,4},{1,5},{2,6},{3,7},{4,0},{5,1},{6,2},{7,3},{8,12},{9,13},{10,... | collective-permute-start | bytes 6152 | tf_op jit(solution)/shard_map/t_y/ppermute | solution.py:116
  106.1 9.8 %collective-permute-start.29 = (bf16[128,1024]{1,0:T(8,128)(2,1)S(1)}, bf16[128,1024]{1,0:T(8,128)(2,1)S(1)}, u32[]{:S(2)}, u32[]{:S(2)}) collective-permute-start(bf16[128,1024]{1,0:T(8,128)(2,1)S(1)} %get-tuple-element.110), channel_id=1, source_target_pairs={{0,8},{1,9},{2,10},{3,11},{4,12},{5,13},{6,14},{7,15},{8,0},{9,1},... | collective-permute-start | bytes 786440 | tf_op jit(solution)/shard_map/r_z1/ppermute | solution.py:116
  110.5 12.0 %collective-permute-start.30 = (bf16[128,1024]{1,0:T(8,128)(2,1)S(1)}, bf16[128,1024]{1,0:T(8,128)(2,1)S(1)}, u32[]{:S(2)}, u32[]{:S(2)}) collective-permute-start(bf16[128,1024]{1,0:T(8,128)(2,1)S(1)} %get-tuple-element.111), channel_id=1, source_target_pairs={{0,24},{1,25},{2,26},{3,27},{4,28},{5,29},{6,30},{7,31},{8,16},{9,... | collective-permute-start | bytes 786440 | tf_op jit(solution)/shard_map/r_z3/ppermute | solution.py:116
  (23 other events, 135.0 us)

commit v5 on v4

--- a/solution.py
+++ b/solution.py
@@ -549,7 +549,8 @@
     corner_b, right_b = send(corner_b, LEFT, "r_corner1"), send(right_b, LEFT, "r_right1")
     sums, value = stage_add(place, near, base_a, right_a, left_a)
     left_b, value = stage_corner(after(at_block, value), far, left_b, corner_b)
-    more, kept = stage_add(after(at_block, value, sums[2]), far, base_b, right_b, left_b)
+    early = sums[2]
+    more, kept = stage_add(after(at_block, value), far, base_b, right_b, left_b)
     sums.update(more)
     grad_in = last_sum(at_block, sums[0], [sums[d] for d in (2, 1, 3)], BF16)
 
@@ -559,7 +560,7 @@
     term = term + send(after(term, base_b), TO_X, "t_x")
     term = after(term, value)
     term = jnp.stack([term[0], send(term[1], TO_Y, "t_y")], axis=1)
-    term = after(term, kept)
+    term = after(term, kept, early)
     slots = [term[0]] + [send(term[d], TO_Z[d], f"t_z{d}") for d in range(1, NZ)]
     slot_grad = jnp.zeros((experts, tokens), F32)
     ids = jnp.arange(experts, dtype=jnp.int32)

time: 124 us -> 122 us (0.984)
  waiting for transfers between devices: 45.9 us -> 42.2 us
  starting transfers between devices: 39.5 us -> 40.9 us
    ppermute x37, waiting for transfers between devices: 45.9 us -> 42.2 us  [send(): return lax.ppermute(value, BOTH, pairs)]
    ppermute x37, starting transfers between devices: 39.5 us -> 40.9 us  [send(): return lax.ppermute(value, BOTH, pairs)]
  transfers between devices with their start and end apart: 37 -> 37, of which waited for: 20 -> 19; matrix products, arithmetic and copies ran while one was open for 1% -> 1% of each run, Pallas kernels for 23% -> 24%
where the time goes in v5:
time: 122 us; the launch traced here: 121 us
  waiting for transfers between devices  42.2 us (35%)
  starting transfers between devices  40.9 us (34%)
  Pallas kernels  30.3 us (25%)
  local copies, waits for them, and re-layouts  5.92 us (5%)
    ppermute x37, waiting for transfers between devices, send(): return lax.ppermute(value, BOTH, pairs)  42.2 us
    ppermute x37, starting transfers between devices, send(): return lax.ppermute(value, BOTH, pairs)  40.9 us
    pallas_call x11, Pallas kernels, kernel(): pl.pallas_call(body, out_shape=outs, grid_spec=pltpu.PrefetchScalarGridSp...  25.8 us
    unnamed x20, local copies, waits for them, and re-layouts  5.9 us
    pallas_call x2, Pallas kernels, prepare(): pl.pallas_call(body, out_shape=[out] * 3, grid_spec=pltpu.PrefetchScalarG...  2.53 us
  transfers between devices with their start and end apart: 37, of which 19 were waited for; matrix products, arithmetic and copies ran while one was open for 1% of the time, Pallas kernels for 24%

profile of v5, /device:TPU:0, one launch (start us, length us, event | category | flops | bytes accessed | tf_op | source)
XLA Modules:
  0.0 121.0 jit_solution(10135926927167729504)
XLA Ops:
  1.1 2.0 %pack.1 = (bf16[136,1024]{1,0:T(8,128)(2,1)}, f32[8,128]{1,0:T(8,128)}) custom-call(bf16[128,1024]{1,0:T(8,128)(2,1)} %g_ref.1, s32[8,128]{1,0:T(8,128)} %bitcast.46, bf16[8,128]{1,0:T(8,128)(2,1)} %bitcast.47), custom_call_target="tpu_custom_call" | custom-call | tf_op jit(solution)/shard_map/pack/pallas_call | solution.py:177
  3.1 3.6 %collective-permute-start = (bf16[136,1024]{1,0:T(8,128)(2,1)}, bf16[136,1024]{1,0:T(8,128)(2,1)S(1)}, u32[]{:S(2)}, u32[]{:S(2)}) collective-permute-start(bf16[136,1024]{1,0:T(8,128)(2,1)} %get-tuple-element.60.refs_0_), channel_id=1, source_target_pairs={{0,16},{1,17},{2,18},{3,19},{4,20},{5,21},{6,22},{7,23},{8,24},{9,... | collective-permute-start | bytes 835592 | tf_op jit(solution)/shard_map/z2/ppermute | solution.py:116
  6.7 1.6 %collective-permute-start.1 = (bf16[136,1024]{1,0:T(8,128)(2,1)}, bf16[136,1024]{1,0:T(8,128)(2,1)S(1)}, u32[]{:S(2)}, u32[]{:S(2)}) collective-permute-start(bf16[136,1024]{1,0:T(8,128)(2,1)} %get-tuple-element.60.refs_0_), channel_id=1, source_target_pairs={{0,8},{1,9},{2,10},{3,11},{4,12},{5,13},{6,14},{7,15},{8,0},{9,1},... | collective-permute-start | bytes 835592 | tf_op jit(solution)/shard_map/z1/ppermute | solution.py:116
  8.3 1.5 %collective-permute-start.2 = (bf16[136,1024]{1,0:T(8,128)(2,1)}, bf16[136,1024]{1,0:T(8,128)(2,1)S(1)}, u32[]{:S(2)}, u32[]{:S(2)}) collective-permute-start(bf16[136,1024]{1,0:T(8,128)(2,1)} %get-tuple-element.60.refs_0_), channel_id=1, source_target_pairs={{0,4},{1,3},{2,6},{3,1},{4,0},{5,7},{6,2},{7,5},{8,12},{9,11},{10,... | collective-permute-start | bytes 835592 | tf_op jit(solution)/shard_map/first0/ppermute | solution.py:116
  11.3 9.0 %collective-permute-done.refs_3_.refs_4_ = bf16[136,1024]{1,0:T(8,128)(2,1)S(1)} collective-permute-done((bf16[136,1024]{1,0:T(8,128)(2,1)}, bf16[136,1024]{1,0:T(8,128)(2,1)S(1)}, u32[]{:S(2)}, u32[]{:S(2)}) %collective-permute-start) | collective-permute-done | bytes 278560 | tf_op jit(solution)/shard_map/z2/ppermute | solution.py:116
  20.6 1.6 %collective-permute-start.5 = (bf16[136,1024]{1,0:T(8,128)(2,1)S(1)}, bf16[136,1024]{1,0:T(8,128)(2,1)S(1)}, u32[]{:S(2)}, u32[]{:S(2)}) collective-permute-start(bf16[136,1024]{1,0:T(8,128)(2,1)S(1)} %collective-permute-done.refs_3_.refs_4_), channel_id=1, source_target_pairs={{0,8},{1,9},{2,10},{3,11},{4,12},{5,13},{6,14},{7,15},{8,0},{9,1},... | collective-permute-start | bytes 835592 | tf_op jit(solution)/shard_map/z3/ppermute | solution.py:116
  22.1 1.5 %collective-permute-start.6 = (bf16[136,1024]{1,0:T(8,128)(2,1)S(1)}, bf16[136,1024]{1,0:T(8,128)(2,1)S(1)}, u32[]{:S(2)}, u32[]{:S(2)}) collective-permute-start(bf16[136,1024]{1,0:T(8,128)(2,1)S(1)} %collective-permute-done.refs_3_.refs_4_), channel_id=1, source_target_pairs={{0,4},{1,3},{2,6},{3,1},{4,0},{5,7},{6,2},{7,5},{8,12},{9,11},{10,... | collective-permute-start | bytes 835592 | tf_op jit(solution)/shard_map/first2/ppermute | solution.py:116
  23.7 1.5 %collective-permute-start.7 = (bf16[136,1024]{1,0:T(8,128)(2,1)S(1)}, bf16[136,1024]{1,0:T(8,128)(2,1)S(1)}, u32[]{:S(2)}, u32[]{:S(2)}) collective-permute-start(bf16[136,1024]{1,0:T(8,128)(2,1)S(1)} %collective-permute-done.refs_3_.refs_4_), channel_id=1, source_target_pairs={{0,2},{1,5},{2,0},{3,7},{4,6},{5,1},{6,4},{7,3},{8,10},{9,13},{10,... | collective-permute-start | bytes 835592 | tf_op jit(solution)/shard_map/second2/ppermute | solution.py:116
  25.7 4.0 %collective-permute-done.5.refs_3_.refs_4_ = bf16[136,1024]{1,0:T(8,128)(2,1)S(1)} collective-permute-done((bf16[136,1024]{1,0:T(8,128)(2,1)S(1)}, bf16[136,1024]{1,0:T(8,128)(2,1)S(1)}, u32[]{:S(2)}, u32[]{:S(2)}) %collective-permute-start.5) | collective-permute-done | bytes 278560 | tf_op jit(solution)/shard_map/z3/ppermute | solution.py:116
  29.7 1.7 %collective-permute-done.6.refs_4_.refs_5_ = bf16[136,1024]{1,0:T(8,128)(2,1)S(1)} collective-permute-done((bf16[136,1024]{1,0:T(8,128)(2,1)S(1)}, bf16[136,1024]{1,0:T(8,128)(2,1)S(1)}, u32[]{:S(2)}, u32[]{:S(2)}) %collective-permute-start.6) | collective-permute-done | bytes 278560 | tf_op jit(solution)/shard_map/first2/ppermute | solution.py:116
  31.4 2.5 %collective-permute-done.8.refs_3_ = bf16[136,1024]{1,0:T(8,128)(2,1)S(1)} collective-permute-done((bf16[136,1024]{1,0:T(8,128)(2,1)S(1)}, bf16[136,1024]{1,0:T(8,128)(2,1)S(1)}, u32[]{:S(2)}, u32[]{:S(2)}) %collective-permute-start.8) | collective-permute-done | bytes 278560 | tf_op jit(solution)/shard_map/third0/ppermute | solution.py:116
  35.5 1.5 %collective-permute-start.11 = (bf16[136,1024]{1,0:T(8,128)(2,1)S(1)}, bf16[136,1024]{1,0:T(8,128)(2,1)S(1)}, u32[]{:S(2)}, u32[]{:S(2)}) collective-permute-start(bf16[136,1024]{1,0:T(8,128)(2,1)S(1)} %collective-permute-done.1.refs_0_), channel_id=1, source_target_pairs={{0,4},{1,3},{2,6},{3,1},{4,0},{5,7},{6,2},{7,5},{8,12},{9,11},{10,... | collective-permute-start | bytes 835592 | tf_op jit(solution)/shard_map/first1/ppermute | solution.py:116
  43.7 4.7 %hidden.2 = (f32[512,384]{1,0:T(8,128)S(1)}, bf16[512,384]{1,0:T(8,128)(2,1)S(1)}) custom-call(s32[1]{0:T(128)} %bitcast.s_ref, bf16[136,1024]{1,0:T(8,128)(2,1)S(1)} %copy-done.4, bf16[136,1024]{1,0:T(8,128)(2,1)S(1)} %collective-permute-done.2.refs_1_, bf16[136,1024]{1,0:T(8,128)(2,1)S(1)} %collective-permute-done.3.refs_2_, ...), custom_call_target="tpu_custom_call" | custom-call | tf_op jit(solution)/shard_map/hidden/pallas_call | solution.py:136
  49.8 1.6 %collective-permute-done.15.b_ref = bf16[512,384]{1,0:T(8,128)(2,1)S(1)} collective-permute-done((bf16[512,384]{1,0:T(8,128)(2,1)S(1)}, bf16[512,384]{1,0:T(8,128)(2,1)S(1)}, u32[]{:S(2)}, u32[]{:S(2)}) %collective-permute-start.15) | collective-permute-done | bytes 393248 | tf_op jit(solution)/shard_map/swap_bh0/ppermute | solution.py:116
  55.1 6.1 %input.2 = (bf16[256,1024]{1,0:T(8,128)(2,1)S(1)}, bf16[256,1024]{1,0:T(8,128)(2,1)}, bf16[256,1024]{1,0:T(8,128)(2,1)S(1)}, bf16[256,1024]{1,0:T(8,128)(2,1)S(1)}) custom-call(s32[1]{0:T(128)} %bitcast.s_ref, bf16[512,768]{1,0:T(8,128)(2,1)S(1)} %get-tuple-element.82.m_ref, bf16[512,768]{1,0:T(8,128)(2,1)S(1)} %collective-permute-done.16.t_ref, ...), custom_call_target="tpu_custom_call" | custom-call | tf_op jit(solution)/shard_map/input/pallas_call | solution.py:136
  64.6 4.7 %hidden.3 = (f32[512,384]{1,0:T(8,128)S(1)}, bf16[512,384]{1,0:T(8,128)(2,1)S(1)}) custom-call(s32[1]{0:T(128)} %bitcast.s_ref, bf16[136,1024]{1,0:T(8,128)(2,1)S(1)} %collective-permute-done.1.refs_0_, bf16[136,1024]{1,0:T(8,128)(2,1)S(1)} %collective-permute-done.11.refs_1_, bf16[136,1024]{1,0:T(8,128)(2,1)S(1)} %collective-permute-done.12.refs_2_, ...), custom_call_target="tpu_custom_call" | custom-call | tf_op jit(solution)/shard_map/hidden/pallas_call | solution.py:136
  74.2 6.3 %input.3 = (bf16[256,1024]{1,0:T(8,128)(2,1)}, bf16[256,1024]{1,0:T(8,128)(2,1)S(1)}, bf16[256,1024]{1,0:T(8,128)(2,1)S(1)}, bf16[256,1024]{1,0:T(8,128)(2,1)S(1)}) custom-call(s32[1]{0:T(128)} %bitcast.s_ref, bf16[512,768]{1,0:T(8,128)(2,1)S(1)} %get-tuple-element.99.m_ref, bf16[512,768]{1,0:T(8,128)(2,1)S(1)} %collective-permute-done.22.t_ref, ...), custom_call_target="tpu_custom_call" | custom-call | tf_op jit(solution)/shard_map/input/pallas_call | solution.py:136
  90.1 2.3 %collective-permute-start.25 = (bf16[128,1024]{1,0:T(8,128)(2,1)S(1)}, bf16[128,1024]{1,0:T(8,128)(2,1)S(1)}, u32[]{:S(2)}, u32[]{:S(2)}) collective-permute-start(bf16[128,1024]{1,0:T(8,128)(2,1)S(1)} %get-tuple-element.104), channel_id=1, source_target_pairs={{0,16},{1,17},{2,18},{3,19},{4,20},{5,21},{6,22},{7,23},{8,24},{9,... | collective-permute-start | bytes 786440 | tf_op jit(solution)/shard_map/r_z2/ppermute | solution.py:116
  96.0 7.1 %collective-permute-done.33 = f32[4,128]{1,0:T(4,128)S(1)} collective-permute-done((f32[4,128]{1,0:T(4,128)S(1)}, f32[4,128]{1,0:T(4,128)S(1)}, u32[]{:S(2)}, u32[]{:S(2)}) %collective-permute-start.33) | collective-permute-done | bytes 2080 | tf_op jit(solution)/shard_map/t_y/ppermute | solution.py:116
  103.6 1.9 %collective-permute-start.34 = (f32[2,128]{1,0:T(2,128)S(1)}, f32[2,128]{1,0:T(2,128)S(1)}, u32[]{:S(2)}, u32[]{:S(2)}) collective-permute-start(f32[2,128]{1,0:T(2,128)S(1)} %bitcast.51), channel_id=1, source_target_pairs={{0,24},{1,25},{2,26},{3,27},{4,28},{5,29},{6,30},{7,31},{8,16},{9,... | collective-permute-start | bytes 3080 | tf_op jit(solution)/shard_map/t_z3/ppermute | solution.py:116
  106.5 1.5 %collective-permute-start.35 = (f32[2,128]{1,0:T(2,128)S(1)}, f32[2,128]{1,0:T(2,128)S(1)}, u32[]{:S(2)}, u32[]{:S(2)}) collective-permute-start(f32[2,128]{1,0:T(2,128)S(1)} %bitcast.50), channel_id=1, source_target_pairs={{0,16},{1,17},{2,18},{3,19},{4,20},{5,21},{6,22},{7,23},{8,24},{9,... | collective-permute-start | bytes 3080 | tf_op jit(solution)/shard_map/t_z2/ppermute | solution.py:116
  108.0 2.8 %collective-permute-start.30 = (bf16[128,1024]{1,0:T(8,128)(2,1)S(1)}, bf16[128,1024]{1,0:T(8,128)(2,1)S(1)}, u32[]{:S(2)}, u32[]{:S(2)}) collective-permute-start(bf16[128,1024]{1,0:T(8,128)(2,1)S(1)} %get-tuple-element.111), channel_id=1, source_target_pairs={{0,24},{1,25},{2,26},{3,27},{4,28},{5,29},{6,30},{7,31},{8,16},{9,... | collective-permute-start | bytes 786440 | tf_op jit(solution)/shard_map/r_z3/ppermute | solution.py:116
  110.9 2.2 %collective-permute-done.35 = f32[2,128]{1,0:T(2,128)S(1)} collective-permute-done((f32[2,128]{1,0:T(2,128)S(1)}, f32[2,128]{1,0:T(2,128)S(1)}, u32[]{:S(2)}, u32[]{:S(2)}) %collective-permute-start.35) | collective-permute-done | bytes 1056 | tf_op jit(solution)/shard_map/t_z2/ppermute | solution.py:116
  114.7 5.5 %collective-permute-done.30.refs_2_ = bf16[128,1024]{1,0:T(8,128)(2,1)S(1)} collective-permute-done((bf16[128,1024]{1,0:T(8,128)(2,1)S(1)}, bf16[128,1024]{1,0:T(8,128)(2,1)S(1)}, u32[]{:S(2)}, u32[]{:S(2)}) %collective-permute-start.30) | collective-permute-done | bytes 262176 | tf_op jit(solution)/shard_map/r_z3/ppermute | solution.py:116
  (102 shorter events, 41.5 us)
Async XLA Ops:
  0.6 19.9 %collective-permute-start.4 = (bf16[384,4096]{1,0:T(8,128)(2,1)}, bf16[384,4096]{1,0:T(8,128)(2,1)}, u32[]{:S(2)}, u32[]{:S(2)}) collective-permute-start(bf16[384,4096]{1,0:T(8,128)(2,1)} %bitcast.37), channel_id=1, source_target_pairs={{0,1},{1,0},{2,3},{3,2},{4,5},{5,4},{6,7},{7,6},{8,9},{9,8},{10,11... | collective-permute-start | bytes 9437192 | tf_op jit(solution)/shard_map/weights/ppermute | solution.py:116
  3.1 17.2 %collective-permute-start = (bf16[136,1024]{1,0:T(8,128)(2,1)}, bf16[136,1024]{1,0:T(8,128)(2,1)S(1)}, u32[]{:S(2)}, u32[]{:S(2)}) collective-permute-start(bf16[136,1024]{1,0:T(8,128)(2,1)} %get-tuple-element.60.refs_0_), channel_id=1, source_target_pairs={{0,16},{1,17},{2,18},{3,19},{4,20},{5,21},{6,22},{7,23},{8,24},{9,... | collective-permute-start | bytes 835592 | tf_op jit(solution)/shard_map/z2/ppermute | solution.py:116
  6.7 13.8 %collective-permute-start.1 = (bf16[136,1024]{1,0:T(8,128)(2,1)}, bf16[136,1024]{1,0:T(8,128)(2,1)S(1)}, u32[]{:S(2)}, u32[]{:S(2)}) collective-permute-start(bf16[136,1024]{1,0:T(8,128)(2,1)} %get-tuple-element.60.refs_0_), channel_id=1, source_target_pairs={{0,8},{1,9},{2,10},{3,11},{4,12},{5,13},{6,14},{7,15},{8,0},{9,1},... | collective-permute-start | bytes 835592 | tf_op jit(solution)/shard_map/z1/ppermute | solution.py:116
  8.3 12.2 %collective-permute-start.2 = (bf16[136,1024]{1,0:T(8,128)(2,1)}, bf16[136,1024]{1,0:T(8,128)(2,1)S(1)}, u32[]{:S(2)}, u32[]{:S(2)}) collective-permute-start(bf16[136,1024]{1,0:T(8,128)(2,1)} %get-tuple-element.60.refs_0_), channel_id=1, source_target_pairs={{0,4},{1,3},{2,6},{3,1},{4,0},{5,7},{6,2},{7,5},{8,12},{9,11},{10,... | collective-permute-start | bytes 835592 | tf_op jit(solution)/shard_map/first0/ppermute | solution.py:116
  9.8 10.7 %collective-permute-start.3 = (bf16[136,1024]{1,0:T(8,128)(2,1)}, bf16[136,1024]{1,0:T(8,128)(2,1)S(1)}, u32[]{:S(2)}, u32[]{:S(2)}) collective-permute-start(bf16[136,1024]{1,0:T(8,128)(2,1)} %get-tuple-element.60.refs_0_), channel_id=1, source_target_pairs={{0,2},{1,5},{2,0},{3,7},{4,6},{5,1},{6,4},{7,3},{8,10},{9,13},{10,... | collective-permute-start | bytes 835592 | tf_op jit(solution)/shard_map/second0/ppermute | solution.py:116
  20.5 13.4 %collective-permute-start.9 = (bf16[4096,384]{1,0:T(8,128)(2,1)}, bf16[4096,384]{1,0:T(8,128)(2,1)S(1)}, u32[]{:S(2)}, u32[]{:S(2)}) collective-permute-start(bf16[4096,384]{1,0:T(8,128)(2,1)} %bitcast.40), channel_id=1, source_target_pairs={{0,1},{1,0},{2,3},{3,2},{4,5},{5,4},{6,7},{7,6},{8,9},{9,8},{10,11... | collective-permute-start | bytes 9437192 | tf_op jit(solution)/shard_map/weights/ppermute | solution.py:116
  22.1 9.2 %collective-permute-start.6 = (bf16[136,1024]{1,0:T(8,128)(2,1)S(1)}, bf16[136,1024]{1,0:T(8,128)(2,1)S(1)}, u32[]{:S(2)}, u32[]{:S(2)}) collective-permute-start(bf16[136,1024]{1,0:T(8,128)(2,1)S(1)} %collective-permute-done.refs_3_.refs_4_), channel_id=1, source_target_pairs={{0,4},{1,3},{2,6},{3,1},{4,0},{5,7},{6,2},{7,5},{8,12},{9,11},{10,... | collective-permute-start | bytes 835592 | tf_op jit(solution)/shard_map/first2/ppermute | solution.py:116
  33.9 15.8 %collective-permute-start.13 = (bf16[4096,384]{1,0:T(8,128)(2,1)}, bf16[4096,384]{1,0:T(8,128)(2,1)}, u32[]{:S(2)}, u32[]{:S(2)}) collective-permute-start(bf16[4096,384]{1,0:T(8,128)(2,1)} %bitcast.43), channel_id=1, source_target_pairs={{0,1},{1,0},{2,3},{3,2},{4,5},{5,4},{6,7},{7,6},{8,9},{9,8},{10,11... | collective-permute-start | bytes 9437192 | tf_op jit(solution)/shard_map/weights/ppermute | solution.py:116
  35.5 12.9 %collective-permute-start.11 = (bf16[136,1024]{1,0:T(8,128)(2,1)S(1)}, bf16[136,1024]{1,0:T(8,128)(2,1)S(1)}, u32[]{:S(2)}, u32[]{:S(2)}) collective-permute-start(bf16[136,1024]{1,0:T(8,128)(2,1)S(1)} %collective-permute-done.1.refs_0_), channel_id=1, source_target_pairs={{0,4},{1,3},{2,6},{3,1},{4,0},{5,7},{6,2},{7,5},{8,12},{9,11},{10,... | collective-permute-start | bytes 835592 | tf_op jit(solution)/shard_map/first1/ppermute | solution.py:116
  37.0 12.7 %collective-permute-start.12 = (bf16[136,1024]{1,0:T(8,128)(2,1)S(1)}, bf16[136,1024]{1,0:T(8,128)(2,1)S(1)}, u32[]{:S(2)}, u32[]{:S(2)}) collective-permute-start(bf16[136,1024]{1,0:T(8,128)(2,1)S(1)} %collective-permute-done.1.refs_0_), channel_id=1, source_target_pairs={{0,2},{1,5},{2,0},{3,7},{4,6},{5,1},{6,4},{7,3},{8,10},{9,13},{10,... | collective-permute-start | bytes 835592 | tf_op jit(solution)/shard_map/second1/ppermute | solution.py:116
  38.0 11.6 %collective-permute-start.14 = (bf16[136,1024]{1,0:T(8,128)(2,1)S(1)}, bf16[136,1024]{1,0:T(8,128)(2,1)S(1)}, u32[]{:S(2)}, u32[]{:S(2)}) collective-permute-start(bf16[136,1024]{1,0:T(8,128)(2,1)S(1)} %collective-permute-done.5.refs_3_.refs_4_), channel_id=1, source_target_pairs={{0,4},{1,3},{2,6},{3,1},{4,0},{5,7},{6,2},{7,5},{8,12},{9,11},{10,... | collective-permute-start | bytes 835592 | tf_op jit(solution)/shard_map/first3/ppermute | solution.py:116
  52.1 10.3 %collective-permute-start.17 = (bf16[136,1024]{1,0:T(8,128)(2,1)S(1)}, bf16[136,1024]{1,0:T(8,128)(2,1)S(1)}, u32[]{:S(2)}, u32[]{:S(2)}) collective-permute-start(bf16[136,1024]{1,0:T(8,128)(2,1)S(1)} %collective-permute-done.5.refs_3_.refs_4_), channel_id=1, source_target_pairs={{0,2},{1,5},{2,0},{3,7},{4,6},{5,1},{6,4},{7,3},{8,10},{9,13},{10,... | collective-permute-start | bytes 835592 | tf_op jit(solution)/shard_map/second3/ppermute | solution.py:116
  53.0 10.6 %collective-permute-start.18 = (bf16[136,1024]{1,0:T(8,128)(2,1)S(1)}, bf16[136,1024]{1,0:T(8,128)(2,1)S(1)}, u32[]{:S(2)}, u32[]{:S(2)}) collective-permute-start(bf16[136,1024]{1,0:T(8,128)(2,1)S(1)} %collective-permute-done.11.refs_1_), channel_id=1, source_target_pairs={{0,2},{1,5},{2,0},{3,7},{4,6},{5,1},{6,4},{7,3},{8,10},{9,13},{10,... | collective-permute-start | bytes 835592 | tf_op jit(solution)/shard_map/third1/ppermute | solution.py:116
  54.1 10.5 %collective-permute-start.19 = (bf16[136,1024]{1,0:T(8,128)(2,1)S(1)}, bf16[136,1024]{1,0:T(8,128)(2,1)S(1)}, u32[]{:S(2)}, u32[]{:S(2)}) collective-permute-start(bf16[136,1024]{1,0:T(8,128)(2,1)S(1)} %collective-permute-done.14.refs_4_.refs_5_), channel_id=1, source_target_pairs={{0,2},{1,5},{2,0},{3,7},{4,6},{5,1},{6,4},{7,3},{8,10},{9,13},{10,... | collective-permute-start | bytes 835592 | tf_op jit(solution)/shard_map/third3/ppermute | solution.py:116
  61.2 9.2 %collective-permute-start.20 = (bf16[256,1024]{1,0:T(8,128)(2,1)S(1)}, bf16[256,1024]{1,0:T(8,128)(2,1)S(1)}, u32[]{:S(2)}, u32[]{:S(2)}) collective-permute-start(bf16[256,1024]{1,0:T(8,128)(2,1)S(1)} %get-tuple-element.94), channel_id=1, source_target_pairs={{0,2},{1,5},{2,0},{3,7},{4,6},{5,1},{6,4},{7,3},{8,10},{9,13},{10,... | collective-permute-start | bytes 1572872 | tf_op jit(solution)/shard_map/r_corner0/ppermute | solution.py:116
  71.7 15.1 %collective-permute-start.23 = (bf16[256,1024]{1,0:T(8,128)(2,1)}, bf16[256,1024]{1,0:T(8,128)(2,1)}, u32[]{:S(2)}, u32[]{:S(2)}) collective-permute-start(bf16[256,1024]{1,0:T(8,128)(2,1)} %get-tuple-element.102), channel_id=1, source_target_pairs={{0,2},{1,5},{2,0},{3,7},{4,6},{5,1},{6,4},{7,3},{8,10},{9,13},{10,... | collective-permute-start | bytes 1572872 | tf_op jit(solution)/shard_map/r_right0/ppermute | solution.py:116
  72.8 14.9 %collective-permute-start.24 = (bf16[256,1024]{1,0:T(8,128)(2,1)S(1)}, bf16[256,1024]{1,0:T(8,128)(2,1)}, u32[]{:S(2)}, u32[]{:S(2)}) collective-permute-start(bf16[256,1024]{1,0:T(8,128)(2,1)S(1)} %corner.2), channel_id=1, source_target_pairs={{0,4},{1,3},{2,6},{3,1},{4,0},{5,7},{6,2},{7,5},{8,12},{9,11},{10,... | collective-permute-start | bytes 1572872 | tf_op jit(solution)/shard_map/r_left0/ppermute | solution.py:116
  82.2 10.2 %collective-permute-start.26 = (bf16[256,1024]{1,0:T(8,128)(2,1)}, bf16[256,1024]{1,0:T(8,128)(2,1)S(1)}, u32[]{:S(2)}, u32[]{:S(2)}) collective-permute-start(bf16[256,1024]{1,0:T(8,128)(2,1)} %get-tuple-element.107), channel_id=1, source_target_pairs={{0,2},{1,5},{2,0},{3,7},{4,6},{5,1},{6,4},{7,3},{8,10},{9,13},{10,... | collective-permute-start | bytes 1572872 | tf_op jit(solution)/shard_map/r_corner1/ppermute | solution.py:116
  84.2 10.8 %collective-permute-start.32 = (f32[2,4,128]{2,1,0:T(4,128)S(1)}, f32[2,4,128]{2,1,0:T(4,128)S(1)}, u32[]{:S(2)}, u32[]{:S(2)}) collective-permute-start(f32[2,4,128]{2,1,0:T(4,128)S(1)} %fusion), channel_id=1, source_target_pairs={{0,2},{1,3},{2,0},{3,1},{4,6},{5,7},{6,4},{7,5},{8,10},{9,11},{10,... | collective-permute-start | bytes 12296 | tf_op jit(solution)/shard_map/t_x/ppermute | solution.py:116
  89.0 14.1 %collective-permute-start.27 = (bf16[256,1024]{1,0:T(8,128)(2,1)}, bf16[256,1024]{1,0:T(8,128)(2,1)S(1)}, u32[]{:S(2)}, u32[]{:S(2)}) collective-permute-start(bf16[256,1024]{1,0:T(8,128)(2,1)} %copy-done.7), channel_id=1, source_target_pairs={{0,2},{1,5},{2,0},{3,7},{4,6},{5,1},{6,4},{7,3},{8,10},{9,13},{10,... | collective-permute-start | bytes 1572872 | tf_op jit(solution)/shard_map/r_right1/ppermute | solution.py:116
  90.1 13.5 %collective-permute-start.25 = (bf16[128,1024]{1,0:T(8,128)(2,1)S(1)}, bf16[128,1024]{1,0:T(8,128)(2,1)S(1)}, u32[]{:S(2)}, u32[]{:S(2)}) collective-permute-start(bf16[128,1024]{1,0:T(8,128)(2,1)S(1)} %get-tuple-element.104), channel_id=1, source_target_pairs={{0,16},{1,17},{2,18},{3,19},{4,20},{5,21},{6,22},{7,23},{8,24},{9,... | collective-permute-start | bytes 786440 | tf_op jit(solution)/shard_map/r_z2/ppermute | solution.py:116
  93.8 9.3 %collective-permute-start.28 = (bf16[256,1024]{1,0:T(8,128)(2,1)S(1)}, bf16[256,1024]{1,0:T(8,128)(2,1)S(1)}, u32[]{:S(2)}, u32[]{:S(2)}) collective-permute-start(bf16[256,1024]{1,0:T(8,128)(2,1)S(1)} %corner.3), channel_id=1, source_target_pairs={{0,4},{1,3},{2,6},{3,1},{4,0},{5,7},{6,2},{7,5},{8,12},{9,11},{10,... | collective-permute-start | bytes 1572872 | tf_op jit(solution)/shard_map/r_left1/ppermute | solution.py:116
  105.4 9.3 %collective-permute-start.29 = (bf16[128,1024]{1,0:T(8,128)(2,1)S(1)}, bf16[128,1024]{1,0:T(8,128)(2,1)S(1)}, u32[]{:S(2)}, u32[]{:S(2)}) collective-permute-start(bf16[128,1024]{1,0:T(8,128)(2,1)S(1)} %get-tuple-element.110), channel_id=1, source_target_pairs={{0,8},{1,9},{2,10},{3,11},{4,12},{5,13},{6,14},{7,15},{8,0},{9,1},... | collective-permute-start | bytes 786440 | tf_op jit(solution)/shard_map/r_z1/ppermute | solution.py:116
  108.0 12.1 %collective-permute-start.30 = (bf16[128,1024]{1,0:T(8,128)(2,1)S(1)}, bf16[128,1024]{1,0:T(8,128)(2,1)S(1)}, u32[]{:S(2)}, u32[]{:S(2)}) collective-permute-start(bf16[128,1024]{1,0:T(8,128)(2,1)S(1)} %get-tuple-element.111), channel_id=1, source_target_pairs={{0,24},{1,25},{2,26},{3,27},{4,28},{5,29},{6,30},{7,31},{8,16},{9,... | collective-permute-start | bytes 786440 | tf_op jit(solution)/shard_map/r_z3/ppermute | solution.py:116
  (23 other events, 135.3 us)

commit v6 on v5

--- a/solution.py
+++ b/solution.py
@@ -242,50 +242,52 @@
     count = len(pieces)
     half = count * tokens
     rows = NY * half
+    steps = 2
+    wide = quarter // steps
 
     def body(s_ref, *refs):
         near = refs[: 4 * count]
         d_ref, o_ref, mine, theirs, rows_v, w_v, row_sem, w_sem = refs[4 * count :]
         x, c = s_ref[0] // NC, s_ref[0] % NC
 
-        def columns(q):
-            return pl.ds(pl.multiple_of(q * quarter, quarter), quarter)
-
-        def weight(dx, k):
-            source = (d_ref, o_ref)[k].at[:, columns(2 * (x ^ dx) + c)]
-            return pltpu.make_async_copy(source, w_v.at[dx, pl.ds(k * hid, hid), :], w_sem.at[dx, k])
-
-        def piece(i, j, dx, dy):
-            target = rows_v.at[dx, pl.ds(dy * half + i * tokens, tokens), :]
-            source = near[4 * i + j].at[pl.ds(0, tokens), :]
-            return pltpu.make_async_copy(source, target, row_sem.at[i, dx, dy])
-
-        def begin(dx):
+        def weight(dx, h, k):
+            first = pl.multiple_of((2 * (x ^ dx) + c) * quarter + h * wide, wide)
+            source = (d_ref, o_ref)[k].at[:, pl.ds(first, wide)]
+            return pltpu.make_async_copy(source, w_v.at[dx, h, pl.ds(k * hid, hid), :], w_sem.at[dx, h, k])
+
+        def piece(i, j, dx, h, dy):
+            target = rows_v.at[dx, h, pl.ds(dy * half + i * tokens, tokens), :]
+            source = near[4 * i + j].at[pl.ds(0, tokens), pl.ds(h * wide, wide)]
+            return pltpu.make_async_copy(source, target, row_sem.at[i, dx, h, dy])
+
+        def begin(dx, h):
             for k in (1, 0):
-                weight(dx, k).start()
+                weight(dx, h, k).start()
             for i in range(count):
-                piece(i, 0 if dx == 0 else 3, dx, dx).start()
+                piece(i, 0 if dx == 0 else 3, dx, h, dx).start()
 
                 @pl.when(c == dx)
-                def _(i=i, dx=dx):
-                    piece(i, 1, dx, 1 - dx).start()
+                def _(i=i, dx=dx, h=h):
+                    piece(i, 1, dx, h, 1 - dx).start()
 
                 @pl.when(c != dx)
-                def _(i=i, dx=dx):
-                    piece(i, 2, dx, 1 - dx).start()
-
+                def _(i=i, dx=dx, h=h):
+                    piece(i, 2, dx, h, 1 - dx).start()
+
+        order = [(dx, h) for dx in range(NX) for h in range(steps)]
+        begin(*order[0])
+        begin(*order[1])
         total = None
-        begin(0)
-        for dx in range(NX):
+        for n, (dx, h) in enumerate(order):
             for i in range(count):
                 for dy in range(NY):
-                    piece(i, 0, dx, dy).wait()
+                    piece(i, 0, dx, h, dy).wait()
             for k in (1, 0):
-                weight(dx, k).wait()
-            if dx + 1 < NX:
-                begin(dx + 1)
-            part = dot_nt(rows_v[dx], w_v[dx])
-            total = part if dx == 0 else total + part
+                weight(dx, h, k).wait()
+            if n + 2 < len(order):
+                begin(*order[n + 2])
+            part = dot_nt(rows_v[dx, h], w_v[dx, h])
+            total = part if n == 0 else total + part
         mine[...] = total[:, :hid]
         theirs[...] = total[:, hid:].astype(BF16)
 
@@ -303,10 +305,10 @@
         down,
         got,
         scratch=[
-            pltpu.VMEM((NX, rows, quarter), BF16),
-            pltpu.VMEM((NX, 2 * hid, quarter), BF16),
-            pltpu.SemaphoreType.DMA((count, NX, NY)),
-            pltpu.SemaphoreType.DMA((NX, 2)),
+            pltpu.VMEM((NX, steps, rows, wide), BF16),
+            pltpu.VMEM((NX, steps, 2 * hid, wide), BF16),
+            pltpu.SemaphoreType.DMA((count, NX, steps, NY)),
+            pltpu.SemaphoreType.DMA((NX, steps, 2)),
         ],
     )
 

time: 122 us -> 121 us (level)
  transfers between devices with their start and end apart: 37 -> 37, of which waited for: 19 -> 17; matrix products, arithmetic and copies ran while one was open for 1% -> 1% of each run, Pallas kernels for 24% -> 23%
where the time goes in v6:
time: 121 us
  waiting for transfers between devices  43.2 us (36%)
  starting transfers between devices  40.6 us (34%)
  Pallas kernels  29.3 us (24%)
  local copies, waits for them, and re-layouts  5.93 us (5%)
    ppermute x37, waiting for transfers between devices, send(): return lax.ppermute(value, BOTH, pairs)  43.2 us
    ppermute x37, starting transfers between devices, send(): return lax.ppermute(value, BOTH, pairs)  40.6 us
    pallas_call x11, Pallas kernels, kernel(): pl.pallas_call(body, out_shape=outs, grid_spec=pltpu.PrefetchScalarGridSp...  24.8 us
    unnamed x20, local copies, waits for them, and re-layouts  5.9 us
    pallas_call x2, Pallas kernels, prepare(): pl.pallas_call(body, out_shape=[out] * 3, grid_spec=pltpu.PrefetchScalarG...  2.53 us
  transfers between devices with their start and end apart: 37, of which 17 were waited for; matrix products, arithmetic and copies ran while one was open for 1% of the time, Pallas kernels for 23%

profile of v6, /device:TPU:0, one launch (start us, length us, event | category | flops | bytes accessed | tf_op | source)
XLA Modules:
  0.0 120.8 jit_solution(1964415540096344195)
XLA Ops:
  1.1 2.0 %pack.1 = (bf16[136,1024]{1,0:T(8,128)(2,1)}, f32[8,128]{1,0:T(8,128)}) custom-call(bf16[128,1024]{1,0:T(8,128)(2,1)} %g_ref.1, s32[8,128]{1,0:T(8,128)} %bitcast.46, bf16[8,128]{1,0:T(8,128)(2,1)} %bitcast.47), custom_call_target="tpu_custom_call" | custom-call | tf_op jit(solution)/shard_map/pack/pallas_call | solution.py:177
  3.1 3.6 %collective-permute-start = (bf16[136,1024]{1,0:T(8,128)(2,1)}, bf16[136,1024]{1,0:T(8,128)(2,1)S(1)}, u32[]{:S(2)}, u32[]{:S(2)}) collective-permute-start(bf16[136,1024]{1,0:T(8,128)(2,1)} %get-tuple-element.60.refs_0_), channel_id=1, source_target_pairs={{0,16},{1,17},{2,18},{3,19},{4,20},{5,21},{6,22},{7,23},{8,24},{9,... | collective-permute-start | bytes 835592 | tf_op jit(solution)/shard_map/z2/ppermute | solution.py:116
  6.7 1.6 %collective-permute-start.1 = (bf16[136,1024]{1,0:T(8,128)(2,1)}, bf16[136,1024]{1,0:T(8,128)(2,1)S(1)}, u32[]{:S(2)}, u32[]{:S(2)}) collective-permute-start(bf16[136,1024]{1,0:T(8,128)(2,1)} %get-tuple-element.60.refs_0_), channel_id=1, source_target_pairs={{0,8},{1,9},{2,10},{3,11},{4,12},{5,13},{6,14},{7,15},{8,0},{9,1},... | collective-permute-start | bytes 835592 | tf_op jit(solution)/shard_map/z1/ppermute | solution.py:116
  8.3 1.5 %collective-permute-start.2 = (bf16[136,1024]{1,0:T(8,128)(2,1)}, bf16[136,1024]{1,0:T(8,128)(2,1)S(1)}, u32[]{:S(2)}, u32[]{:S(2)}) collective-permute-start(bf16[136,1024]{1,0:T(8,128)(2,1)} %get-tuple-element.60.refs_0_), channel_id=1, source_target_pairs={{0,4},{1,3},{2,6},{3,1},{4,0},{5,7},{6,2},{7,5},{8,12},{9,11},{10,... | collective-permute-start | bytes 835592 | tf_op jit(solution)/shard_map/first0/ppermute | solution.py:116
  11.3 9.0 %collective-permute-done.refs_3_.refs_4_ = bf16[136,1024]{1,0:T(8,128)(2,1)S(1)} collective-permute-done((bf16[136,1024]{1,0:T(8,128)(2,1)}, bf16[136,1024]{1,0:T(8,128)(2,1)S(1)}, u32[]{:S(2)}, u32[]{:S(2)}) %collective-permute-start) | collective-permute-done | bytes 278560 | tf_op jit(solution)/shard_map/z2/ppermute | solution.py:116
  20.6 1.6 %collective-permute-start.5 = (bf16[136,1024]{1,0:T(8,128)(2,1)S(1)}, bf16[136,1024]{1,0:T(8,128)(2,1)S(1)}, u32[]{:S(2)}, u32[]{:S(2)}) collective-permute-start(bf16[136,1024]{1,0:T(8,128)(2,1)S(1)} %collective-permute-done.refs_3_.refs_4_), channel_id=1, source_target_pairs={{0,8},{1,9},{2,10},{3,11},{4,12},{5,13},{6,14},{7,15},{8,0},{9,1},... | collective-permute-start | bytes 835592 | tf_op jit(solution)/shard_map/z3/ppermute | solution.py:116
  22.1 1.5 %collective-permute-start.6 = (bf16[136,1024]{1,0:T(8,128)(2,1)S(1)}, bf16[136,1024]{1,0:T(8,128)(2,1)S(1)}, u32[]{:S(2)}, u32[]{:S(2)}) collective-permute-start(bf16[136,1024]{1,0:T(8,128)(2,1)S(1)} %collective-permute-done.refs_3_.refs_4_), channel_id=1, source_target_pairs={{0,4},{1,3},{2,6},{3,1},{4,0},{5,7},{6,2},{7,5},{8,12},{9,11},{10,... | collective-permute-start | bytes 835592 | tf_op jit(solution)/shard_map/first2/ppermute | solution.py:116
  25.7 4.0 %collective-permute-done.5.refs_3_.refs_4_ = bf16[136,1024]{1,0:T(8,128)(2,1)S(1)} collective-permute-done((bf16[136,1024]{1,0:T(8,128)(2,1)S(1)}, bf16[136,1024]{1,0:T(8,128)(2,1)S(1)}, u32[]{:S(2)}, u32[]{:S(2)}) %collective-permute-start.5) | collective-permute-done | bytes 278560 | tf_op jit(solution)/shard_map/z3/ppermute | solution.py:116
  29.7 1.7 %collective-permute-done.6.refs_4_.refs_5_ = bf16[136,1024]{1,0:T(8,128)(2,1)S(1)} collective-permute-done((bf16[136,1024]{1,0:T(8,128)(2,1)S(1)}, bf16[136,1024]{1,0:T(8,128)(2,1)S(1)}, u32[]{:S(2)}, u32[]{:S(2)}) %collective-permute-start.6) | collective-permute-done | bytes 278560 | tf_op jit(solution)/shard_map/first2/ppermute | solution.py:116
  31.4 2.5 %collective-permute-done.8.refs_3_ = bf16[136,1024]{1,0:T(8,128)(2,1)S(1)} collective-permute-done((bf16[136,1024]{1,0:T(8,128)(2,1)S(1)}, bf16[136,1024]{1,0:T(8,128)(2,1)S(1)}, u32[]{:S(2)}, u32[]{:S(2)}) %collective-permute-start.8) | collective-permute-done | bytes 278560 | tf_op jit(solution)/shard_map/third0/ppermute | solution.py:116
  35.5 1.5 %collective-permute-start.11 = (bf16[136,1024]{1,0:T(8,128)(2,1)S(1)}, bf16[136,1024]{1,0:T(8,128)(2,1)S(1)}, u32[]{:S(2)}, u32[]{:S(2)}) collective-permute-start(bf16[136,1024]{1,0:T(8,128)(2,1)S(1)} %collective-permute-done.1.refs_0_), channel_id=1, source_target_pairs={{0,4},{1,3},{2,6},{3,1},{4,0},{5,7},{6,2},{7,5},{8,12},{9,11},{10,... | collective-permute-start | bytes 835592 | tf_op jit(solution)/shard_map/first1/ppermute | solution.py:116
  43.7 4.2 %hidden.2 = (f32[512,384]{1,0:T(8,128)S(1)}, bf16[512,384]{1,0:T(8,128)(2,1)S(1)}) custom-call(s32[1]{0:T(128)} %bitcast.s_ref, bf16[136,1024]{1,0:T(8,128)(2,1)S(1)} %copy-done.4, bf16[136,1024]{1,0:T(8,128)(2,1)S(1)} %collective-permute-done.2.refs_1_, bf16[136,1024]{1,0:T(8,128)(2,1)S(1)} %collective-permute-done.3.refs_2_, ...), custom_call_target="tpu_custom_call" | custom-call | tf_op jit(solution)/shard_map/hidden/pallas_call | solution.py:136
  47.9 1.8 %collective-permute-done.12.refs_2_ = bf16[136,1024]{1,0:T(8,128)(2,1)S(1)} collective-permute-done((bf16[136,1024]{1,0:T(8,128)(2,1)S(1)}, bf16[136,1024]{1,0:T(8,128)(2,1)S(1)}, u32[]{:S(2)}, u32[]{:S(2)}) %collective-permute-start.12) | collective-permute-done | bytes 278560 | tf_op jit(solution)/shard_map/second1/ppermute | solution.py:116
  49.8 1.6 %collective-permute-done.15.b_ref = bf16[512,384]{1,0:T(8,128)(2,1)S(1)} collective-permute-done((bf16[512,384]{1,0:T(8,128)(2,1)S(1)}, bf16[512,384]{1,0:T(8,128)(2,1)S(1)}, u32[]{:S(2)}, u32[]{:S(2)}) %collective-permute-start.15) | collective-permute-done | bytes 393248 | tf_op jit(solution)/shard_map/swap_bh0/ppermute | solution.py:116
  55.1 6.1 %input.2 = (bf16[256,1024]{1,0:T(8,128)(2,1)S(1)}, bf16[256,1024]{1,0:T(8,128)(2,1)}, bf16[256,1024]{1,0:T(8,128)(2,1)S(1)}, bf16[256,1024]{1,0:T(8,128)(2,1)S(1)}) custom-call(s32[1]{0:T(128)} %bitcast.s_ref, bf16[512,768]{1,0:T(8,128)(2,1)S(1)} %get-tuple-element.82.m_ref, bf16[512,768]{1,0:T(8,128)(2,1)S(1)} %collective-permute-done.16.t_ref, ...), custom_call_target="tpu_custom_call" | custom-call | tf_op jit(solution)/shard_map/input/pallas_call | solution.py:136
  64.6 4.2 %hidden.3 = (f32[512,384]{1,0:T(8,128)S(1)}, bf16[512,384]{1,0:T(8,128)(2,1)S(1)}) custom-call(s32[1]{0:T(128)} %bitcast.s_ref, bf16[136,1024]{1,0:T(8,128)(2,1)S(1)} %collective-permute-done.1.refs_0_, bf16[136,1024]{1,0:T(8,128)(2,1)S(1)} %collective-permute-done.11.refs_1_, bf16[136,1024]{1,0:T(8,128)(2,1)S(1)} %collective-permute-done.12.refs_2_, ...), custom_call_target="tpu_custom_call" | custom-call | tf_op jit(solution)/shard_map/hidden/pallas_call | solution.py:136
  68.9 1.6 %collective-permute-done.20.c_ref = bf16[256,1024]{1,0:T(8,128)(2,1)S(1)} collective-permute-done((bf16[256,1024]{1,0:T(8,128)(2,1)S(1)}, bf16[256,1024]{1,0:T(8,128)(2,1)S(1)}, u32[]{:S(2)}, u32[]{:S(2)}) %collective-permute-start.20) | collective-permute-done | bytes 524320 | tf_op jit(solution)/shard_map/r_corner0/ppermute | solution.py:116
  73.8 6.3 %input.3 = (bf16[256,1024]{1,0:T(8,128)(2,1)}, bf16[256,1024]{1,0:T(8,128)(2,1)S(1)}, bf16[256,1024]{1,0:T(8,128)(2,1)S(1)}, bf16[256,1024]{1,0:T(8,128)(2,1)S(1)}) custom-call(s32[1]{0:T(128)} %bitcast.s_ref, bf16[512,768]{1,0:T(8,128)(2,1)S(1)} %get-tuple-element.99.m_ref, bf16[512,768]{1,0:T(8,128)(2,1)S(1)} %collective-permute-done.22.t_ref, ...), custom_call_target="tpu_custom_call" | custom-call | tf_op jit(solution)/shard_map/input/pallas_call | solution.py:136
  89.8 2.3 %collective-permute-start.25 = (bf16[128,1024]{1,0:T(8,128)(2,1)S(1)}, bf16[128,1024]{1,0:T(8,128)(2,1)S(1)}, u32[]{:S(2)}, u32[]{:S(2)}) collective-permute-start(bf16[128,1024]{1,0:T(8,128)(2,1)S(1)} %get-tuple-element.104), channel_id=1, source_target_pairs={{0,16},{1,17},{2,18},{3,19},{4,20},{5,21},{6,22},{7,23},{8,24},{9,... | collective-permute-start | bytes 786440 | tf_op jit(solution)/shard_map/r_z2/ppermute | solution.py:116
  95.7 7.1 %collective-permute-done.33 = f32[4,128]{1,0:T(4,128)S(1)} collective-permute-done((f32[4,128]{1,0:T(4,128)S(1)}, f32[4,128]{1,0:T(4,128)S(1)}, u32[]{:S(2)}, u32[]{:S(2)}) %collective-permute-start.33) | collective-permute-done | bytes 2080 | tf_op jit(solution)/shard_map/t_y/ppermute | solution.py:116
  103.3 2.1 %collective-permute-start.34 = (f32[2,128]{1,0:T(2,128)S(1)}, f32[2,128]{1,0:T(2,128)S(1)}, u32[]{:S(2)}, u32[]{:S(2)}) collective-permute-start(f32[2,128]{1,0:T(2,128)S(1)} %bitcast.51), channel_id=1, source_target_pairs={{0,24},{1,25},{2,26},{3,27},{4,28},{5,29},{6,30},{7,31},{8,16},{9,... | collective-permute-start | bytes 3080 | tf_op jit(solution)/shard_map/t_z3/ppermute | solution.py:116
  107.7 2.8 %collective-permute-start.30 = (bf16[128,1024]{1,0:T(8,128)(2,1)S(1)}, bf16[128,1024]{1,0:T(8,128)(2,1)S(1)}, u32[]{:S(2)}, u32[]{:S(2)}) collective-permute-start(bf16[128,1024]{1,0:T(8,128)(2,1)S(1)} %get-tuple-element.111), channel_id=1, source_target_pairs={{0,24},{1,25},{2,26},{3,27},{4,28},{5,29},{6,30},{7,31},{8,16},{9,... | collective-permute-start | bytes 786440 | tf_op jit(solution)/shard_map/r_z3/ppermute | solution.py:116
  110.6 2.2 %collective-permute-done.35 = f32[2,128]{1,0:T(2,128)S(1)} collective-permute-done((f32[2,128]{1,0:T(2,128)S(1)}, f32[2,128]{1,0:T(2,128)S(1)}, u32[]{:S(2)}, u32[]{:S(2)}) %collective-permute-start.35) | collective-permute-done | bytes 1056 | tf_op jit(solution)/shard_map/t_z2/ppermute | solution.py:116
  114.7 5.3 %collective-permute-done.30.refs_2_ = bf16[128,1024]{1,0:T(8,128)(2,1)S(1)} collective-permute-done((bf16[128,1024]{1,0:T(8,128)(2,1)S(1)}, bf16[128,1024]{1,0:T(8,128)(2,1)S(1)}, u32[]{:S(2)}, u32[]{:S(2)}) %collective-permute-start.30) | collective-permute-done | bytes 262176 | tf_op jit(solution)/shard_map/r_z3/ppermute | solution.py:116
  (102 shorter events, 41.8 us)
Async XLA Ops:
  0.6 19.9 %collective-permute-start.4 = (bf16[384,4096]{1,0:T(8,128)(2,1)}, bf16[384,4096]{1,0:T(8,128)(2,1)}, u32[]{:S(2)}, u32[]{:S(2)}) collective-permute-start(bf16[384,4096]{1,0:T(8,128)(2,1)} %bitcast.37), channel_id=1, source_target_pairs={{0,1},{1,0},{2,3},{3,2},{4,5},{5,4},{6,7},{7,6},{8,9},{9,8},{10,11... | collective-permute-start | bytes 9437192 | tf_op jit(solution)/shard_map/weights/ppermute | solution.py:116
  3.1 17.2 %collective-permute-start = (bf16[136,1024]{1,0:T(8,128)(2,1)}, bf16[136,1024]{1,0:T(8,128)(2,1)S(1)}, u32[]{:S(2)}, u32[]{:S(2)}) collective-permute-start(bf16[136,1024]{1,0:T(8,128)(2,1)} %get-tuple-element.60.refs_0_), channel_id=1, source_target_pairs={{0,16},{1,17},{2,18},{3,19},{4,20},{5,21},{6,22},{7,23},{8,24},{9,... | collective-permute-start | bytes 835592 | tf_op jit(solution)/shard_map/z2/ppermute | solution.py:116
  6.7 13.8 %collective-permute-start.1 = (bf16[136,1024]{1,0:T(8,128)(2,1)}, bf16[136,1024]{1,0:T(8,128)(2,1)S(1)}, u32[]{:S(2)}, u32[]{:S(2)}) collective-permute-start(bf16[136,1024]{1,0:T(8,128)(2,1)} %get-tuple-element.60.refs_0_), channel_id=1, source_target_pairs={{0,8},{1,9},{2,10},{3,11},{4,12},{5,13},{6,14},{7,15},{8,0},{9,1},... | collective-permute-start | bytes 835592 | tf_op jit(solution)/shard_map/z1/ppermute | solution.py:116
  8.3 12.2 %collective-permute-start.2 = (bf16[136,1024]{1,0:T(8,128)(2,1)}, bf16[136,1024]{1,0:T(8,128)(2,1)S(1)}, u32[]{:S(2)}, u32[]{:S(2)}) collective-permute-start(bf16[136,1024]{1,0:T(8,128)(2,1)} %get-tuple-element.60.refs_0_), channel_id=1, source_target_pairs={{0,4},{1,3},{2,6},{3,1},{4,0},{5,7},{6,2},{7,5},{8,12},{9,11},{10,... | collective-permute-start | bytes 835592 | tf_op jit(solution)/shard_map/first0/ppermute | solution.py:116
  9.8 10.7 %collective-permute-start.3 = (bf16[136,1024]{1,0:T(8,128)(2,1)}, bf16[136,1024]{1,0:T(8,128)(2,1)S(1)}, u32[]{:S(2)}, u32[]{:S(2)}) collective-permute-start(bf16[136,1024]{1,0:T(8,128)(2,1)} %get-tuple-element.60.refs_0_), channel_id=1, source_target_pairs={{0,2},{1,5},{2,0},{3,7},{4,6},{5,1},{6,4},{7,3},{8,10},{9,13},{10,... | collective-permute-start | bytes 835592 | tf_op jit(solution)/shard_map/second0/ppermute | solution.py:116
  20.5 13.4 %collective-permute-start.9 = (bf16[4096,384]{1,0:T(8,128)(2,1)}, bf16[4096,384]{1,0:T(8,128)(2,1)S(1)}, u32[]{:S(2)}, u32[]{:S(2)}) collective-permute-start(bf16[4096,384]{1,0:T(8,128)(2,1)} %bitcast.40), channel_id=1, source_target_pairs={{0,1},{1,0},{2,3},{3,2},{4,5},{5,4},{6,7},{7,6},{8,9},{9,8},{10,11... | collective-permute-start | bytes 9437192 | tf_op jit(solution)/shard_map/weights/ppermute | solution.py:116
  22.1 9.2 %collective-permute-start.6 = (bf16[136,1024]{1,0:T(8,128)(2,1)S(1)}, bf16[136,1024]{1,0:T(8,128)(2,1)S(1)}, u32[]{:S(2)}, u32[]{:S(2)}) collective-permute-start(bf16[136,1024]{1,0:T(8,128)(2,1)S(1)} %collective-permute-done.refs_3_.refs_4_), channel_id=1, source_target_pairs={{0,4},{1,3},{2,6},{3,1},{4,0},{5,7},{6,2},{7,5},{8,12},{9,11},{10,... | collective-permute-start | bytes 835592 | tf_op jit(solution)/shard_map/first2/ppermute | solution.py:116
  33.9 15.8 %collective-permute-start.13 = (bf16[4096,384]{1,0:T(8,128)(2,1)}, bf16[4096,384]{1,0:T(8,128)(2,1)}, u32[]{:S(2)}, u32[]{:S(2)}) collective-permute-start(bf16[4096,384]{1,0:T(8,128)(2,1)} %bitcast.43), channel_id=1, source_target_pairs={{0,1},{1,0},{2,3},{3,2},{4,5},{5,4},{6,7},{7,6},{8,9},{9,8},{10,11... | collective-permute-start | bytes 9437192 | tf_op jit(solution)/shard_map/weights/ppermute | solution.py:116
  35.5 12.4 %collective-permute-start.11 = (bf16[136,1024]{1,0:T(8,128)(2,1)S(1)}, bf16[136,1024]{1,0:T(8,128)(2,1)S(1)}, u32[]{:S(2)}, u32[]{:S(2)}) collective-permute-start(bf16[136,1024]{1,0:T(8,128)(2,1)S(1)} %collective-permute-done.1.refs_0_), channel_id=1, source_target_pairs={{0,4},{1,3},{2,6},{3,1},{4,0},{5,7},{6,2},{7,5},{8,12},{9,11},{10,... | collective-permute-start | bytes 835592 | tf_op jit(solution)/shard_map/first1/ppermute | solution.py:116
  37.0 12.7 %collective-permute-start.12 = (bf16[136,1024]{1,0:T(8,128)(2,1)S(1)}, bf16[136,1024]{1,0:T(8,128)(2,1)S(1)}, u32[]{:S(2)}, u32[]{:S(2)}) collective-permute-start(bf16[136,1024]{1,0:T(8,128)(2,1)S(1)} %collective-permute-done.1.refs_0_), channel_id=1, source_target_pairs={{0,2},{1,5},{2,0},{3,7},{4,6},{5,1},{6,4},{7,3},{8,10},{9,13},{10,... | collective-permute-start | bytes 835592 | tf_op jit(solution)/shard_map/second1/ppermute | solution.py:116
  38.0 11.6 %collective-permute-start.14 = (bf16[136,1024]{1,0:T(8,128)(2,1)S(1)}, bf16[136,1024]{1,0:T(8,128)(2,1)S(1)}, u32[]{:S(2)}, u32[]{:S(2)}) collective-permute-start(bf16[136,1024]{1,0:T(8,128)(2,1)S(1)} %collective-permute-done.5.refs_3_.refs_4_), channel_id=1, source_target_pairs={{0,4},{1,3},{2,6},{3,1},{4,0},{5,7},{6,2},{7,5},{8,12},{9,11},{10,... | collective-permute-start | bytes 835592 | tf_op jit(solution)/shard_map/first3/ppermute | solution.py:116
  52.1 10.3 %collective-permute-start.17 = (bf16[136,1024]{1,0:T(8,128)(2,1)S(1)}, bf16[136,1024]{1,0:T(8,128)(2,1)S(1)}, u32[]{:S(2)}, u32[]{:S(2)}) collective-permute-start(bf16[136,1024]{1,0:T(8,128)(2,1)S(1)} %collective-permute-done.5.refs_3_.refs_4_), channel_id=1, source_target_pairs={{0,2},{1,5},{2,0},{3,7},{4,6},{5,1},{6,4},{7,3},{8,10},{9,13},{10,... | collective-permute-start | bytes 835592 | tf_op jit(solution)/shard_map/second3/ppermute | solution.py:116
  53.0 10.6 %collective-permute-start.18 = (bf16[136,1024]{1,0:T(8,128)(2,1)S(1)}, bf16[136,1024]{1,0:T(8,128)(2,1)S(1)}, u32[]{:S(2)}, u32[]{:S(2)}) collective-permute-start(bf16[136,1024]{1,0:T(8,128)(2,1)S(1)} %collective-permute-done.11.refs_1_), channel_id=1, source_target_pairs={{0,2},{1,5},{2,0},{3,7},{4,6},{5,1},{6,4},{7,3},{8,10},{9,13},{10,... | collective-permute-start | bytes 835592 | tf_op jit(solution)/shard_map/third1/ppermute | solution.py:116
  54.1 10.5 %collective-permute-start.19 = (bf16[136,1024]{1,0:T(8,128)(2,1)S(1)}, bf16[136,1024]{1,0:T(8,128)(2,1)S(1)}, u32[]{:S(2)}, u32[]{:S(2)}) collective-permute-start(bf16[136,1024]{1,0:T(8,128)(2,1)S(1)} %collective-permute-done.14.refs_4_.refs_5_), channel_id=1, source_target_pairs={{0,2},{1,5},{2,0},{3,7},{4,6},{5,1},{6,4},{7,3},{8,10},{9,13},{10,... | collective-permute-start | bytes 835592 | tf_op jit(solution)/shard_map/third3/ppermute | solution.py:116
  61.2 9.2 %collective-permute-start.20 = (bf16[256,1024]{1,0:T(8,128)(2,1)S(1)}, bf16[256,1024]{1,0:T(8,128)(2,1)S(1)}, u32[]{:S(2)}, u32[]{:S(2)}) collective-permute-start(bf16[256,1024]{1,0:T(8,128)(2,1)S(1)} %get-tuple-element.94), channel_id=1, source_target_pairs={{0,2},{1,5},{2,0},{3,7},{4,6},{5,1},{6,4},{7,3},{8,10},{9,13},{10,... | collective-permute-start | bytes 1572872 | tf_op jit(solution)/shard_map/r_corner0/ppermute | solution.py:116
  71.3 14.8 %collective-permute-start.23 = (bf16[256,1024]{1,0:T(8,128)(2,1)}, bf16[256,1024]{1,0:T(8,128)(2,1)}, u32[]{:S(2)}, u32[]{:S(2)}) collective-permute-start(bf16[256,1024]{1,0:T(8,128)(2,1)} %get-tuple-element.102), channel_id=1, source_target_pairs={{0,2},{1,5},{2,0},{3,7},{4,6},{5,1},{6,4},{7,3},{8,10},{9,13},{10,... | collective-permute-start | bytes 1572872 | tf_op jit(solution)/shard_map/r_right0/ppermute | solution.py:116
  72.5 14.9 %collective-permute-start.24 = (bf16[256,1024]{1,0:T(8,128)(2,1)S(1)}, bf16[256,1024]{1,0:T(8,128)(2,1)}, u32[]{:S(2)}, u32[]{:S(2)}) collective-permute-start(bf16[256,1024]{1,0:T(8,128)(2,1)S(1)} %corner.2), channel_id=1, source_target_pairs={{0,4},{1,3},{2,6},{3,1},{4,0},{5,7},{6,2},{7,5},{8,12},{9,11},{10,... | collective-permute-start | bytes 1572872 | tf_op jit(solution)/shard_map/r_left0/ppermute | solution.py:116
  81.7 10.4 %collective-permute-start.26 = (bf16[256,1024]{1,0:T(8,128)(2,1)}, bf16[256,1024]{1,0:T(8,128)(2,1)S(1)}, u32[]{:S(2)}, u32[]{:S(2)}) collective-permute-start(bf16[256,1024]{1,0:T(8,128)(2,1)} %get-tuple-element.107), channel_id=1, source_target_pairs={{0,2},{1,5},{2,0},{3,7},{4,6},{5,1},{6,4},{7,3},{8,10},{9,13},{10,... | collective-permute-start | bytes 1572872 | tf_op jit(solution)/shard_map/r_corner1/ppermute | solution.py:116
  84.1 10.7 %collective-permute-start.32 = (f32[2,4,128]{2,1,0:T(4,128)S(1)}, f32[2,4,128]{2,1,0:T(4,128)S(1)}, u32[]{:S(2)}, u32[]{:S(2)}) collective-permute-start(f32[2,4,128]{2,1,0:T(4,128)S(1)} %fusion), channel_id=1, source_target_pairs={{0,2},{1,3},{2,0},{3,1},{4,6},{5,7},{6,4},{7,5},{8,10},{9,11},{10,... | collective-permute-start | bytes 12296 | tf_op jit(solution)/shard_map/t_x/ppermute | solution.py:116
  88.8 14.0 %collective-permute-start.27 = (bf16[256,1024]{1,0:T(8,128)(2,1)}, bf16[256,1024]{1,0:T(8,128)(2,1)S(1)}, u32[]{:S(2)}, u32[]{:S(2)}) collective-permute-start(bf16[256,1024]{1,0:T(8,128)(2,1)} %copy-done.7), channel_id=1, source_target_pairs={{0,2},{1,5},{2,0},{3,7},{4,6},{5,1},{6,4},{7,3},{8,10},{9,13},{10,... | collective-permute-start | bytes 1572872 | tf_op jit(solution)/shard_map/r_right1/ppermute | solution.py:116
  89.8 13.5 %collective-permute-start.25 = (bf16[128,1024]{1,0:T(8,128)(2,1)S(1)}, bf16[128,1024]{1,0:T(8,128)(2,1)S(1)}, u32[]{:S(2)}, u32[]{:S(2)}) collective-permute-start(bf16[128,1024]{1,0:T(8,128)(2,1)S(1)} %get-tuple-element.104), channel_id=1, source_target_pairs={{0,16},{1,17},{2,18},{3,19},{4,20},{5,21},{6,22},{7,23},{8,24},{9,... | collective-permute-start | bytes 786440 | tf_op jit(solution)/shard_map/r_z2/ppermute | solution.py:116
  93.4 9.4 %collective-permute-start.28 = (bf16[256,1024]{1,0:T(8,128)(2,1)S(1)}, bf16[256,1024]{1,0:T(8,128)(2,1)S(1)}, u32[]{:S(2)}, u32[]{:S(2)}) collective-permute-start(bf16[256,1024]{1,0:T(8,128)(2,1)S(1)} %corner.3), channel_id=1, source_target_pairs={{0,4},{1,3},{2,6},{3,1},{4,0},{5,7},{6,2},{7,5},{8,12},{9,11},{10,... | collective-permute-start | bytes 1572872 | tf_op jit(solution)/shard_map/r_left1/ppermute | solution.py:116
  105.3 9.3 %collective-permute-start.29 = (bf16[128,1024]{1,0:T(8,128)(2,1)S(1)}, bf16[128,1024]{1,0:T(8,128)(2,1)S(1)}, u32[]{:S(2)}, u32[]{:S(2)}) collective-permute-start(bf16[128,1024]{1,0:T(8,128)(2,1)S(1)} %get-tuple-element.110), channel_id=1, source_target_pairs={{0,8},{1,9},{2,10},{3,11},{4,12},{5,13},{6,14},{7,15},{8,0},{9,1},... | collective-permute-start | bytes 786440 | tf_op jit(solution)/shard_map/r_z1/ppermute | solution.py:116
  107.7 12.2 %collective-permute-start.30 = (bf16[128,1024]{1,0:T(8,128)(2,1)S(1)}, bf16[128,1024]{1,0:T(8,128)(2,1)S(1)}, u32[]{:S(2)}, u32[]{:S(2)}) collective-permute-start(bf16[128,1024]{1,0:T(8,128)(2,1)S(1)} %get-tuple-element.111), channel_id=1, source_target_pairs={{0,24},{1,25},{2,26},{3,27},{4,28},{5,29},{6,30},{7,31},{8,16},{9,... | collective-permute-start | bytes 786440 | tf_op jit(solution)/shard_map/r_z3/ppermute | solution.py:116
  (23 other events, 135.9 us)

commit v7 on v6

--- a/solution.py
+++ b/solution.py
@@ -433,7 +433,7 @@
 def add_pieces(block, base, first, second, types):
     rows, cols = base.shape
     part = rows // len(types)
-    wide = cols // 2
+    wide = cols
 
     def body(s_ref, b_ref, f_ref, g_ref, *outs):
         for i, out in enumerate(outs):
@@ -442,7 +442,7 @@
 
     spec = lambda n: pl.BlockSpec((n, wide), lambda i, s: (0, i))
     outs = [shape_of((part, cols), t) for t in types]
-    return kernel("add", body, outs, (2,), [spec(rows)] * 3, [spec(part)] * len(outs), block, base, first, second)
+    return kernel("add", body, outs, (1,), [spec(rows)] * 3, [spec(part)] * len(outs), block, base, first, second)
 
 
 def add_corner(block, base, corner):
@@ -451,8 +451,8 @@
     def body(s_ref, b_ref, c_ref, out):
         out[...] = (b_ref[...].astype(F32) + c_ref[...].astype(F32)).astype(BF16)
 
-    spec = pl.BlockSpec((rows, cols // 2), lambda i, s: (0, i))
-    return kernel("corner", body, shape_of(base.shape, BF16), (2,), [spec] * 2, spec, block, base, corner)
+    spec = pl.BlockSpec((rows, cols), lambda i, s: (0, i))
+    return kernel("corner", body, shape_of(base.shape, BF16), (1,), [spec] * 2, spec, block, base, corner)
 
 
 def last_sum(block, keep, parts, out_type):

time: 121 us -> 121 us (level)
  transfers between devices with their start and end apart: 37 -> 37, of which waited for: 17 -> 18; matrix products, arithmetic and copies ran while one was open for 1% -> 1% of each run, Pallas kernels for 23% -> 23%
where the time goes in v7:
time: 121 us; the launch traced here: 120 us
  waiting for transfers between devices  43.4 us (36%)
  starting transfers between devices  40.6 us (34%)
  Pallas kernels  28.9 us (24%)
  local copies, waits for them, and re-layouts  5.92 us (5%)
    ppermute x37, waiting for transfers between devices, send(): return lax.ppermute(value, BOTH, pairs)  43.4 us
    ppermute x37, starting transfers between devices, send(): return lax.ppermute(value, BOTH, pairs)  40.6 us
    pallas_call x11, Pallas kernels, kernel(): pl.pallas_call(body, out_shape=outs, grid_spec=pltpu.PrefetchScalarGridSp...  24.4 us
    unnamed x20, local copies, waits for them, and re-layouts  5.9 us
    pallas_call x2, Pallas kernels, prepare(): pl.pallas_call(body, out_shape=[out] * 3, grid_spec=pltpu.PrefetchScalarG...  2.53 us
  transfers between devices with their start and end apart: 37, of which 18 were waited for; matrix products, arithmetic and copies ran while one was open for 1% of the time, Pallas kernels for 23%

profile of v7, /device:TPU:0, one launch (start us, length us, event | category | flops | bytes accessed | tf_op | source)
XLA Modules:
  0.0 120.5 jit_solution(5270928415939620216)
XLA Ops:
  1.1 2.0 %pack.1 = (bf16[136,1024]{1,0:T(8,128)(2,1)}, f32[8,128]{1,0:T(8,128)}) custom-call(bf16[128,1024]{1,0:T(8,128)(2,1)} %g_ref.1, s32[8,128]{1,0:T(8,128)} %bitcast.46, bf16[8,128]{1,0:T(8,128)(2,1)} %bitcast.47), custom_call_target="tpu_custom_call" | custom-call | tf_op jit(solution)/shard_map/pack/pallas_call | solution.py:177
  3.1 3.6 %collective-permute-start = (bf16[136,1024]{1,0:T(8,128)(2,1)}, bf16[136,1024]{1,0:T(8,128)(2,1)S(1)}, u32[]{:S(2)}, u32[]{:S(2)}) collective-permute-start(bf16[136,1024]{1,0:T(8,128)(2,1)} %get-tuple-element.60.refs_0_), channel_id=1, source_target_pairs={{0,16},{1,17},{2,18},{3,19},{4,20},{5,21},{6,22},{7,23},{8,24},{9,... | collective-permute-start | bytes 835592 | tf_op jit(solution)/shard_map/z2/ppermute | solution.py:116
  6.7 1.6 %collective-permute-start.1 = (bf16[136,1024]{1,0:T(8,128)(2,1)}, bf16[136,1024]{1,0:T(8,128)(2,1)S(1)}, u32[]{:S(2)}, u32[]{:S(2)}) collective-permute-start(bf16[136,1024]{1,0:T(8,128)(2,1)} %get-tuple-element.60.refs_0_), channel_id=1, source_target_pairs={{0,8},{1,9},{2,10},{3,11},{4,12},{5,13},{6,14},{7,15},{8,0},{9,1},... | collective-permute-start | bytes 835592 | tf_op jit(solution)/shard_map/z1/ppermute | solution.py:116
  8.3 1.5 %collective-permute-start.2 = (bf16[136,1024]{1,0:T(8,128)(2,1)}, bf16[136,1024]{1,0:T(8,128)(2,1)S(1)}, u32[]{:S(2)}, u32[]{:S(2)}) collective-permute-start(bf16[136,1024]{1,0:T(8,128)(2,1)} %get-tuple-element.60.refs_0_), channel_id=1, source_target_pairs={{0,4},{1,3},{2,6},{3,1},{4,0},{5,7},{6,2},{7,5},{8,12},{9,11},{10,... | collective-permute-start | bytes 835592 | tf_op jit(solution)/shard_map/first0/ppermute | solution.py:116
  11.3 9.0 %collective-permute-done.refs_3_.refs_4_ = bf16[136,1024]{1,0:T(8,128)(2,1)S(1)} collective-permute-done((bf16[136,1024]{1,0:T(8,128)(2,1)}, bf16[136,1024]{1,0:T(8,128)(2,1)S(1)}, u32[]{:S(2)}, u32[]{:S(2)}) %collective-permute-start) | collective-permute-done | bytes 278560 | tf_op jit(solution)/shard_map/z2/ppermute | solution.py:116
  20.6 1.6 %collective-permute-start.5 = (bf16[136,1024]{1,0:T(8,128)(2,1)S(1)}, bf16[136,1024]{1,0:T(8,128)(2,1)S(1)}, u32[]{:S(2)}, u32[]{:S(2)}) collective-permute-start(bf16[136,1024]{1,0:T(8,128)(2,1)S(1)} %collective-permute-done.refs_3_.refs_4_), channel_id=1, source_target_pairs={{0,8},{1,9},{2,10},{3,11},{4,12},{5,13},{6,14},{7,15},{8,0},{9,1},... | collective-permute-start | bytes 835592 | tf_op jit(solution)/shard_map/z3/ppermute | solution.py:116
  25.7 4.0 %collective-permute-done.5.refs_3_.refs_4_ = bf16[136,1024]{1,0:T(8,128)(2,1)S(1)} collective-permute-done((bf16[136,1024]{1,0:T(8,128)(2,1)S(1)}, bf16[136,1024]{1,0:T(8,128)(2,1)S(1)}, u32[]{:S(2)}, u32[]{:S(2)}) %collective-permute-start.5) | collective-permute-done | bytes 278560 | tf_op jit(solution)/shard_map/z3/ppermute | solution.py:116
  29.7 1.7 %collective-permute-done.6.refs_4_.refs_5_ = bf16[136,1024]{1,0:T(8,128)(2,1)S(1)} collective-permute-done((bf16[136,1024]{1,0:T(8,128)(2,1)S(1)}, bf16[136,1024]{1,0:T(8,128)(2,1)S(1)}, u32[]{:S(2)}, u32[]{:S(2)}) %collective-permute-start.6) | collective-permute-done | bytes 278560 | tf_op jit(solution)/shard_map/first2/ppermute | solution.py:116
  31.4 2.5 %collective-permute-done.8.refs_3_ = bf16[136,1024]{1,0:T(8,128)(2,1)S(1)} collective-permute-done((bf16[136,1024]{1,0:T(8,128)(2,1)S(1)}, bf16[136,1024]{1,0:T(8,128)(2,1)S(1)}, u32[]{:S(2)}, u32[]{:S(2)}) %collective-permute-start.8) | collective-permute-done | bytes 278560 | tf_op jit(solution)/shard_map/third0/ppermute | solution.py:116
  43.7 4.2 %hidden.2 = (f32[512,384]{1,0:T(8,128)S(1)}, bf16[512,384]{1,0:T(8,128)(2,1)S(1)}) custom-call(s32[1]{0:T(128)} %bitcast.s_ref, bf16[136,1024]{1,0:T(8,128)(2,1)S(1)} %copy-done.4, bf16[136,1024]{1,0:T(8,128)(2,1)S(1)} %collective-permute-done.2.refs_1_, bf16[136,1024]{1,0:T(8,128)(2,1)S(1)} %collective-permute-done.3.refs_2_, ...), custom_call_target="tpu_custom_call" | custom-call | tf_op jit(solution)/shard_map/hidden/pallas_call | solution.py:136
  47.9 1.8 %collective-permute-done.12.refs_2_ = bf16[136,1024]{1,0:T(8,128)(2,1)S(1)} collective-permute-done((bf16[136,1024]{1,0:T(8,128)(2,1)S(1)}, bf16[136,1024]{1,0:T(8,128)(2,1)S(1)}, u32[]{:S(2)}, u32[]{:S(2)}) %collective-permute-start.12) | collective-permute-done | bytes 278560 | tf_op jit(solution)/shard_map/second1/ppermute | solution.py:116
  49.8 1.6 %collective-permute-done.15.b_ref = bf16[512,384]{1,0:T(8,128)(2,1)S(1)} collective-permute-done((bf16[512,384]{1,0:T(8,128)(2,1)S(1)}, bf16[512,384]{1,0:T(8,128)(2,1)S(1)}, u32[]{:S(2)}, u32[]{:S(2)}) %collective-permute-start.15) | collective-permute-done | bytes 393248 | tf_op jit(solution)/shard_map/swap_bh0/ppermute | solution.py:116
  55.1 6.1 %input.2 = (bf16[256,1024]{1,0:T(8,128)(2,1)S(1)}, bf16[256,1024]{1,0:T(8,128)(2,1)}, bf16[256,1024]{1,0:T(8,128)(2,1)S(1)}, bf16[256,1024]{1,0:T(8,128)(2,1)S(1)}) custom-call(s32[1]{0:T(128)} %bitcast.s_ref, bf16[512,768]{1,0:T(8,128)(2,1)S(1)} %get-tuple-element.82.m_ref, bf16[512,768]{1,0:T(8,128)(2,1)S(1)} %collective-permute-done.16.t_ref, ...), custom_call_target="tpu_custom_call" | custom-call | tf_op jit(solution)/shard_map/input/pallas_call | solution.py:136
  64.6 4.2 %hidden.3 = (f32[512,384]{1,0:T(8,128)S(1)}, bf16[512,384]{1,0:T(8,128)(2,1)S(1)}) custom-call(s32[1]{0:T(128)} %bitcast.s_ref, bf16[136,1024]{1,0:T(8,128)(2,1)S(1)} %collective-permute-done.1.refs_0_, bf16[136,1024]{1,0:T(8,128)(2,1)S(1)} %collective-permute-done.11.refs_1_, bf16[136,1024]{1,0:T(8,128)(2,1)S(1)} %collective-permute-done.12.refs_2_, ...), custom_call_target="tpu_custom_call" | custom-call | tf_op jit(solution)/shard_map/hidden/pallas_call | solution.py:136
  68.9 1.6 %collective-permute-done.20.c_ref = bf16[256,1024]{1,0:T(8,128)(2,1)S(1)} collective-permute-done((bf16[256,1024]{1,0:T(8,128)(2,1)S(1)}, bf16[256,1024]{1,0:T(8,128)(2,1)S(1)}, u32[]{:S(2)}, u32[]{:S(2)}) %collective-permute-start.20) | collective-permute-done | bytes 524320 | tf_op jit(solution)/shard_map/r_corner0/ppermute | solution.py:116
  73.8 6.3 %input.3 = (bf16[256,1024]{1,0:T(8,128)(2,1)}, bf16[256,1024]{1,0:T(8,128)(2,1)S(1)}, bf16[256,1024]{1,0:T(8,128)(2,1)S(1)}, bf16[256,1024]{1,0:T(8,128)(2,1)S(1)}) custom-call(s32[1]{0:T(128)} %bitcast.s_ref, bf16[512,768]{1,0:T(8,128)(2,1)S(1)} %get-tuple-element.99.m_ref, bf16[512,768]{1,0:T(8,128)(2,1)S(1)} %collective-permute-done.22.t_ref, ...), custom_call_target="tpu_custom_call" | custom-call | tf_op jit(solution)/shard_map/input/pallas_call | solution.py:136
  89.7 2.3 %collective-permute-start.25 = (bf16[128,1024]{1,0:T(8,128)(2,1)S(1)}, bf16[128,1024]{1,0:T(8,128)(2,1)S(1)}, u32[]{:S(2)}, u32[]{:S(2)}) collective-permute-start(bf16[128,1024]{1,0:T(8,128)(2,1)S(1)} %get-tuple-element.104), channel_id=1, source_target_pairs={{0,16},{1,17},{2,18},{3,19},{4,20},{5,21},{6,22},{7,23},{8,24},{9,... | collective-permute-start | bytes 786440 | tf_op jit(solution)/shard_map/r_z2/ppermute | solution.py:116
  93.2 1.5 %collective-permute-start.28 = (bf16[256,1024]{1,0:T(8,128)(2,1)S(1)}, bf16[256,1024]{1,0:T(8,128)(2,1)S(1)}, u32[]{:S(2)}, u32[]{:S(2)}) collective-permute-start(bf16[256,1024]{1,0:T(8,128)(2,1)S(1)} %corner.3), channel_id=1, source_target_pairs={{0,4},{1,3},{2,6},{3,1},{4,0},{5,7},{6,2},{7,5},{8,12},{9,11},{10,... | collective-permute-start | bytes 1572872 | tf_op jit(solution)/shard_map/r_left1/ppermute | solution.py:116
  95.4 7.2 %collective-permute-done.33 = f32[4,128]{1,0:T(4,128)S(1)} collective-permute-done((f32[4,128]{1,0:T(4,128)S(1)}, f32[4,128]{1,0:T(4,128)S(1)}, u32[]{:S(2)}, u32[]{:S(2)}) %collective-permute-start.33) | collective-permute-done | bytes 2080 | tf_op jit(solution)/shard_map/t_y/ppermute | solution.py:116
  103.1 2.0 %collective-permute-start.34 = (f32[2,128]{1,0:T(2,128)S(1)}, f32[2,128]{1,0:T(2,128)S(1)}, u32[]{:S(2)}, u32[]{:S(2)}) collective-permute-start(f32[2,128]{1,0:T(2,128)S(1)} %bitcast.51), channel_id=1, source_target_pairs={{0,24},{1,25},{2,26},{3,27},{4,28},{5,29},{6,30},{7,31},{8,16},{9,... | collective-permute-start | bytes 3080 | tf_op jit(solution)/shard_map/t_z3/ppermute | solution.py:116
  105.8 1.7 %collective-permute-start.35 = (f32[2,128]{1,0:T(2,128)S(1)}, f32[2,128]{1,0:T(2,128)S(1)}, u32[]{:S(2)}, u32[]{:S(2)}) collective-permute-start(f32[2,128]{1,0:T(2,128)S(1)} %bitcast.50), channel_id=1, source_target_pairs={{0,16},{1,17},{2,18},{3,19},{4,20},{5,21},{6,22},{7,23},{8,24},{9,... | collective-permute-start | bytes 3080 | tf_op jit(solution)/shard_map/t_z2/ppermute | solution.py:116
  107.5 2.7 %collective-permute-start.30 = (bf16[128,1024]{1,0:T(8,128)(2,1)S(1)}, bf16[128,1024]{1,0:T(8,128)(2,1)S(1)}, u32[]{:S(2)}, u32[]{:S(2)}) collective-permute-start(bf16[128,1024]{1,0:T(8,128)(2,1)S(1)} %get-tuple-element.111), channel_id=1, source_target_pairs={{0,24},{1,25},{2,26},{3,27},{4,28},{5,29},{6,30},{7,31},{8,16},{9,... | collective-permute-start | bytes 786440 | tf_op jit(solution)/shard_map/r_z3/ppermute | solution.py:116
  110.2 2.2 %collective-permute-done.35 = f32[2,128]{1,0:T(2,128)S(1)} collective-permute-done((f32[2,128]{1,0:T(2,128)S(1)}, f32[2,128]{1,0:T(2,128)S(1)}, u32[]{:S(2)}, u32[]{:S(2)}) %collective-permute-start.35) | collective-permute-done | bytes 1056 | tf_op jit(solution)/shard_map/t_z2/ppermute | solution.py:116
  114.7 5.0 %collective-permute-done.30.refs_2_ = bf16[128,1024]{1,0:T(8,128)(2,1)S(1)} collective-permute-done((bf16[128,1024]{1,0:T(8,128)(2,1)S(1)}, bf16[128,1024]{1,0:T(8,128)(2,1)S(1)}, u32[]{:S(2)}, u32[]{:S(2)}) %collective-permute-start.30) | collective-permute-done | bytes 262176 | tf_op jit(solution)/shard_map/r_z3/ppermute | solution.py:116
  (102 shorter events, 41.8 us)
Async XLA Ops:
  0.6 19.9 %collective-permute-start.4 = (bf16[384,4096]{1,0:T(8,128)(2,1)}, bf16[384,4096]{1,0:T(8,128)(2,1)}, u32[]{:S(2)}, u32[]{:S(2)}) collective-permute-start(bf16[384,4096]{1,0:T(8,128)(2,1)} %bitcast.37), channel_id=1, source_target_pairs={{0,1},{1,0},{2,3},{3,2},{4,5},{5,4},{6,7},{7,6},{8,9},{9,8},{10,11... | collective-permute-start | bytes 9437192 | tf_op jit(solution)/shard_map/weights/ppermute | solution.py:116
  3.1 17.2 %collective-permute-start = (bf16[136,1024]{1,0:T(8,128)(2,1)}, bf16[136,1024]{1,0:T(8,128)(2,1)S(1)}, u32[]{:S(2)}, u32[]{:S(2)}) collective-permute-start(bf16[136,1024]{1,0:T(8,128)(2,1)} %get-tuple-element.60.refs_0_), channel_id=1, source_target_pairs={{0,16},{1,17},{2,18},{3,19},{4,20},{5,21},{6,22},{7,23},{8,24},{9,... | collective-permute-start | bytes 835592 | tf_op jit(solution)/shard_map/z2/ppermute | solution.py:116
  6.7 13.8 %collective-permute-start.1 = (bf16[136,1024]{1,0:T(8,128)(2,1)}, bf16[136,1024]{1,0:T(8,128)(2,1)S(1)}, u32[]{:S(2)}, u32[]{:S(2)}) collective-permute-start(bf16[136,1024]{1,0:T(8,128)(2,1)} %get-tuple-element.60.refs_0_), channel_id=1, source_target_pairs={{0,8},{1,9},{2,10},{3,11},{4,12},{5,13},{6,14},{7,15},{8,0},{9,1},... | collective-permute-start | bytes 835592 | tf_op jit(solution)/shard_map/z1/ppermute | solution.py:116
  8.3 12.2 %collective-permute-start.2 = (bf16[136,1024]{1,0:T(8,128)(2,1)}, bf16[136,1024]{1,0:T(8,128)(2,1)S(1)}, u32[]{:S(2)}, u32[]{:S(2)}) collective-permute-start(bf16[136,1024]{1,0:T(8,128)(2,1)} %get-tuple-element.60.refs_0_), channel_id=1, source_target_pairs={{0,4},{1,3},{2,6},{3,1},{4,0},{5,7},{6,2},{7,5},{8,12},{9,11},{10,... | collective-permute-start | bytes 835592 | tf_op jit(solution)/shard_map/first0/ppermute | solution.py:116
  9.8 10.7 %collective-permute-start.3 = (bf16[136,1024]{1,0:T(8,128)(2,1)}, bf16[136,1024]{1,0:T(8,128)(2,1)S(1)}, u32[]{:S(2)}, u32[]{:S(2)}) collective-permute-start(bf16[136,1024]{1,0:T(8,128)(2,1)} %get-tuple-element.60.refs_0_), channel_id=1, source_target_pairs={{0,2},{1,5},{2,0},{3,7},{4,6},{5,1},{6,4},{7,3},{8,10},{9,13},{10,... | collective-permute-start | bytes 835592 | tf_op jit(solution)/shard_map/second0/ppermute | solution.py:116
  20.5 13.4 %collective-permute-start.9 = (bf16[4096,384]{1,0:T(8,128)(2,1)}, bf16[4096,384]{1,0:T(8,128)(2,1)S(1)}, u32[]{:S(2)}, u32[]{:S(2)}) collective-permute-start(bf16[4096,384]{1,0:T(8,128)(2,1)} %bitcast.40), channel_id=1, source_target_pairs={{0,1},{1,0},{2,3},{3,2},{4,5},{5,4},{6,7},{7,6},{8,9},{9,8},{10,11... | collective-permute-start | bytes 9437192 | tf_op jit(solution)/shard_map/weights/ppermute | solution.py:116
  22.1 9.2 %collective-permute-start.6 = (bf16[136,1024]{1,0:T(8,128)(2,1)S(1)}, bf16[136,1024]{1,0:T(8,128)(2,1)S(1)}, u32[]{:S(2)}, u32[]{:S(2)}) collective-permute-start(bf16[136,1024]{1,0:T(8,128)(2,1)S(1)} %collective-permute-done.refs_3_.refs_4_), channel_id=1, source_target_pairs={{0,4},{1,3},{2,6},{3,1},{4,0},{5,7},{6,2},{7,5},{8,12},{9,11},{10,... | collective-permute-start | bytes 835592 | tf_op jit(solution)/shard_map/first2/ppermute | solution.py:116
  33.9 15.8 %collective-permute-start.13 = (bf16[4096,384]{1,0:T(8,128)(2,1)}, bf16[4096,384]{1,0:T(8,128)(2,1)}, u32[]{:S(2)}, u32[]{:S(2)}) collective-permute-start(bf16[4096,384]{1,0:T(8,128)(2,1)} %bitcast.43), channel_id=1, source_target_pairs={{0,1},{1,0},{2,3},{3,2},{4,5},{5,4},{6,7},{7,6},{8,9},{9,8},{10,11... | collective-permute-start | bytes 9437192 | tf_op jit(solution)/shard_map/weights/ppermute | solution.py:116
  35.5 12.4 %collective-permute-start.11 = (bf16[136,1024]{1,0:T(8,128)(2,1)S(1)}, bf16[136,1024]{1,0:T(8,128)(2,1)S(1)}, u32[]{:S(2)}, u32[]{:S(2)}) collective-permute-start(bf16[136,1024]{1,0:T(8,128)(2,1)S(1)} %collective-permute-done.1.refs_0_), channel_id=1, source_target_pairs={{0,4},{1,3},{2,6},{3,1},{4,0},{5,7},{6,2},{7,5},{8,12},{9,11},{10,... | collective-permute-start | bytes 835592 | tf_op jit(solution)/shard_map/first1/ppermute | solution.py:116
  37.0 12.7 %collective-permute-start.12 = (bf16[136,1024]{1,0:T(8,128)(2,1)S(1)}, bf16[136,1024]{1,0:T(8,128)(2,1)S(1)}, u32[]{:S(2)}, u32[]{:S(2)}) collective-permute-start(bf16[136,1024]{1,0:T(8,128)(2,1)S(1)} %collective-permute-done.1.refs_0_), channel_id=1, source_target_pairs={{0,2},{1,5},{2,0},{3,7},{4,6},{5,1},{6,4},{7,3},{8,10},{9,13},{10,... | collective-permute-start | bytes 835592 | tf_op jit(solution)/shard_map/second1/ppermute | solution.py:116
  38.0 11.6 %collective-permute-start.14 = (bf16[136,1024]{1,0:T(8,128)(2,1)S(1)}, bf16[136,1024]{1,0:T(8,128)(2,1)S(1)}, u32[]{:S(2)}, u32[]{:S(2)}) collective-permute-start(bf16[136,1024]{1,0:T(8,128)(2,1)S(1)} %collective-permute-done.5.refs_3_.refs_4_), channel_id=1, source_target_pairs={{0,4},{1,3},{2,6},{3,1},{4,0},{5,7},{6,2},{7,5},{8,12},{9,11},{10,... | collective-permute-start | bytes 835592 | tf_op jit(solution)/shard_map/first3/ppermute | solution.py:116
  52.1 10.3 %collective-permute-start.17 = (bf16[136,1024]{1,0:T(8,128)(2,1)S(1)}, bf16[136,1024]{1,0:T(8,128)(2,1)S(1)}, u32[]{:S(2)}, u32[]{:S(2)}) collective-permute-start(bf16[136,1024]{1,0:T(8,128)(2,1)S(1)} %collective-permute-done.5.refs_3_.refs_4_), channel_id=1, source_target_pairs={{0,2},{1,5},{2,0},{3,7},{4,6},{5,1},{6,4},{7,3},{8,10},{9,13},{10,... | collective-permute-start | bytes 835592 | tf_op jit(solution)/shard_map/second3/ppermute | solution.py:116
  53.0 10.6 %collective-permute-start.18 = (bf16[136,1024]{1,0:T(8,128)(2,1)S(1)}, bf16[136,1024]{1,0:T(8,128)(2,1)S(1)}, u32[]{:S(2)}, u32[]{:S(2)}) collective-permute-start(bf16[136,1024]{1,0:T(8,128)(2,1)S(1)} %collective-permute-done.11.refs_1_), channel_id=1, source_target_pairs={{0,2},{1,5},{2,0},{3,7},{4,6},{5,1},{6,4},{7,3},{8,10},{9,13},{10,... | collective-permute-start | bytes 835592 | tf_op jit(solution)/shard_map/third1/ppermute | solution.py:116
  54.1 10.5 %collective-permute-start.19 = (bf16[136,1024]{1,0:T(8,128)(2,1)S(1)}, bf16[136,1024]{1,0:T(8,128)(2,1)S(1)}, u32[]{:S(2)}, u32[]{:S(2)}) collective-permute-start(bf16[136,1024]{1,0:T(8,128)(2,1)S(1)} %collective-permute-done.14.refs_4_.refs_5_), channel_id=1, source_target_pairs={{0,2},{1,5},{2,0},{3,7},{4,6},{5,1},{6,4},{7,3},{8,10},{9,13},{10,... | collective-permute-start | bytes 835592 | tf_op jit(solution)/shard_map/third3/ppermute | solution.py:116
  61.2 9.2 %collective-permute-start.20 = (bf16[256,1024]{1,0:T(8,128)(2,1)S(1)}, bf16[256,1024]{1,0:T(8,128)(2,1)S(1)}, u32[]{:S(2)}, u32[]{:S(2)}) collective-permute-start(bf16[256,1024]{1,0:T(8,128)(2,1)S(1)} %get-tuple-element.94), channel_id=1, source_target_pairs={{0,2},{1,5},{2,0},{3,7},{4,6},{5,1},{6,4},{7,3},{8,10},{9,13},{10,... | collective-permute-start | bytes 1572872 | tf_op jit(solution)/shard_map/r_corner0/ppermute | solution.py:116
  71.2 14.8 %collective-permute-start.23 = (bf16[256,1024]{1,0:T(8,128)(2,1)}, bf16[256,1024]{1,0:T(8,128)(2,1)}, u32[]{:S(2)}, u32[]{:S(2)}) collective-permute-start(bf16[256,1024]{1,0:T(8,128)(2,1)} %get-tuple-element.102), channel_id=1, source_target_pairs={{0,2},{1,5},{2,0},{3,7},{4,6},{5,1},{6,4},{7,3},{8,10},{9,13},{10,... | collective-permute-start | bytes 1572872 | tf_op jit(solution)/shard_map/r_right0/ppermute | solution.py:116
  72.3 14.9 %collective-permute-start.24 = (bf16[256,1024]{1,0:T(8,128)(2,1)S(1)}, bf16[256,1024]{1,0:T(8,128)(2,1)}, u32[]{:S(2)}, u32[]{:S(2)}) collective-permute-start(bf16[256,1024]{1,0:T(8,128)(2,1)S(1)} %corner.2), channel_id=1, source_target_pairs={{0,4},{1,3},{2,6},{3,1},{4,0},{5,7},{6,2},{7,5},{8,12},{9,11},{10,... | collective-permute-start | bytes 1572872 | tf_op jit(solution)/shard_map/r_left0/ppermute | solution.py:116
  81.7 10.3 %collective-permute-start.26 = (bf16[256,1024]{1,0:T(8,128)(2,1)}, bf16[256,1024]{1,0:T(8,128)(2,1)S(1)}, u32[]{:S(2)}, u32[]{:S(2)}) collective-permute-start(bf16[256,1024]{1,0:T(8,128)(2,1)} %get-tuple-element.107), channel_id=1, source_target_pairs={{0,2},{1,5},{2,0},{3,7},{4,6},{5,1},{6,4},{7,3},{8,10},{9,13},{10,... | collective-permute-start | bytes 1572872 | tf_op jit(solution)/shard_map/r_corner1/ppermute | solution.py:116
  84.0 10.8 %collective-permute-start.32 = (f32[2,4,128]{2,1,0:T(4,128)S(1)}, f32[2,4,128]{2,1,0:T(4,128)S(1)}, u32[]{:S(2)}, u32[]{:S(2)}) collective-permute-start(f32[2,4,128]{2,1,0:T(4,128)S(1)} %fusion), channel_id=1, source_target_pairs={{0,2},{1,3},{2,0},{3,1},{4,6},{5,7},{6,4},{7,5},{8,10},{9,11},{10,... | collective-permute-start | bytes 12296 | tf_op jit(solution)/shard_map/t_x/ppermute | solution.py:116
  88.6 14.0 %collective-permute-start.27 = (bf16[256,1024]{1,0:T(8,128)(2,1)}, bf16[256,1024]{1,0:T(8,128)(2,1)S(1)}, u32[]{:S(2)}, u32[]{:S(2)}) collective-permute-start(bf16[256,1024]{1,0:T(8,128)(2,1)} %copy-done.7), channel_id=1, source_target_pairs={{0,2},{1,5},{2,0},{3,7},{4,6},{5,1},{6,4},{7,3},{8,10},{9,13},{10,... | collective-permute-start | bytes 1572872 | tf_op jit(solution)/shard_map/r_right1/ppermute | solution.py:116
  89.7 13.4 %collective-permute-start.25 = (bf16[128,1024]{1,0:T(8,128)(2,1)S(1)}, bf16[128,1024]{1,0:T(8,128)(2,1)S(1)}, u32[]{:S(2)}, u32[]{:S(2)}) collective-permute-start(bf16[128,1024]{1,0:T(8,128)(2,1)S(1)} %get-tuple-element.104), channel_id=1, source_target_pairs={{0,16},{1,17},{2,18},{3,19},{4,20},{5,21},{6,22},{7,23},{8,24},{9,... | collective-permute-start | bytes 786440 | tf_op jit(solution)/shard_map/r_z2/ppermute | solution.py:116
  93.2 9.4 %collective-permute-start.28 = (bf16[256,1024]{1,0:T(8,128)(2,1)S(1)}, bf16[256,1024]{1,0:T(8,128)(2,1)S(1)}, u32[]{:S(2)}, u32[]{:S(2)}) collective-permute-start(bf16[256,1024]{1,0:T(8,128)(2,1)S(1)} %corner.3), channel_id=1, source_target_pairs={{0,4},{1,3},{2,6},{3,1},{4,0},{5,7},{6,2},{7,5},{8,12},{9,11},{10,... | collective-permute-start | bytes 1572872 | tf_op jit(solution)/shard_map/r_left1/ppermute | solution.py:116
  105.2 9.5 %collective-permute-start.29 = (bf16[128,1024]{1,0:T(8,128)(2,1)S(1)}, bf16[128,1024]{1,0:T(8,128)(2,1)S(1)}, u32[]{:S(2)}, u32[]{:S(2)}) collective-permute-start(bf16[128,1024]{1,0:T(8,128)(2,1)S(1)} %get-tuple-element.110), channel_id=1, source_target_pairs={{0,8},{1,9},{2,10},{3,11},{4,12},{5,13},{6,14},{7,15},{8,0},{9,1},... | collective-permute-start | bytes 786440 | tf_op jit(solution)/shard_map/r_z1/ppermute | solution.py:116
  107.5 12.1 %collective-permute-start.30 = (bf16[128,1024]{1,0:T(8,128)(2,1)S(1)}, bf16[128,1024]{1,0:T(8,128)(2,1)S(1)}, u32[]{:S(2)}, u32[]{:S(2)}) collective-permute-start(bf16[128,1024]{1,0:T(8,128)(2,1)S(1)} %get-tuple-element.111), channel_id=1, source_target_pairs={{0,24},{1,25},{2,26},{3,27},{4,28},{5,29},{6,30},{7,31},{8,16},{9,... | collective-permute-start | bytes 786440 | tf_op jit(solution)/shard_map/r_z3/ppermute | solution.py:116
  (23 other events, 135.8 us)

commit v8 on v7

--- a/solution.py
+++ b/solution.py
@@ -129,6 +129,7 @@
 
 
 HINT = pl.CostEstimate(flops=0, transcendentals=0, bytes_accessed=0)
+SMALL = pltpu.CompilerParams(vmem_limit_bytes=40 << 20)
 LARGE = pltpu.CompilerParams(vmem_limit_bytes=48 << 20)
 
 
@@ -139,7 +140,7 @@
         grid_spec=pltpu.PrefetchScalarGridSpec(
             num_scalar_prefetch=1, grid=grid, in_specs=in_specs, out_specs=out_specs, scratch_shapes=scratch
         ),
-        compiler_params=LARGE,
+        compiler_params=LARGE if name in ("hidden", "input") else SMALL,
         cost_estimate=HINT,
         name=name,
     )(*args)

time: 121 us -> 121 us (level)
  no operation moved by 1% of the time
where the time goes in v8:
time: 121 us; the launch traced here: 120 us
  waiting for transfers between devices  43.4 us (36%)
  starting transfers between devices  40.6 us (34%)
  Pallas kernels  28.9 us (24%)
  local copies, waits for them, and re-layouts  5.92 us (5%)
    ppermute x37, waiting for transfers between devices, send(): return lax.ppermute(value, BOTH, pairs)  43.4 us
    ppermute x37, starting transfers between devices, send(): return lax.ppermute(value, BOTH, pairs)  40.6 us
    pallas_call x11, Pallas kernels, kernel(): pl.pallas_call(body, out_shape=outs, grid_spec=pltpu.PrefetchScalarGridSp...  24.4 us
    unnamed x20, local copies, waits for them, and re-layouts  5.9 us
    pallas_call x2, Pallas kernels, prepare(): pl.pallas_call(body, out_shape=[out] * 3, grid_spec=pltpu.PrefetchScalarG...  2.53 us
  transfers between devices with their start and end apart: 37, of which 18 were waited for; matrix products, arithmetic and copies ran while one was open for 1% of the time, Pallas kernels for 23%

profile of v8, /device:TPU:0, one launch (start us, length us, event | category | flops | bytes accessed | tf_op | source)
XLA Modules:
  0.0 120.5 jit_solution(1593746955407833336)
XLA Ops:
  1.1 2.0 %pack.1 = (bf16[136,1024]{1,0:T(8,128)(2,1)}, f32[8,128]{1,0:T(8,128)}) custom-call(bf16[128,1024]{1,0:T(8,128)(2,1)} %g_ref.1, s32[8,128]{1,0:T(8,128)} %bitcast.46, bf16[8,128]{1,0:T(8,128)(2,1)} %bitcast.47), custom_call_target="tpu_custom_call" | custom-call | tf_op jit(solution)/shard_map/pack/pallas_call | solution.py:178
  3.1 3.6 %collective-permute-start = (bf16[136,1024]{1,0:T(8,128)(2,1)}, bf16[136,1024]{1,0:T(8,128)(2,1)S(1)}, u32[]{:S(2)}, u32[]{:S(2)}) collective-permute-start(bf16[136,1024]{1,0:T(8,128)(2,1)} %get-tuple-element.60.refs_0_), channel_id=1, source_target_pairs={{0,16},{1,17},{2,18},{3,19},{4,20},{5,21},{6,22},{7,23},{8,24},{9,... | collective-permute-start | bytes 835592 | tf_op jit(solution)/shard_map/z2/ppermute | solution.py:116
  6.7 1.6 %collective-permute-start.1 = (bf16[136,1024]{1,0:T(8,128)(2,1)}, bf16[136,1024]{1,0:T(8,128)(2,1)S(1)}, u32[]{:S(2)}, u32[]{:S(2)}) collective-permute-start(bf16[136,1024]{1,0:T(8,128)(2,1)} %get-tuple-element.60.refs_0_), channel_id=1, source_target_pairs={{0,8},{1,9},{2,10},{3,11},{4,12},{5,13},{6,14},{7,15},{8,0},{9,1},... | collective-permute-start | bytes 835592 | tf_op jit(solution)/shard_map/z1/ppermute | solution.py:116
  11.3 9.0 %collective-permute-done.refs_3_.refs_4_ = bf16[136,1024]{1,0:T(8,128)(2,1)S(1)} collective-permute-done((bf16[136,1024]{1,0:T(8,128)(2,1)}, bf16[136,1024]{1,0:T(8,128)(2,1)S(1)}, u32[]{:S(2)}, u32[]{:S(2)}) %collective-permute-start) | collective-permute-done | bytes 278560 | tf_op jit(solution)/shard_map/z2/ppermute | solution.py:116
  20.6 1.6 %collective-permute-start.5 = (bf16[136,1024]{1,0:T(8,128)(2,1)S(1)}, bf16[136,1024]{1,0:T(8,128)(2,1)S(1)}, u32[]{:S(2)}, u32[]{:S(2)}) collective-permute-start(bf16[136,1024]{1,0:T(8,128)(2,1)S(1)} %collective-permute-done.refs_3_.refs_4_), channel_id=1, source_target_pairs={{0,8},{1,9},{2,10},{3,11},{4,12},{5,13},{6,14},{7,15},{8,0},{9,1},... | collective-permute-start | bytes 835592 | tf_op jit(solution)/shard_map/z3/ppermute | solution.py:116
  22.1 1.5 %collective-permute-start.6 = (bf16[136,1024]{1,0:T(8,128)(2,1)S(1)}, bf16[136,1024]{1,0:T(8,128)(2,1)S(1)}, u32[]{:S(2)}, u32[]{:S(2)}) collective-permute-start(bf16[136,1024]{1,0:T(8,128)(2,1)S(1)} %collective-permute-done.refs_3_.refs_4_), channel_id=1, source_target_pairs={{0,4},{1,3},{2,6},{3,1},{4,0},{5,7},{6,2},{7,5},{8,12},{9,11},{10,... | collective-permute-start | bytes 835592 | tf_op jit(solution)/shard_map/first2/ppermute | solution.py:116
  25.7 4.0 %collective-permute-done.5.refs_3_.refs_4_ = bf16[136,1024]{1,0:T(8,128)(2,1)S(1)} collective-permute-done((bf16[136,1024]{1,0:T(8,128)(2,1)S(1)}, bf16[136,1024]{1,0:T(8,128)(2,1)S(1)}, u32[]{:S(2)}, u32[]{:S(2)}) %collective-permute-start.5) | collective-permute-done | bytes 278560 | tf_op jit(solution)/shard_map/z3/ppermute | solution.py:116
  29.7 1.7 %collective-permute-done.6.refs_4_.refs_5_ = bf16[136,1024]{1,0:T(8,128)(2,1)S(1)} collective-permute-done((bf16[136,1024]{1,0:T(8,128)(2,1)S(1)}, bf16[136,1024]{1,0:T(8,128)(2,1)S(1)}, u32[]{:S(2)}, u32[]{:S(2)}) %collective-permute-start.6) | collective-permute-done | bytes 278560 | tf_op jit(solution)/shard_map/first2/ppermute | solution.py:116
  31.4 2.5 %collective-permute-done.8.refs_3_ = bf16[136,1024]{1,0:T(8,128)(2,1)S(1)} collective-permute-done((bf16[136,1024]{1,0:T(8,128)(2,1)S(1)}, bf16[136,1024]{1,0:T(8,128)(2,1)S(1)}, u32[]{:S(2)}, u32[]{:S(2)}) %collective-permute-start.8) | collective-permute-done | bytes 278560 | tf_op jit(solution)/shard_map/third0/ppermute | solution.py:116
  43.7 4.2 %hidden.2 = (f32[512,384]{1,0:T(8,128)S(1)}, bf16[512,384]{1,0:T(8,128)(2,1)S(1)}) custom-call(s32[1]{0:T(128)} %bitcast.s_ref, bf16[136,1024]{1,0:T(8,128)(2,1)S(1)} %copy-done.4, bf16[136,1024]{1,0:T(8,128)(2,1)S(1)} %collective-permute-done.2.refs_1_, bf16[136,1024]{1,0:T(8,128)(2,1)S(1)} %collective-permute-done.3.refs_2_, ...), custom_call_target="tpu_custom_call" | custom-call | tf_op jit(solution)/shard_map/hidden/pallas_call | solution.py:137
  47.9 1.8 %collective-permute-done.12.refs_2_ = bf16[136,1024]{1,0:T(8,128)(2,1)S(1)} collective-permute-done((bf16[136,1024]{1,0:T(8,128)(2,1)S(1)}, bf16[136,1024]{1,0:T(8,128)(2,1)S(1)}, u32[]{:S(2)}, u32[]{:S(2)}) %collective-permute-start.12) | collective-permute-done | bytes 278560 | tf_op jit(solution)/shard_map/second1/ppermute | solution.py:116
  49.8 1.6 %collective-permute-done.15.b_ref = bf16[512,384]{1,0:T(8,128)(2,1)S(1)} collective-permute-done((bf16[512,384]{1,0:T(8,128)(2,1)S(1)}, bf16[512,384]{1,0:T(8,128)(2,1)S(1)}, u32[]{:S(2)}, u32[]{:S(2)}) %collective-permute-start.15) | collective-permute-done | bytes 393248 | tf_op jit(solution)/shard_map/swap_bh0/ppermute | solution.py:116
  55.1 6.1 %input.2 = (bf16[256,1024]{1,0:T(8,128)(2,1)S(1)}, bf16[256,1024]{1,0:T(8,128)(2,1)}, bf16[256,1024]{1,0:T(8,128)(2,1)S(1)}, bf16[256,1024]{1,0:T(8,128)(2,1)S(1)}) custom-call(s32[1]{0:T(128)} %bitcast.s_ref, bf16[512,768]{1,0:T(8,128)(2,1)S(1)} %get-tuple-element.82.m_ref, bf16[512,768]{1,0:T(8,128)(2,1)S(1)} %collective-permute-done.16.t_ref, ...), custom_call_target="tpu_custom_call" | custom-call | tf_op jit(solution)/shard_map/input/pallas_call | solution.py:137
  64.6 4.2 %hidden.3 = (f32[512,384]{1,0:T(8,128)S(1)}, bf16[512,384]{1,0:T(8,128)(2,1)S(1)}) custom-call(s32[1]{0:T(128)} %bitcast.s_ref, bf16[136,1024]{1,0:T(8,128)(2,1)S(1)} %collective-permute-done.1.refs_0_, bf16[136,1024]{1,0:T(8,128)(2,1)S(1)} %collective-permute-done.11.refs_1_, bf16[136,1024]{1,0:T(8,128)(2,1)S(1)} %collective-permute-done.12.refs_2_, ...), custom_call_target="tpu_custom_call" | custom-call | tf_op jit(solution)/shard_map/hidden/pallas_call | solution.py:137
  68.9 1.6 %collective-permute-done.20.c_ref = bf16[256,1024]{1,0:T(8,128)(2,1)S(1)} collective-permute-done((bf16[256,1024]{1,0:T(8,128)(2,1)S(1)}, bf16[256,1024]{1,0:T(8,128)(2,1)S(1)}, u32[]{:S(2)}, u32[]{:S(2)}) %collective-permute-start.20) | collective-permute-done | bytes 524320 | tf_op jit(solution)/shard_map/r_corner0/ppermute | solution.py:116
  73.8 6.3 %input.3 = (bf16[256,1024]{1,0:T(8,128)(2,1)}, bf16[256,1024]{1,0:T(8,128)(2,1)S(1)}, bf16[256,1024]{1,0:T(8,128)(2,1)S(1)}, bf16[256,1024]{1,0:T(8,128)(2,1)S(1)}) custom-call(s32[1]{0:T(128)} %bitcast.s_ref, bf16[512,768]{1,0:T(8,128)(2,1)S(1)} %get-tuple-element.99.m_ref, bf16[512,768]{1,0:T(8,128)(2,1)S(1)} %collective-permute-done.22.t_ref, ...), custom_call_target="tpu_custom_call" | custom-call | tf_op jit(solution)/shard_map/input/pallas_call | solution.py:137
  89.7 2.3 %collective-permute-start.25 = (bf16[128,1024]{1,0:T(8,128)(2,1)S(1)}, bf16[128,1024]{1,0:T(8,128)(2,1)S(1)}, u32[]{:S(2)}, u32[]{:S(2)}) collective-permute-start(bf16[128,1024]{1,0:T(8,128)(2,1)S(1)} %get-tuple-element.104), channel_id=1, source_target_pairs={{0,16},{1,17},{2,18},{3,19},{4,20},{5,21},{6,22},{7,23},{8,24},{9,... | collective-permute-start | bytes 786440 | tf_op jit(solution)/shard_map/r_z2/ppermute | solution.py:116
  93.2 1.5 %collective-permute-start.28 = (bf16[256,1024]{1,0:T(8,128)(2,1)S(1)}, bf16[256,1024]{1,0:T(8,128)(2,1)S(1)}, u32[]{:S(2)}, u32[]{:S(2)}) collective-permute-start(bf16[256,1024]{1,0:T(8,128)(2,1)S(1)} %corner.3), channel_id=1, source_target_pairs={{0,4},{1,3},{2,6},{3,1},{4,0},{5,7},{6,2},{7,5},{8,12},{9,11},{10,... | collective-permute-start | bytes 1572872 | tf_op jit(solution)/shard_map/r_left1/ppermute | solution.py:116
  95.4 7.2 %collective-permute-done.33 = f32[4,128]{1,0:T(4,128)S(1)} collective-permute-done((f32[4,128]{1,0:T(4,128)S(1)}, f32[4,128]{1,0:T(4,128)S(1)}, u32[]{:S(2)}, u32[]{:S(2)}) %collective-permute-start.33) | collective-permute-done | bytes 2080 | tf_op jit(solution)/shard_map/t_y/ppermute | solution.py:116
  103.1 2.0 %collective-permute-start.34 = (f32[2,128]{1,0:T(2,128)S(1)}, f32[2,128]{1,0:T(2,128)S(1)}, u32[]{:S(2)}, u32[]{:S(2)}) collective-permute-start(f32[2,128]{1,0:T(2,128)S(1)} %bitcast.51), channel_id=1, source_target_pairs={{0,24},{1,25},{2,26},{3,27},{4,28},{5,29},{6,30},{7,31},{8,16},{9,... | collective-permute-start | bytes 3080 | tf_op jit(solution)/shard_map/t_z3/ppermute | solution.py:116
  105.8 1.7 %collective-permute-start.35 = (f32[2,128]{1,0:T(2,128)S(1)}, f32[2,128]{1,0:T(2,128)S(1)}, u32[]{:S(2)}, u32[]{:S(2)}) collective-permute-start(f32[2,128]{1,0:T(2,128)S(1)} %bitcast.50), channel_id=1, source_target_pairs={{0,16},{1,17},{2,18},{3,19},{4,20},{5,21},{6,22},{7,23},{8,24},{9,... | collective-permute-start | bytes 3080 | tf_op jit(solution)/shard_map/t_z2/ppermute | solution.py:116
  107.5 2.7 %collective-permute-start.30 = (bf16[128,1024]{1,0:T(8,128)(2,1)S(1)}, bf16[128,1024]{1,0:T(8,128)(2,1)S(1)}, u32[]{:S(2)}, u32[]{:S(2)}) collective-permute-start(bf16[128,1024]{1,0:T(8,128)(2,1)S(1)} %get-tuple-element.111), channel_id=1, source_target_pairs={{0,24},{1,25},{2,26},{3,27},{4,28},{5,29},{6,30},{7,31},{8,16},{9,... | collective-permute-start | bytes 786440 | tf_op jit(solution)/shard_map/r_z3/ppermute | solution.py:116
  110.2 2.2 %collective-permute-done.35 = f32[2,128]{1,0:T(2,128)S(1)} collective-permute-done((f32[2,128]{1,0:T(2,128)S(1)}, f32[2,128]{1,0:T(2,128)S(1)}, u32[]{:S(2)}, u32[]{:S(2)}) %collective-permute-start.35) | collective-permute-done | bytes 1056 | tf_op jit(solution)/shard_map/t_z2/ppermute | solution.py:116
  114.7 5.0 %collective-permute-done.30.refs_2_ = bf16[128,1024]{1,0:T(8,128)(2,1)S(1)} collective-permute-done((bf16[128,1024]{1,0:T(8,128)(2,1)S(1)}, bf16[128,1024]{1,0:T(8,128)(2,1)S(1)}, u32[]{:S(2)}, u32[]{:S(2)}) %collective-permute-start.30) | collective-permute-done | bytes 262176 | tf_op jit(solution)/shard_map/r_z3/ppermute | solution.py:116
  (102 shorter events, 41.8 us)
Async XLA Ops:
  0.6 19.9 %collective-permute-start.4 = (bf16[384,4096]{1,0:T(8,128)(2,1)}, bf16[384,4096]{1,0:T(8,128)(2,1)}, u32[]{:S(2)}, u32[]{:S(2)}) collective-permute-start(bf16[384,4096]{1,0:T(8,128)(2,1)} %bitcast.37), channel_id=1, source_target_pairs={{0,1},{1,0},{2,3},{3,2},{4,5},{5,4},{6,7},{7,6},{8,9},{9,8},{10,11... | collective-permute-start | bytes 9437192 | tf_op jit(solution)/shard_map/weights/ppermute | solution.py:116
  3.1 17.2 %collective-permute-start = (bf16[136,1024]{1,0:T(8,128)(2,1)}, bf16[136,1024]{1,0:T(8,128)(2,1)S(1)}, u32[]{:S(2)}, u32[]{:S(2)}) collective-permute-start(bf16[136,1024]{1,0:T(8,128)(2,1)} %get-tuple-element.60.refs_0_), channel_id=1, source_target_pairs={{0,16},{1,17},{2,18},{3,19},{4,20},{5,21},{6,22},{7,23},{8,24},{9,... | collective-permute-start | bytes 835592 | tf_op jit(solution)/shard_map/z2/ppermute | solution.py:116
  6.7 13.8 %collective-permute-start.1 = (bf16[136,1024]{1,0:T(8,128)(2,1)}, bf16[136,1024]{1,0:T(8,128)(2,1)S(1)}, u32[]{:S(2)}, u32[]{:S(2)}) collective-permute-start(bf16[136,1024]{1,0:T(8,128)(2,1)} %get-tuple-element.60.refs_0_), channel_id=1, source_target_pairs={{0,8},{1,9},{2,10},{3,11},{4,12},{5,13},{6,14},{7,15},{8,0},{9,1},... | collective-permute-start | bytes 835592 | tf_op jit(solution)/shard_map/z1/ppermute | solution.py:116
  8.3 12.2 %collective-permute-start.2 = (bf16[136,1024]{1,0:T(8,128)(2,1)}, bf16[136,1024]{1,0:T(8,128)(2,1)S(1)}, u32[]{:S(2)}, u32[]{:S(2)}) collective-permute-start(bf16[136,1024]{1,0:T(8,128)(2,1)} %get-tuple-element.60.refs_0_), channel_id=1, source_target_pairs={{0,4},{1,3},{2,6},{3,1},{4,0},{5,7},{6,2},{7,5},{8,12},{9,11},{10,... | collective-permute-start | bytes 835592 | tf_op jit(solution)/shard_map/first0/ppermute | solution.py:116
  9.8 10.7 %collective-permute-start.3 = (bf16[136,1024]{1,0:T(8,128)(2,1)}, bf16[136,1024]{1,0:T(8,128)(2,1)S(1)}, u32[]{:S(2)}, u32[]{:S(2)}) collective-permute-start(bf16[136,1024]{1,0:T(8,128)(2,1)} %get-tuple-element.60.refs_0_), channel_id=1, source_target_pairs={{0,2},{1,5},{2,0},{3,7},{4,6},{5,1},{6,4},{7,3},{8,10},{9,13},{10,... | collective-permute-start | bytes 835592 | tf_op jit(solution)/shard_map/second0/ppermute | solution.py:116
  20.5 13.4 %collective-permute-start.9 = (bf16[4096,384]{1,0:T(8,128)(2,1)}, bf16[4096,384]{1,0:T(8,128)(2,1)S(1)}, u32[]{:S(2)}, u32[]{:S(2)}) collective-permute-start(bf16[4096,384]{1,0:T(8,128)(2,1)} %bitcast.40), channel_id=1, source_target_pairs={{0,1},{1,0},{2,3},{3,2},{4,5},{5,4},{6,7},{7,6},{8,9},{9,8},{10,11... | collective-permute-start | bytes 9437192 | tf_op jit(solution)/shard_map/weights/ppermute | solution.py:116
  22.1 9.2 %collective-permute-start.6 = (bf16[136,1024]{1,0:T(8,128)(2,1)S(1)}, bf16[136,1024]{1,0:T(8,128)(2,1)S(1)}, u32[]{:S(2)}, u32[]{:S(2)}) collective-permute-start(bf16[136,1024]{1,0:T(8,128)(2,1)S(1)} %collective-permute-done.refs_3_.refs_4_), channel_id=1, source_target_pairs={{0,4},{1,3},{2,6},{3,1},{4,0},{5,7},{6,2},{7,5},{8,12},{9,11},{10,... | collective-permute-start | bytes 835592 | tf_op jit(solution)/shard_map/first2/ppermute | solution.py:116
  33.9 15.8 %collective-permute-start.13 = (bf16[4096,384]{1,0:T(8,128)(2,1)}, bf16[4096,384]{1,0:T(8,128)(2,1)}, u32[]{:S(2)}, u32[]{:S(2)}) collective-permute-start(bf16[4096,384]{1,0:T(8,128)(2,1)} %bitcast.43), channel_id=1, source_target_pairs={{0,1},{1,0},{2,3},{3,2},{4,5},{5,4},{6,7},{7,6},{8,9},{9,8},{10,11... | collective-permute-start | bytes 9437192 | tf_op jit(solution)/shard_map/weights/ppermute | solution.py:116
  35.5 12.4 %collective-permute-start.11 = (bf16[136,1024]{1,0:T(8,128)(2,1)S(1)}, bf16[136,1024]{1,0:T(8,128)(2,1)S(1)}, u32[]{:S(2)}, u32[]{:S(2)}) collective-permute-start(bf16[136,1024]{1,0:T(8,128)(2,1)S(1)} %collective-permute-done.1.refs_0_), channel_id=1, source_target_pairs={{0,4},{1,3},{2,6},{3,1},{4,0},{5,7},{6,2},{7,5},{8,12},{9,11},{10,... | collective-permute-start | bytes 835592 | tf_op jit(solution)/shard_map/first1/ppermute | solution.py:116
  37.0 12.7 %collective-permute-start.12 = (bf16[136,1024]{1,0:T(8,128)(2,1)S(1)}, bf16[136,1024]{1,0:T(8,128)(2,1)S(1)}, u32[]{:S(2)}, u32[]{:S(2)}) collective-permute-start(bf16[136,1024]{1,0:T(8,128)(2,1)S(1)} %collective-permute-done.1.refs_0_), channel_id=1, source_target_pairs={{0,2},{1,5},{2,0},{3,7},{4,6},{5,1},{6,4},{7,3},{8,10},{9,13},{10,... | collective-permute-start | bytes 835592 | tf_op jit(solution)/shard_map/second1/ppermute | solution.py:116
  38.0 11.6 %collective-permute-start.14 = (bf16[136,1024]{1,0:T(8,128)(2,1)S(1)}, bf16[136,1024]{1,0:T(8,128)(2,1)S(1)}, u32[]{:S(2)}, u32[]{:S(2)}) collective-permute-start(bf16[136,1024]{1,0:T(8,128)(2,1)S(1)} %collective-permute-done.5.refs_3_.refs_4_), channel_id=1, source_target_pairs={{0,4},{1,3},{2,6},{3,1},{4,0},{5,7},{6,2},{7,5},{8,12},{9,11},{10,... | collective-permute-start | bytes 835592 | tf_op jit(solution)/shard_map/first3/ppermute | solution.py:116
  52.1 10.3 %collective-permute-start.17 = (bf16[136,1024]{1,0:T(8,128)(2,1)S(1)}, bf16[136,1024]{1,0:T(8,128)(2,1)S(1)}, u32[]{:S(2)}, u32[]{:S(2)}) collective-permute-start(bf16[136,1024]{1,0:T(8,128)(2,1)S(1)} %collective-permute-done.5.refs_3_.refs_4_), channel_id=1, source_target_pairs={{0,2},{1,5},{2,0},{3,7},{4,6},{5,1},{6,4},{7,3},{8,10},{9,13},{10,... | collective-permute-start | bytes 835592 | tf_op jit(solution)/shard_map/second3/ppermute | solution.py:116
  53.1 10.6 %collective-permute-start.18 = (bf16[136,1024]{1,0:T(8,128)(2,1)S(1)}, bf16[136,1024]{1,0:T(8,128)(2,1)S(1)}, u32[]{:S(2)}, u32[]{:S(2)}) collective-permute-start(bf16[136,1024]{1,0:T(8,128)(2,1)S(1)} %collective-permute-done.11.refs_1_), channel_id=1, source_target_pairs={{0,2},{1,5},{2,0},{3,7},{4,6},{5,1},{6,4},{7,3},{8,10},{9,13},{10,... | collective-permute-start | bytes 835592 | tf_op jit(solution)/shard_map/third1/ppermute | solution.py:116
  54.1 10.5 %collective-permute-start.19 = (bf16[136,1024]{1,0:T(8,128)(2,1)S(1)}, bf16[136,1024]{1,0:T(8,128)(2,1)S(1)}, u32[]{:S(2)}, u32[]{:S(2)}) collective-permute-start(bf16[136,1024]{1,0:T(8,128)(2,1)S(1)} %collective-permute-done.14.refs_4_.refs_5_), channel_id=1, source_target_pairs={{0,2},{1,5},{2,0},{3,7},{4,6},{5,1},{6,4},{7,3},{8,10},{9,13},{10,... | collective-permute-start | bytes 835592 | tf_op jit(solution)/shard_map/third3/ppermute | solution.py:116
  61.2 9.2 %collective-permute-start.20 = (bf16[256,1024]{1,0:T(8,128)(2,1)S(1)}, bf16[256,1024]{1,0:T(8,128)(2,1)S(1)}, u32[]{:S(2)}, u32[]{:S(2)}) collective-permute-start(bf16[256,1024]{1,0:T(8,128)(2,1)S(1)} %get-tuple-element.94), channel_id=1, source_target_pairs={{0,2},{1,5},{2,0},{3,7},{4,6},{5,1},{6,4},{7,3},{8,10},{9,13},{10,... | collective-permute-start | bytes 1572872 | tf_op jit(solution)/shard_map/r_corner0/ppermute | solution.py:116
  71.2 14.8 %collective-permute-start.23 = (bf16[256,1024]{1,0:T(8,128)(2,1)}, bf16[256,1024]{1,0:T(8,128)(2,1)}, u32[]{:S(2)}, u32[]{:S(2)}) collective-permute-start(bf16[256,1024]{1,0:T(8,128)(2,1)} %get-tuple-element.102), channel_id=1, source_target_pairs={{0,2},{1,5},{2,0},{3,7},{4,6},{5,1},{6,4},{7,3},{8,10},{9,13},{10,... | collective-permute-start | bytes 1572872 | tf_op jit(solution)/shard_map/r_right0/ppermute | solution.py:116
  72.3 14.9 %collective-permute-start.24 = (bf16[256,1024]{1,0:T(8,128)(2,1)S(1)}, bf16[256,1024]{1,0:T(8,128)(2,1)}, u32[]{:S(2)}, u32[]{:S(2)}) collective-permute-start(bf16[256,1024]{1,0:T(8,128)(2,1)S(1)} %corner.2), channel_id=1, source_target_pairs={{0,4},{1,3},{2,6},{3,1},{4,0},{5,7},{6,2},{7,5},{8,12},{9,11},{10,... | collective-permute-start | bytes 1572872 | tf_op jit(solution)/shard_map/r_left0/ppermute | solution.py:116
  81.7 10.3 %collective-permute-start.26 = (bf16[256,1024]{1,0:T(8,128)(2,1)}, bf16[256,1024]{1,0:T(8,128)(2,1)S(1)}, u32[]{:S(2)}, u32[]{:S(2)}) collective-permute-start(bf16[256,1024]{1,0:T(8,128)(2,1)} %get-tuple-element.107), channel_id=1, source_target_pairs={{0,2},{1,5},{2,0},{3,7},{4,6},{5,1},{6,4},{7,3},{8,10},{9,13},{10,... | collective-permute-start | bytes 1572872 | tf_op jit(solution)/shard_map/r_corner1/ppermute | solution.py:116
  84.0 10.8 %collective-permute-start.32 = (f32[2,4,128]{2,1,0:T(4,128)S(1)}, f32[2,4,128]{2,1,0:T(4,128)S(1)}, u32[]{:S(2)}, u32[]{:S(2)}) collective-permute-start(f32[2,4,128]{2,1,0:T(4,128)S(1)} %fusion), channel_id=1, source_target_pairs={{0,2},{1,3},{2,0},{3,1},{4,6},{5,7},{6,4},{7,5},{8,10},{9,11},{10,... | collective-permute-start | bytes 12296 | tf_op jit(solution)/shard_map/t_x/ppermute | solution.py:116
  88.6 14.0 %collective-permute-start.27 = (bf16[256,1024]{1,0:T(8,128)(2,1)}, bf16[256,1024]{1,0:T(8,128)(2,1)S(1)}, u32[]{:S(2)}, u32[]{:S(2)}) collective-permute-start(bf16[256,1024]{1,0:T(8,128)(2,1)} %copy-done.7), channel_id=1, source_target_pairs={{0,2},{1,5},{2,0},{3,7},{4,6},{5,1},{6,4},{7,3},{8,10},{9,13},{10,... | collective-permute-start | bytes 1572872 | tf_op jit(solution)/shard_map/r_right1/ppermute | solution.py:116
  89.7 13.4 %collective-permute-start.25 = (bf16[128,1024]{1,0:T(8,128)(2,1)S(1)}, bf16[128,1024]{1,0:T(8,128)(2,1)S(1)}, u32[]{:S(2)}, u32[]{:S(2)}) collective-permute-start(bf16[128,1024]{1,0:T(8,128)(2,1)S(1)} %get-tuple-element.104), channel_id=1, source_target_pairs={{0,16},{1,17},{2,18},{3,19},{4,20},{5,21},{6,22},{7,23},{8,24},{9,... | collective-permute-start | bytes 786440 | tf_op jit(solution)/shard_map/r_z2/ppermute | solution.py:116
  93.2 9.4 %collective-permute-start.28 = (bf16[256,1024]{1,0:T(8,128)(2,1)S(1)}, bf16[256,1024]{1,0:T(8,128)(2,1)S(1)}, u32[]{:S(2)}, u32[]{:S(2)}) collective-permute-start(bf16[256,1024]{1,0:T(8,128)(2,1)S(1)} %corner.3), channel_id=1, source_target_pairs={{0,4},{1,3},{2,6},{3,1},{4,0},{5,7},{6,2},{7,5},{8,12},{9,11},{10,... | collective-permute-start | bytes 1572872 | tf_op jit(solution)/shard_map/r_left1/ppermute | solution.py:116
  105.2 9.5 %collective-permute-start.29 = (bf16[128,1024]{1,0:T(8,128)(2,1)S(1)}, bf16[128,1024]{1,0:T(8,128)(2,1)S(1)}, u32[]{:S(2)}, u32[]{:S(2)}) collective-permute-start(bf16[128,1024]{1,0:T(8,128)(2,1)S(1)} %get-tuple-element.110), channel_id=1, source_target_pairs={{0,8},{1,9},{2,10},{3,11},{4,12},{5,13},{6,14},{7,15},{8,0},{9,1},... | collective-permute-start | bytes 786440 | tf_op jit(solution)/shard_map/r_z1/ppermute | solution.py:116
  107.5 12.1 %collective-permute-start.30 = (bf16[128,1024]{1,0:T(8,128)(2,1)S(1)}, bf16[128,1024]{1,0:T(8,128)(2,1)S(1)}, u32[]{:S(2)}, u32[]{:S(2)}) collective-permute-start(bf16[128,1024]{1,0:T(8,128)(2,1)S(1)} %get-tuple-element.111), channel_id=1, source_target_pairs={{0,24},{1,25},{2,26},{3,27},{4,28},{5,29},{6,30},{7,31},{8,16},{9,... | collective-permute-start | bytes 786440 | tf_op jit(solution)/shard_map/r_z3/ppermute | solution.py:116
  (23 other events, 135.8 us)
